TPU v7x, 256 devices: a whole 4x4x8 slice. The times are simulated.
256 devices in a mesh: item: 32 (over x, z), store: 8 (over y, core).
Axes of the slice: x: 4, y: 4, z: 8, core: 2. Of those that a mesh axis runs over, the one named last changes fastest.
Arguments:
- predicted_units: bfloat16 [4096, 8, 4096], P('item', None, 'store'), may hold values from 0.049804688 to 5
- product_group: int32 [4096], P('item'), may hold values from 0 to 63, as said below
- product_goal: float32 [4096], P('item'), may hold values from 9830 to 98304
- group_outlet_goal: float32 [64, 4096], P(None, 'store'), may hold values from 153 to 1536
- outlet_date_goal: float32 [8, 4096], P(None, 'store'), may hold values from 1228 to 12288
Outputs:
- product_factor: float32 [4096], P('item')
- group_outlet_factor: float32 [64, 4096], P(None, 'store')
- outlet_date_factor: float32 [8, 4096], P(None, 'store')
- adjusted_tensor: bfloat16 [4096, 8, 4096], P('item', None, 'store')
Inputs may be any that keep to these rules, and one draw needn't show every extreme that they name: `product_group`: category ids never fall along the items, and every category holds at least 32 items; some category holds exactly that many.
All inputs are finite; a program needn't handle non-finite values.
Results may differ from a plain program's by a relative error of at most 0.001.
Values sent between devices are 32-bit elements; how exact they have to be, the bound alone decides.
No kernel may reach another device: no remote copies, remote signals or barrier semaphores. Data moves between devices by JAX's collectives and lax.ppermute only.
A program may use at most 64 MiB of HBM per device.

v0:
```python
import jax
import jax.numpy as jnp
from jax import lax
from jax.sharding import PartitionSpec as P

ROUNDS = 4
INNER = 3


def sent_to_all(array, axis):
    count = lax.axis_size(axis)
    return lax.all_to_all(
        jnp.broadcast_to(array[None], (count, *array.shape)), axis, 0, 0, tiled=True
    )


def taken_together(array, axis):
    return sent_to_all(array, axis).sum(axis=0)


def in_blocks(array, dim, count):
    before, after = (array.shape[:dim], array.shape[dim + 1 :])
    return jnp.moveaxis(array.reshape(*before, count, -1, *after), dim, 0)


def sum_at_owner(array, axis, dim):
    tiles = in_blocks(array, dim, lax.axis_size(axis))
    arrived = lax.all_to_all(tiles, axis, split_axis=0, concat_axis=0, tiled=True)
    return arrived.sum(axis=0)


def laid_out(tiles, dim):
    shape = list(tiles.shape[1:])
    shape[dim] *= tiles.shape[0]
    return jnp.moveaxis(tiles, 0, dim).reshape(shape)


def gather_together(arrays, axis, dims):
    vector = jnp.concatenate([a.reshape(-1) for a in arrays])
    lines, at, done = (lax.all_gather(vector, axis), 0, [])
    for a, dim in zip(arrays, dims):
        tiles = lines[:, at : at + a.size].reshape(-1, *a.shape)
        done.append(laid_out(tiles, dim))
        at += a.size
    return tuple(done)


def shards(predicted_units, product_group, product_goal, group_outlet_goal, outlet_date_goal):
    product_slice, horizon_length, outlet_tally = predicted_units.shape
    cat_count = group_outlet_goal.shape[0]
    indicator_matrix = (
        product_group[:, None] == jnp.arange(cat_count, dtype=jnp.int32)[None, :]
    ).astype(jnp.float32)
    group_outlet_factor = jnp.ones((cat_count, outlet_tally), jnp.float32)
    outlet_date_factor = jnp.ones((horizon_length, outlet_tally), jnp.float32)
    groups = lax.axis_size("item")
    share_width = outlet_tally // groups
    offset = lax.axis_index("item") * share_width

    def spread_tensor(multiplier):
        return jnp.dot(indicator_matrix, multiplier, precision=lax.Precision.HIGHEST)

    def take_share(values):
        return lax.dynamic_slice_in_dim(values, offset, share_width, 1)

    kept_multiplier = group_outlet_factor
    product_factor = jnp.ones((product_slice,), jnp.float32)
    for round_index in range(ROUNDS):
        masked_prediction = spread_tensor(kept_multiplier)[:, None, :] * outlet_date_factor[None]
        product_marginals = jnp.sum(predicted_units * masked_prediction, axis=(1, 2))
        product_factor = product_goal / taken_together(product_marginals, "store")
        pooled_masked_prediction = predicted_units * product_factor[:, None, None]
        merged_matrix = sum_at_owner(
            jnp.einsum(
                "bv,bjz->vjz",
                indicator_matrix,
                pooled_masked_prediction,
                precision=lax.Precision.HIGHEST,
            ),
            "item",
            2,
        )
        cat_target = take_share(group_outlet_goal)
        day_target = take_share(outlet_date_goal)
        day_piece = take_share(outlet_date_factor)
        cat_piece = take_share(kept_multiplier)
        for pass_index in range(INNER):
            cat_piece = cat_target / jnp.sum(merged_matrix * day_piece[None], axis=1)
            day_piece = day_target / jnp.sum(merged_matrix * cat_piece[:, None, :], axis=0)
        kept_multiplier, outlet_date_factor = gather_together(
            (cat_piece, day_piece), "item", (1, 1)
        )
    adjusted_tensor = (
        predicted_units
        * product_factor[:, None, None]
        * spread_tensor(kept_multiplier)[:, None, :]
        * outlet_date_factor[None]
    ).astype(jnp.bfloat16)
    group_outlet_factor = kept_multiplier
    return (product_factor, group_outlet_factor, outlet_date_factor, adjusted_tensor)


def solution(mesh):
    in_specs = (P("item", None, "store"), P("item"), P("item"), P(None, "store"), P(None, "store"))
    out_specs = (P("item"), P(None, "store"), P(None, "store"), P("item", None, "store"))
    return jax.shard_map(shards, mesh=mesh, in_specs=in_specs, out_specs=out_specs, check_vma=False)
```

profile of v0, /device:TPU:8, one launch (start us, length us, event | category | flops | bytes accessed | tf_op | source)
XLA Modules:
  0.0 425.5 jit_solution(9454693394187111874)
XLA Ops:
  0.7 1.0 fusion.12
  1.7 2.3 fusion
  4.0 8.5 %all_to_all.44 = f32[8,1,128]{2,1,0:T(1,128)S(1)} all-to-all(f32[8,1,128]{2,1,0:T(1,128)S(1)} %broadcast_in_dim.11), channel_id=1, replica_groups=mesh['item'=32,'store'=8] {'store'}, dimensions={0} | all-to-all | bytes 8192 | tf_op jit(solution)/shard_map/all_to_all | solution.py:12
  12.5 0.7 div.84
  13.4 2.6 fusion.10
  16.3 2.3 reshape.189
  18.6 11.3 %all-to-all-start.1 = ((f32[32,1,8192]{2,1,0:T(1,128)}), f32[32,1,8192]{2,1,0:T(1,128)S(1)}, u32[]{:S(2)}, u32[]{:S(2)}) async-start(f32[32,1,8192]{2,1,0:T(1,128)} %reshape.189), calls=%async_computation.1 | async-start | bytes 2097152 | tf_op jit(solution)/shard_map/all_to_all | solution.py:28
  30.0 28.4 %all-to-all-done.1 = f32[32,1,8192]{2,1,0:T(1,128)S(1)} async-done(((f32[32,1,8192]{2,1,0:T(1,128)}), f32[32,1,8192]{2,1,0:T(1,128)S(1)}, u32[]{:S(2)}, u32[]{:S(2)}) %all-to-all-start.1) | async-done | bytes 1048608 | tf_op jit(solution)/shard_map/all_to_all | solution.py:28
  58.5 0.5 broadcast.45
  59.0 4.4 %reduce.5 = f32[32,8192]{1,0:T(8,128)} reduce(f32[32,1,8192]{2,1,0:T(1,128)S(1)} %all-to-all-done.1, f32[]{:T(128)} %broadcast.45), dimensions={1}, to_apply=%all_to_all.29.reduce_sub_computation | reduce | bytes 2097156 | tf_op jit(solution)/shard_map/all_to_all | solution.py:28
  63.4 2.0 reshape.190
  65.4 0.3 fusion.50
  66.8 46.2 %all-gather.4 = f32[32,1,1152]{2,1,0:T(1,128)S(1)} all-gather(f32[1,1,1152]{2,1,0:T(1,128)S(1)} %reshape.176), channel_id=2, replica_groups=mesh['item'=32,'store'=8] {'item'}, dimensions={0}, use_global_device_ids=true | all-gather | bytes 152064 | tf_op jit(solution)/shard_map/all_gather | solution.py:40
  113.6 0.3 fusion.22
  114.2 1.0 fusion.1
  115.2 7.7 %all_to_all.45 = f32[8,1,128]{2,1,0:T(1,128)S(1)} all-to-all(f32[8,1,128]{2,1,0:T(1,128)S(1)} %broadcast_in_dim.12), channel_id=1, replica_groups=mesh['item'=32,'store'=8] {'store'}, dimensions={0} | all-to-all | bytes 8192 | tf_op jit(solution)/shard_map/all_to_all | solution.py:12
  123.1 2.6 fusion.8
  126.0 2.3 reshape.191
  128.2 5.2 %all-to-all-start.3 = ((f32[32,1,8192]{2,1,0:T(1,128)}), f32[32,1,8192]{2,1,0:T(1,128)S(1)}, u32[]{:S(2)}, u32[]{:S(2)}) async-start(f32[32,1,8192]{2,1,0:T(1,128)} %reshape.191), calls=%async_computation.3 | async-start | bytes 2097152 | tf_op jit(solution)/shard_map/all_to_all | solution.py:28
  133.5 28.5 %all-to-all-done.3 = f32[32,1,8192]{2,1,0:T(1,128)S(1)} async-done(((f32[32,1,8192]{2,1,0:T(1,128)}), f32[32,1,8192]{2,1,0:T(1,128)S(1)}, u32[]{:S(2)}, u32[]{:S(2)}) %all-to-all-start.3) | async-done | bytes 1048608 | tf_op jit(solution)/shard_map/all_to_all | solution.py:28
  162.0 4.4 %reduce.6 = f32[32,8192]{1,0:T(8,128)} reduce(f32[32,1,8192]{2,1,0:T(1,128)S(1)} %all-to-all-done.3, f32[]{:T(128)} %broadcast.45), dimensions={1}, to_apply=%all_to_all.31.reduce_sub_computation | reduce | bytes 2097156 | tf_op jit(solution)/shard_map/all_to_all | solution.py:28
  166.4 2.0 reshape.192
  169.7 46.3 %all-gather.5 = f32[32,1,1152]{2,1,0:T(1,128)S(1)} all-gather(f32[1,1,1152]{2,1,0:T(1,128)S(1)} %reshape.178), channel_id=3, replica_groups=mesh['item'=32,'store'=8] {'item'}, dimensions={0}, use_global_device_ids=true | all-gather | bytes 152064 | tf_op jit(solution)/shard_map/all_gather | solution.py:40
  216.3 0.3 copy.143
  216.6 0.3 fusion.24
  217.1 1.0 fusion.2
  218.2 7.6 %all_to_all.46 = f32[8,1,128]{2,1,0:T(1,128)S(1)} all-to-all(f32[8,1,128]{2,1,0:T(1,128)S(1)} %broadcast_in_dim.13), channel_id=1, replica_groups=mesh['item'=32,'store'=8] {'store'}, dimensions={0} | all-to-all | bytes 8192 | tf_op jit(solution)/shard_map/all_to_all | solution.py:12
  226.1 2.6 fusion.6
  228.9 2.3 reshape.193
  231.2 5.2 %all-to-all-start.5 = ((f32[32,1,8192]{2,1,0:T(1,128)}), f32[32,1,8192]{2,1,0:T(1,128)S(1)}, u32[]{:S(2)}, u32[]{:S(2)}) async-start(f32[32,1,8192]{2,1,0:T(1,128)} %reshape.193), calls=%async_computation.5 | async-start | bytes 2097152 | tf_op jit(solution)/shard_map/all_to_all | solution.py:28
  236.5 28.5 %all-to-all-done.5 = f32[32,1,8192]{2,1,0:T(1,128)S(1)} async-done(((f32[32,1,8192]{2,1,0:T(1,128)}), f32[32,1,8192]{2,1,0:T(1,128)S(1)}, u32[]{:S(2)}, u32[]{:S(2)}) %all-to-all-start.5) | async-done | bytes 1048608 | tf_op jit(solution)/shard_map/all_to_all | solution.py:28
  265.0 4.4 %reduce.7 = f32[32,8192]{1,0:T(8,128)} reduce(f32[32,1,8192]{2,1,0:T(1,128)S(1)} %all-to-all-done.5, f32[]{:T(128)} %broadcast.45), dimensions={1}, to_apply=%all_to_all.33.reduce_sub_computation | reduce | bytes 2097156 | tf_op jit(solution)/shard_map/all_to_all | solution.py:28
  269.4 2.0 reshape.194
  272.7 46.3 %all-gather.6 = f32[32,1,1152]{2,1,0:T(1,128)S(1)} all-gather(f32[1,1,1152]{2,1,0:T(1,128)S(1)} %reshape.180), channel_id=4, replica_groups=mesh['item'=32,'store'=8] {'item'}, dimensions={0}, use_global_device_ids=true | all-gather | bytes 152064 | tf_op jit(solution)/shard_map/all_gather | solution.py:40
  319.3 0.3 copy.152
  319.6 0.3 fusion.26
  320.2 1.0 fusion.3
  321.2 7.6 %all_to_all.47 = f32[8,1,128]{2,1,0:T(1,128)S(1)} all-to-all(f32[8,1,128]{2,1,0:T(1,128)S(1)} %broadcast_in_dim.14), channel_id=1, replica_groups=mesh['item'=32,'store'=8] {'store'}, dimensions={0} | all-to-all | bytes 8192 | tf_op jit(solution)/shard_map/all_to_all | solution.py:12
  329.1 2.6 fusion.4
  331.9 2.3 reshape.195
  334.2 5.2 %all-to-all-start.7 = ((f32[32,1,8192]{2,1,0:T(1,128)}), f32[32,1,8192]{2,1,0:T(1,128)S(1)}, u32[]{:S(2)}, u32[]{:S(2)}) async-start(f32[32,1,8192]{2,1,0:T(1,128)} %reshape.195), calls=%async_computation.7 | async-start | bytes 2097152 | tf_op jit(solution)/shard_map/all_to_all | solution.py:28
  339.5 28.5 %all-to-all-done.7 = f32[32,1,8192]{2,1,0:T(1,128)S(1)} async-done(((f32[32,1,8192]{2,1,0:T(1,128)}), f32[32,1,8192]{2,1,0:T(1,128)S(1)}, u32[]{:S(2)}, u32[]{:S(2)}) %all-to-all-start.7) | async-done | bytes 1048608 | tf_op jit(solution)/shard_map/all_to_all | solution.py:28
  368.0 4.4 %reduce.8 = f32[32,8192]{1,0:T(8,128)} reduce(f32[32,1,8192]{2,1,0:T(1,128)S(1)} %all-to-all-done.7, f32[]{:T(128)} %broadcast.45), dimensions={1}, to_apply=%all_to_all.35.reduce_sub_computation | reduce | bytes 2097156 | tf_op jit(solution)/shard_map/all_to_all | solution.py:28
  372.4 2.0 reshape.196
  375.7 46.1 %all-gather.7 = f32[32,1,1152]{2,1,0:T(1,128)S(1)} all-gather(f32[1,1,1152]{2,1,0:T(1,128)S(1)} %reshape.182), channel_id=5, replica_groups=mesh['item'=32,'store'=8] {'item'}, dimensions={0}, use_global_device_ids=true | all-gather | bytes 152064 | tf_op jit(solution)/shard_map/all_gather | solution.py:40
  422.4 0.8 copy.163
  423.1 0.3 fusion.20
  423.7 1.3 multiply_convert_fusion
  (130 shorter events, 9.3 us)
Async XLA Ops:
  0.6 29.3 %copy-start = (f32[64,512]{1,0:T(8,128)S(1)}, f32[64,512]{1,0:T(8,128)}, u32[]{:S(2)}) copy-start(f32[64,512]{1,0:T(8,128)} %param.8) | copy-start | bytes 393220
  0.6 12.6 %copy-start.1 = (bf16[128,8,512]{2,1,0:T(8,128)(2,1)S(1)}, bf16[128,8,512]{2,1,0:T(8,128)(2,1)}, u32[]{:S(2)}) copy-start(bf16[128,8,512]{2,1,0:T(8,128)(2,1)} %param.5) | copy-start | bytes 3145732
  1.7 11.7 %copy-start.4 = (s32[128]{0:T(128)S(1)}, s32[128]{0:T(128)}, u32[]{:S(2)}) copy-start(s32[128]{0:T(128)} %param.6) | copy-start | bytes 1540
  18.6 39.9 %all-to-all-start.1 = ((f32[32,1,8192]{2,1,0:T(1,128)}), f32[32,1,8192]{2,1,0:T(1,128)S(1)}, u32[]{:S(2)}, u32[]{:S(2)}) async-start(f32[32,1,8192]{2,1,0:T(1,128)} %reshape.189), calls=%async_computation.1 | async-start | bytes 2097152 | tf_op jit(solution)/shard_map/all_to_all | solution.py:28
  63.4 2.4 copy-start.2
  113.3 9.6 %copy-start.6 = (f32[128]{0:T(128)S(1)}, f32[128]{0:T(128)}, u32[]{:S(2)}) copy-start(f32[128]{0:T(128)} %param.7) | copy-start | bytes 1540
  128.2 33.8 %all-to-all-start.3 = ((f32[32,1,8192]{2,1,0:T(1,128)}), f32[32,1,8192]{2,1,0:T(1,128)S(1)}, u32[]{:S(2)}, u32[]{:S(2)}) async-start(f32[32,1,8192]{2,1,0:T(1,128)} %reshape.191), calls=%async_computation.3 | async-start | bytes 2097152 | tf_op jit(solution)/shard_map/all_to_all | solution.py:28
  231.2 33.8 %all-to-all-start.5 = ((f32[32,1,8192]{2,1,0:T(1,128)}), f32[32,1,8192]{2,1,0:T(1,128)S(1)}, u32[]{:S(2)}, u32[]{:S(2)}) async-start(f32[32,1,8192]{2,1,0:T(1,128)} %reshape.193), calls=%async_computation.5 | async-start | bytes 2097152 | tf_op jit(solution)/shard_map/all_to_all | solution.py:28
  328.9 94.8 %copy-start.5 = (f32[128]{0:T(128)}, f32[128]{0:T(128)S(1)}, u32[]{:S(2)}) copy-start(f32[128]{0:T(128)S(1)} %div.105) | copy-start | bytes 1540
  334.2 33.8 %all-to-all-start.7 = ((f32[32,1,8192]{2,1,0:T(1,128)}), f32[32,1,8192]{2,1,0:T(1,128)S(1)}, u32[]{:S(2)}, u32[]{:S(2)}) async-start(f32[32,1,8192]{2,1,0:T(1,128)} %reshape.195), calls=%async_computation.7 | async-start | bytes 2097152 | tf_op jit(solution)/shard_map/all_to_all | solution.py:28
  423.7 1.4 copy-start.3
where the time goes:
time: 434 us; the launch traced here: 425 us
  blocking collectives  216 us (50%)
  waiting for transfers between devices  114 us (26%)
  other arithmetic  29.8 us (7%)
  starting transfers between devices  26.9 us (6%)
  local copies, waits for them, and re-layouts  23.9 us (6%)
  matrix products  12.8 us (3%)
    all_gather x4, blocking collectives, gather_together(): lines, at, done = (lax.all_gather(vector, axis), 0, [])  185 us
    all_to_all x4, waiting for transfers between devices, sum_at_owner(): lax.all_to_all(tiles, axis, split_axis=0, concat_axis=0, tiled=True)  114 us
    all_to_all x4, blocking collectives, sent_to_all(): lax.all_to_all(jnp.broadcast_to(array[None], (count, *array.shape)), axis...  31.5 us
    all_to_all x4, starting transfers between devices, sum_at_owner(): lax.all_to_all(tiles, axis, split_axis=0, concat_axis=0, tiled=True)  26.9 us
    unnamed x28, local copies, waits for them, and re-layouts  18 us
    all_to_all x4, other arithmetic, sum_at_owner(): lax.all_to_all(tiles, axis, split_axis=0, concat_axis=0, tiled=True)  17.6 us
    dot_general x4, matrix products, shards(): jnp.einsum('bv,bjz->vjz', indicator_matrix, pooled_masked_prediction, pre...  10.5 us
  transfers between devices with their start and end apart: 4, of which 4 were waited for; matrix products, arithmetic and copies ran while one was open for 0% of the time, Pallas kernels for 0%

commit v1 on v0

v1 whole, which is shorter than its diff:
```python
import functools

import jax
import jax.numpy as jnp
from jax import lax
from jax.experimental import pallas as pl
from jax.experimental.pallas import tpu as pltpu
from jax.sharding import PartitionSpec as P

ROUNDS = 4
INNER = 3
LANES = 128
SUB = 8
SLOTS = 5
BASE_ROW = 7

F32 = jnp.float32
BF16 = jnp.bfloat16


def iota(shape, dim):
    return lax.broadcasted_iota(jnp.int32, shape, dim)


def two_parts(x):
    high = x.astype(BF16)
    low = (x - high.astype(F32)).astype(BF16)
    return high, low


def swap_blocks(tiles):
    count = len(tiles)
    width = LANES // count
    group = iota(tiles[0].shape, 1) // width
    bit = 1
    while bit < count:
        low = (group & bit) == 0
        fresh = []
        for a in range(count):
            other = tiles[a ^ bit]
            if a & bit == 0:
                fresh.append(jnp.where(low, tiles[a], pltpu.roll(other, bit * width, 1)))
            else:
                fresh.append(jnp.where(low, pltpu.roll(other, LANES - bit * width, 1), tiles[a]))
        tiles = fresh
        bit *= 2
    return tiles


def eight_sum(x):
    lane = iota(x.shape, 1)
    for bit in (1, 2, 4):
        x = x + jnp.where((lane & bit) == 0, pltpu.roll(x, LANES - bit, 1), pltpu.roll(x, bit, 1))
    return x


def compacted(rows):
    row = iota((SUB, LANES), 0)
    tile = rows[0]
    for q in range(1, SUB):
        tile = jnp.where(row == q, rows[q], tile)
    tile = eight_sum(tile)
    kept = jnp.where((iota((SUB, LANES), 1) & 7) == row, tile, 0.0)
    return jnp.sum(kept, axis=0, keepdims=True)


def expanded(line):
    line = jnp.broadcast_to(line, (SUB, LANES))
    return eight_sum(jnp.where((iota((SUB, LANES), 1) & 7) == iota((SUB, LANES), 0), line, 0.0))


def first_kernel(x_ref, flat_ref, out_ref):
    items, days, stores = x_ref.shape
    flat = x_ref[...].astype(F32).reshape(items * days, stores).astype(BF16)
    flat_ref[...] = flat
    sums = lax.dot_general(
        jnp.ones((SUB, stores), BF16), flat, (((1,), (1,)), ((), ())), preferred_element_type=F32
    )
    line = compacted([sums[:, q * LANES : (q + 1) * LANES] for q in range(SUB)])
    out_ref[...] = jnp.broadcast_to(line[None], out_ref.shape)


def margin_kernel(back_ref, flat_ref, tid_ref, out_ref):
    stores = flat_ref.shape[1]
    columns = []
    for t in range(stores // LANES):
        columns.append(jnp.concatenate(swap_blocks([back_ref[t * SUB + j] for j in range(SUB)]), axis=0))
    weights = jnp.concatenate(columns, axis=1)
    parts = jnp.concatenate(two_parts(weights), axis=0)
    sums = lax.dot_general(parts, flat_ref[...], (((1,), (1,)), ((), ())), preferred_element_type=F32)
    half = weights.shape[0]
    sums = sums[:half] + sums[half:]
    which = iota((half, LANES), 0)
    rows = []
    for q in range(SUB):
        kept = jnp.where(which == tid_ref[q : q + 1, :], sums[:, q * LANES : (q + 1) * LANES], 0.0)
        rows.append(jnp.broadcast_to(jnp.sum(kept, axis=0, keepdims=True), (SUB, LANES)))
    line = compacted(rows)
    out_ref[...] = jnp.broadcast_to(line[None], out_ref.shape)


def pool_kernel(margin_ref, goal_ref, flat_ref, tid_ref, base_ref, out_ref, factor_ref):
    stores = flat_ref.shape[1]
    total = jnp.sum(margin_ref[...], axis=0)
    factor = goal_ref[...] / total
    factor_ref[...] = factor
    spread = expanded(factor)
    half = SUB * SUB
    which = iota((half, LANES), 0)
    columns = []
    for q in range(SUB):
        columns.append(jnp.where(which == tid_ref[q : q + 1, :], spread[q : q + 1, :], 0.0))
    weights = jnp.concatenate(columns, axis=1)
    parts = jnp.concatenate(two_parts(weights), axis=0)
    sums = jnp.dot(parts, flat_ref[...], preferred_element_type=F32)
    sums = sums[:half] + sums[half:]
    row = iota((SUB, LANES), 0)
    base = jnp.broadcast_to(base_ref[...], (SUB, LANES))
    for t in range(stores // LANES):
        tiles = [sums[d * SUB : (d + 1) * SUB, t * LANES : (t + 1) * LANES] for d in range(SUB)]
        for j, tile in enumerate(swap_blocks(tiles)):
            out_ref[t * SUB + j] = jnp.where(row == BASE_ROW, base, tile)


def owner_kernel(last, taken_ref, cat_goal_ref, day_goal_ref, day_ref, out_ref, *day_out):
    devices = taken_ref.shape[0]
    cats = cat_goal_ref.shape[0]
    taken = taken_ref[...]
    slot = iota(taken.shape, 1)
    base = taken[:, BASE_ROW : BASE_ROW + 1, :].astype(jnp.int32)
    place = ((base + slot == iota(taken.shape, 2)) & (slot < SLOTS)).astype(F32)
    place = place.reshape(devices * SUB, LANES).astype(BF16)
    parts = jnp.concatenate(two_parts(taken.reshape(devices * SUB, LANES)), axis=1)
    merged = lax.dot_general(place, parts, (((0,), (0,)), ((), ())), preferred_element_type=F32)
    merged = (merged[:, :LANES] + merged[:, LANES:])[:cats]
    cat_goal, day_goal = cat_goal_ref[...], day_goal_ref[...]
    width = LANES // SUB
    day = day_ref[...]
    for _ in range(INNER):
        below = merged * day
        step = LANES // 2
        while step >= width:
            below = below + pltpu.roll(below, step, 1)
            step //= 2
        cat = cat_goal / below
        day = day_goal / jnp.sum(merged * cat, axis=0, keepdims=True)
    if last:
        group = iota((SUB, LANES), 1) // width
        tile = cat[:SUB]
        for d in range(1, SUB):
            tile = jnp.where(group == d, cat[d * SUB : (d + 1) * SUB], tile)
        both = jnp.concatenate([tile, jnp.broadcast_to(day, (SUB, LANES))], axis=0)
        out_ref[...] = jnp.broadcast_to(both[None], out_ref.shape)
        return
    day_out[0][...] = day
    product = jnp.concatenate([cat * day, jnp.zeros((LANES - cats, LANES), F32)], axis=0)
    product = jnp.concatenate(two_parts(product), axis=1)
    sent = jnp.dot(place, product, preferred_element_type=F32)
    out_ref[...] = (sent[:, :LANES] + sent[:, LANES:]).reshape(devices, SUB, LANES)


def closing_kernel(group_ref, factor_ref, back_ref, x_ref, cat_ref, day_ref, out_ref, scale_ref):
    block = x_ref.shape[0]
    stores = x_ref.shape[2]
    first = group_ref[0]
    step = pl.program_id(0)

    @pl.when(step == 0)
    def _():
        row = iota((SUB, LANES), 0)
        for t in range(stores // LANES):
            here = slice(t * LANES, (t + 1) * LANES)
            tiles = swap_blocks([back_ref[t * SUB + j, :SUB] for j in range(SUB)])
            cat_ref[:, here] = jnp.concatenate(tiles, axis=0)
            tiles = swap_blocks([back_ref[t * SUB + j, SUB:] for j in range(SUB)])
            day = tiles[0]
            for d in range(1, SUB):
                day = jnp.where(row == d, tiles[d], day)
            day_ref[:, here] = day
        last = cat_ref.shape[0] - 1
        for s in range(SLOTS):
            at = jnp.minimum(first + s, last)
            scale_ref[s] = cat_ref[pl.ds(at, 1), :] * day_ref[...]

    for i in range(block):
        at = step * block + i
        value = x_ref[i].astype(F32) * factor_ref[at] * scale_ref[group_ref[at] - first]
        out_ref[i] = value.astype(BF16)


def vmem(count):
    return [pl.BlockSpec(memory_space=pltpu.VMEM)] * count


def shards(predicted_units, product_group, product_goal, group_outlet_goal, outlet_date_goal):
    items, days, stores = predicted_units.shape
    cats = group_outlet_goal.shape[0]
    owners = lax.axis_size("item")
    width = stores // owners
    beside = lax.axis_size("store")
    at = lax.axis_index("item") * width

    message = jax.ShapeDtypeStruct((owners, SUB, LANES), F32)
    margin = jax.ShapeDtypeStruct((beside, 1, LANES), F32)
    line = jax.ShapeDtypeStruct((1, LANES), F32)

    slot = product_group - product_group[0]
    tid = jnp.repeat(slot, days).reshape(SUB, LANES) + (jnp.arange(LANES, dtype=jnp.int32) % days)[None] * SUB
    base = jnp.broadcast_to(product_group[:1].astype(F32)[None], (1, LANES))
    goal = product_goal.reshape(SUB, items // SUB).T.reshape(1, LANES)
    cat_goal = jnp.tile(lax.dynamic_slice_in_dim(group_outlet_goal, at, width, 1), (1, days))
    day_goal = lax.dynamic_slice_in_dim(outlet_date_goal, at, width, 1).reshape(1, LANES)
    day = jnp.ones((1, LANES), F32)

    flat, part = pl.pallas_call(
        first_kernel,
        out_shape=(jax.ShapeDtypeStruct((items * days, stores), BF16), margin),
        in_specs=vmem(1),
        out_specs=tuple(vmem(2)),
        name="first",
    )(predicted_units)
    for round_index in range(ROUNDS):
        total = lax.all_to_all(part, "store", 0, 0, tiled=True)
        pooled, factor = pl.pallas_call(
            pool_kernel,
            out_shape=(message, line),
            in_specs=vmem(5),
            out_specs=tuple(vmem(2)),
            name="pool",
        )(total, goal, flat, tid, base)
        taken = lax.all_to_all(pooled, "item", 0, 0, tiled=True)
        if round_index == ROUNDS - 1:
            break
        back, day = pl.pallas_call(
            functools.partial(owner_kernel, False),
            out_shape=(message, line),
            in_specs=vmem(4),
            out_specs=tuple(vmem(2)),
            name="owner",
        )(taken, cat_goal, day_goal, day)
        back = lax.all_to_all(back, "item", 0, 0, tiled=True)
        part = pl.pallas_call(
            margin_kernel,
            out_shape=margin,
            in_specs=vmem(3),
            out_specs=vmem(1)[0],
            name="margin",
        )(back, flat, tid)

    back = pl.pallas_call(
        functools.partial(owner_kernel, True),
        out_shape=jax.ShapeDtypeStruct((owners, 2 * SUB, LANES), F32),
        in_specs=vmem(4),
        out_specs=vmem(1)[0],
        name="owner_last",
    )(taken, cat_goal, day_goal, day)
    back = lax.all_to_all(back, "item", 0, 0, tiled=True)
    product_factor = factor.reshape(items // SUB, SUB).T.reshape(items)
    block = 16
    smem = pl.BlockSpec(memory_space=pltpu.SMEM)
    wide = pl.BlockSpec((block, days, stores), lambda i: (i, 0, 0))
    group_outlet_factor, outlet_date_factor, adjusted_tensor = pl.pallas_call(
        closing_kernel,
        grid=(items // block,),
        out_shape=(
            jax.ShapeDtypeStruct((cats, stores), F32),
            jax.ShapeDtypeStruct((days, stores), F32),
            jax.ShapeDtypeStruct((items, days, stores), BF16),
        ),
        in_specs=[smem, smem, pl.BlockSpec((owners, 2 * SUB, LANES), lambda i: (0, 0, 0)), wide],
        out_specs=(
            pl.BlockSpec((cats, stores), lambda i: (0, 0)),
            pl.BlockSpec((days, stores), lambda i: (0, 0)),
            wide,
        ),
        scratch_shapes=[pltpu.VMEM((SUB, days, stores), F32)],
        name="closing",
    )(product_group, product_factor, back, predicted_units)
    return (product_factor, group_outlet_factor, outlet_date_factor, adjusted_tensor)


def solution(mesh):
    in_specs = (P("item", None, "store"), P("item"), P("item"), P(None, "store"), P(None, "store"))
    out_specs = (P("item"), P(None, "store"), P(None, "store"), P("item", None, "store"))
    return jax.shard_map(shards, mesh=mesh, in_specs=in_specs, out_specs=out_specs, check_vma=False)
```

time: 434 us -> 205 us (0.47); the launches traced: 425 us -> 203 us
  blocking collectives: 216 us -> 117 us
  waiting for transfers between devices: 114 us -> 18.6 us
  Pallas kernels: 0 us -> 37.7 us
  other arithmetic: 29.8 us -> 1.29 us
  local copies, waits for them, and re-layouts: 23.9 us -> 7.85 us
  matrix products: 12.8 us -> 0 us
  starting transfers between devices: 26.9 us -> 20.1 us
    all_gather x4 -> x0, blocking collectives: 185 us -> none  [gather_together(): lines, at, done = (lax.all_gather(vector, axis), 0, [])]
    all_to_all x4 -> x3, waiting for transfers between devices: 114 us -> 18.6 us  [the longest x1 9.72 us: shards(): back = lax.all_to_all(back, 'item', 0, 0, tiled=True)]
    all_to_all x4 -> x9, blocking collectives: 31.5 us -> 117 us  [the longest x3 45.8 us: shards(): taken = lax.all_to_all(pooled, 'item', 0, 0, tiled=True)]
    pallas_call x0 -> x13, Pallas kernels: none -> 37.7 us  [the longest x4 10.7 us: shards(): pl.pallas_call(pool_kernel, out_shape=(message, line), in_specs=vmem(5),...]
    all_to_all x4 -> x0, other arithmetic: 17.6 us -> none  [sum_at_owner(): lax.all_to_all(tiles, axis, split_axis=0, concat_axis=0, tiled=True)]
    unnamed x28 -> x14, local copies, waits for them, and re-layouts: 18 us -> 2.31 us
    dot_general x9 -> x0, matrix products: 12.8 us -> none  [the longest x4 10.5 us: shards(): jnp.einsum('bv,bjz->vjz', indicator_matrix, pooled_masked_prediction, pre...]
    reduce_sum x35 -> x0, other arithmetic: 8.2 us -> none  [the longest x4 5.37 us: shards(): jnp.sum(predicted_units * masked_prediction, axis=(1, 2))]
  transfers between devices with their start and end apart: 4 -> 3, of which waited for: 4 -> 3; matrix products, arithmetic and copies ran while one was open for 0% -> 3% of each run, Pallas kernels for 0% -> 0%
where the time goes in v1:
time: 205 us; the launch traced here: 203 us
  blocking collectives  117 us (57%)
  Pallas kernels  37.7 us (18%)
  starting transfers between devices  20.1 us (10%)
  waiting for transfers between devices  18.6 us (9%)
  local copies, waits for them, and re-layouts  7.85 us (4%)
    all_to_all x3, blocking collectives, shards(): taken = lax.all_to_all(pooled, 'item', 0, 0, tiled=True)  45.8 us
    all_to_all x3, blocking collectives, shards(): back = lax.all_to_all(back, 'item', 0, 0, tiled=True)  44.7 us
    all_to_all x3, blocking collectives, shards(): total = lax.all_to_all(part, 'store', 0, 0, tiled=True)  26.5 us
    all_to_all x1, starting transfers between devices, shards(): taken = lax.all_to_all(pooled, 'item', 0, 0, tiled=True)  10.8 us
    pallas_call x4, Pallas kernels, shards(): pl.pallas_call(pool_kernel, out_shape=(message, line), in_specs=vmem(5),...  10.7 us
    all_to_all x1, waiting for transfers between devices, shards(): back = lax.all_to_all(back, 'item', 0, 0, tiled=True)  9.72 us
    pallas_call x3, Pallas kernels, shards(): pl.pallas_call(margin_kernel, out_shape=margin, in_specs=vmem(3), out_spe...  8.11 us
    pallas_call x3, Pallas kernels, shards(): pl.pallas_call(functools.partial(owner_kernel, False), out_shape=(message...  8.08 us
  transfers between devices with their start and end apart: 3, of which 3 were waited for; matrix products, arithmetic and copies ran while one was open for 3% of the time, Pallas kernels for 0%

profile of v1, /device:TPU:8, one launch (start us, length us, event | category | flops | bytes accessed | tf_op | source)
XLA Modules:
  0.0 203.3 jit_solution(6916283799563495695)
XLA Ops:
  0.6 2.5 %first.1 = (bf16[1024,512]{1,0:T(8,128)(2,1)}, f32[8,1,128]{2,1,0:T(1,128)}) custom-call(bf16[128,8,512]{2,1,0:T(8,128)(2,1)} %x_ref.3), custom_call_target="tpu_custom_call" | custom-call | tf_op jit(solution)/shard_map/first/pallas_call | solution.py:215
  3.1 5.4 %all-to-all-start = ((f32[8,1,128]{2,1,0:T(1,128)}), f32[8,1,128]{2,1,0:T(1,128)S(1)}, u32[]{:S(2)}, u32[]{:S(2)}) async-start(f32[8,1,128]{2,1,0:T(1,128)} %get-tuple-element.20), calls=%async_computation | async-start | bytes 8192 | tf_op jit(solution)/shard_map/all_to_all | solution.py:223
  8.5 0.7 copy-done.4
  9.2 0.1 broadcast_in_dim.19
  9.3 0.1 broadcast_in_dim.21
  9.5 0.6 broadcast_add_fusion.tid_ref
  10.1 0.6 copy-done.5
  10.8 0.6 reshape.44.goal_ref
  11.5 0.8 all-to-all-done.margin_ref
  12.3 0.5 broadcast_in_dim.23.base_ref
  12.8 0.1 copy-done.3
  12.9 2.7 %pool.4 = (f32[32,8,128]{2,1,0:T(8,128)}, f32[1,128]{1,0:T(1,128)}) custom-call(f32[8,1,128]{2,1,0:T(1,128)} %copy-done.3, f32[1,128]{1,0:T(1,128)} %reshape.44.goal_ref, bf16[1024,512]{1,0:T(8,128)(2,1)} %get-tuple-element.21.flat_ref, s32[8,128]{1,0:T(8,128)} %broadcast_add_fusion.tid_ref, f32[1,128]{1,0:T(1,128)} %broadcast_in_dim.23.base_ref), custom_call_target="tpu_custom_call" | custom-call | tf_op jit(solution)/shard_map/pool/pallas_call | solution.py:224
  15.6 10.8 %all-to-all-start.1 = ((f32[32,8,128]{2,1,0:T(8,128)}), f32[32,8,128]{2,1,0:T(8,128)S(1)}, u32[]{:S(2)}, u32[]{:S(2)}) async-start(f32[32,8,128]{2,1,0:T(8,128)} %get-tuple-element.22), calls=%async_computation.1 | async-start | bytes 262144 | tf_op jit(solution)/shard_map/all_to_all | solution.py:231
  26.4 0.8 constant_dynamic-slice_fusion
  27.2 0.6 reshape.45.day_goal_ref
  27.8 0.1 constant_dynamic-slice_fusion.1
  27.9 0.7 copy.13.cat_goal_ref
  28.6 8.0 %all-to-all-done.1.taken_ref = f32[32,8,128]{2,1,0:T(8,128)S(1)} async-done(((f32[32,8,128]{2,1,0:T(8,128)}), f32[32,8,128]{2,1,0:T(8,128)S(1)}, u32[]{:S(2)}, u32[]{:S(2)}) %all-to-all-start.1) | async-done | bytes 131104 | tf_op jit(solution)/shard_map/all_to_all | solution.py:231
  36.7 0.5 broadcast_in_dim.24.day_ref
  37.2 0.1 copy-done.2
  37.3 2.7 %owner.3 = (f32[32,8,128]{2,1,0:T(8,128)}, f32[1,128]{1,0:T(1,128)}) custom-call(f32[32,8,128]{2,1,0:T(8,128)} %copy-done.2, f32[64,128]{1,0:T(8,128)} %copy.13.cat_goal_ref, f32[1,128]{1,0:T(1,128)} %reshape.45.day_goal_ref, f32[1,128]{1,0:T(1,128)} %broadcast_in_dim.24.day_ref), custom_call_target="tpu_custom_call" | custom-call | tf_op jit(solution)/shard_map/owner/pallas_call | solution.py:234
  40.0 14.9 %all_to_all.60.back_ref = f32[32,8,128]{2,1,0:T(8,128)} all-to-all(f32[32,8,128]{2,1,0:T(8,128)} %get-tuple-element.23), channel_id=1, replica_groups=mesh['item'=32,'store'=8] {'item'}, dimensions={0} | all-to-all | bytes 262144 | tf_op jit(solution)/shard_map/all_to_all | solution.py:241
  54.9 2.7 %margin.3 = f32[8,1,128]{2,1,0:T(1,128)} custom-call(f32[32,8,128]{2,1,0:T(8,128)} %all_to_all.60.back_ref, bf16[1024,512]{1,0:T(8,128)(2,1)} %get-tuple-element.21.flat_ref, s32[8,128]{1,0:T(8,128)} %broadcast_add_fusion.tid_ref), custom_call_target="tpu_custom_call" | custom-call | tf_op jit(solution)/shard_map/margin/pallas_call | solution.py:242
  57.6 9.0 %all_to_all.61.margin_ref = f32[8,1,128]{2,1,0:T(1,128)} all-to-all(f32[8,1,128]{2,1,0:T(1,128)} %margin.3), channel_id=1, replica_groups=mesh['item'=32,'store'=8] {'store'}, dimensions={0} | all-to-all | bytes 8192 | tf_op jit(solution)/shard_map/all_to_all | solution.py:223
  66.6 2.7 %pool.5 = (f32[32,8,128]{2,1,0:T(8,128)}, f32[1,128]{1,0:T(1,128)}) custom-call(f32[8,1,128]{2,1,0:T(1,128)} %all_to_all.61.margin_ref, f32[1,128]{1,0:T(1,128)} %reshape.44.goal_ref, bf16[1024,512]{1,0:T(8,128)(2,1)} %get-tuple-element.21.flat_ref, s32[8,128]{1,0:T(8,128)} %broadcast_add_fusion.tid_ref, f32[1,128]{1,0:T(1,128)} %broadcast_in_dim.23.base_ref), custom_call_target="tpu_custom_call" | custom-call | tf_op jit(solution)/shard_map/pool/pallas_call | solution.py:224
  69.2 15.3 %all_to_all.62.taken_ref = f32[32,8,128]{2,1,0:T(8,128)} all-to-all(f32[32,8,128]{2,1,0:T(8,128)} %get-tuple-element.24), channel_id=1, replica_groups=mesh['item'=32,'store'=8] {'item'}, dimensions={0} | all-to-all | bytes 262144 | tf_op jit(solution)/shard_map/all_to_all | solution.py:231
  84.5 2.7 %owner.4 = (f32[32,8,128]{2,1,0:T(8,128)}, f32[1,128]{1,0:T(1,128)}) custom-call(f32[32,8,128]{2,1,0:T(8,128)} %all_to_all.62.taken_ref, f32[64,128]{1,0:T(8,128)} %copy.13.cat_goal_ref, f32[1,128]{1,0:T(1,128)} %reshape.45.day_goal_ref, f32[1,128]{1,0:T(1,128)} %get-tuple-element.25.day_ref), custom_call_target="tpu_custom_call" | custom-call | tf_op jit(solution)/shard_map/owner/pallas_call | solution.py:234
  87.2 14.9 %all_to_all.63.back_ref = f32[32,8,128]{2,1,0:T(8,128)} all-to-all(f32[32,8,128]{2,1,0:T(8,128)} %get-tuple-element.26), channel_id=1, replica_groups=mesh['item'=32,'store'=8] {'item'}, dimensions={0} | all-to-all | bytes 262144 | tf_op jit(solution)/shard_map/all_to_all | solution.py:241
  102.1 2.7 %margin.4 = f32[8,1,128]{2,1,0:T(1,128)} custom-call(f32[32,8,128]{2,1,0:T(8,128)} %all_to_all.63.back_ref, bf16[1024,512]{1,0:T(8,128)(2,1)} %get-tuple-element.21.flat_ref, s32[8,128]{1,0:T(8,128)} %broadcast_add_fusion.tid_ref), custom_call_target="tpu_custom_call" | custom-call | tf_op jit(solution)/shard_map/margin/pallas_call | solution.py:242
  104.8 8.7 %all_to_all.64.margin_ref = f32[8,1,128]{2,1,0:T(1,128)} all-to-all(f32[8,1,128]{2,1,0:T(1,128)} %margin.4), channel_id=1, replica_groups=mesh['item'=32,'store'=8] {'store'}, dimensions={0} | all-to-all | bytes 8192 | tf_op jit(solution)/shard_map/all_to_all | solution.py:223
  113.6 2.7 %pool.6 = (f32[32,8,128]{2,1,0:T(8,128)}, f32[1,128]{1,0:T(1,128)}) custom-call(f32[8,1,128]{2,1,0:T(1,128)} %all_to_all.64.margin_ref, f32[1,128]{1,0:T(1,128)} %reshape.44.goal_ref, bf16[1024,512]{1,0:T(8,128)(2,1)} %get-tuple-element.21.flat_ref, s32[8,128]{1,0:T(8,128)} %broadcast_add_fusion.tid_ref, f32[1,128]{1,0:T(1,128)} %broadcast_in_dim.23.base_ref), custom_call_target="tpu_custom_call" | custom-call | tf_op jit(solution)/shard_map/pool/pallas_call | solution.py:224
  116.2 15.3 %all_to_all.65.taken_ref = f32[32,8,128]{2,1,0:T(8,128)} all-to-all(f32[32,8,128]{2,1,0:T(8,128)} %get-tuple-element.27), channel_id=1, replica_groups=mesh['item'=32,'store'=8] {'item'}, dimensions={0} | all-to-all | bytes 262144 | tf_op jit(solution)/shard_map/all_to_all | solution.py:231
  131.5 2.7 %owner.5 = (f32[32,8,128]{2,1,0:T(8,128)}, f32[1,128]{1,0:T(1,128)}) custom-call(f32[32,8,128]{2,1,0:T(8,128)} %all_to_all.65.taken_ref, f32[64,128]{1,0:T(8,128)} %copy.13.cat_goal_ref, f32[1,128]{1,0:T(1,128)} %reshape.45.day_goal_ref, f32[1,128]{1,0:T(1,128)} %get-tuple-element.28.day_ref), custom_call_target="tpu_custom_call" | custom-call | tf_op jit(solution)/shard_map/owner/pallas_call | solution.py:234
  134.2 14.9 %all_to_all.66.back_ref = f32[32,8,128]{2,1,0:T(8,128)} all-to-all(f32[32,8,128]{2,1,0:T(8,128)} %get-tuple-element.29), channel_id=1, replica_groups=mesh['item'=32,'store'=8] {'item'}, dimensions={0} | all-to-all | bytes 262144 | tf_op jit(solution)/shard_map/all_to_all | solution.py:241
  149.1 2.7 %margin.5 = f32[8,1,128]{2,1,0:T(1,128)} custom-call(f32[32,8,128]{2,1,0:T(8,128)} %all_to_all.66.back_ref, bf16[1024,512]{1,0:T(8,128)(2,1)} %get-tuple-element.21.flat_ref, s32[8,128]{1,0:T(8,128)} %broadcast_add_fusion.tid_ref), custom_call_target="tpu_custom_call" | custom-call | tf_op jit(solution)/shard_map/margin/pallas_call | solution.py:242
  151.8 8.7 %all_to_all.67.margin_ref = f32[8,1,128]{2,1,0:T(1,128)} all-to-all(f32[8,1,128]{2,1,0:T(1,128)} %margin.5), channel_id=1, replica_groups=mesh['item'=32,'store'=8] {'store'}, dimensions={0} | all-to-all | bytes 8192 | tf_op jit(solution)/shard_map/all_to_all | solution.py:223
  160.6 2.7 %pool.7 = (f32[32,8,128]{2,1,0:T(8,128)}, f32[1,128]{1,0:T(1,128)}) custom-call(f32[8,1,128]{2,1,0:T(1,128)} %all_to_all.67.margin_ref, f32[1,128]{1,0:T(1,128)} %reshape.44.goal_ref, bf16[1024,512]{1,0:T(8,128)(2,1)} %get-tuple-element.21.flat_ref, s32[8,128]{1,0:T(8,128)} %broadcast_add_fusion.tid_ref, f32[1,128]{1,0:T(1,128)} %broadcast_in_dim.23.base_ref), custom_call_target="tpu_custom_call" | custom-call | tf_op jit(solution)/shard_map/pool/pallas_call | solution.py:224
  163.2 15.3 %all_to_all.68.taken_ref = f32[32,8,128]{2,1,0:T(8,128)} all-to-all(f32[32,8,128]{2,1,0:T(8,128)} %get-tuple-element.31), channel_id=1, replica_groups=mesh['item'=32,'store'=8] {'item'}, dimensions={0} | all-to-all | bytes 262144 | tf_op jit(solution)/shard_map/all_to_all | solution.py:231
  178.5 2.5 %owner_last.1 = f32[32,16,128]{2,1,0:T(8,128)} custom-call(f32[32,8,128]{2,1,0:T(8,128)} %all_to_all.68.taken_ref, f32[64,128]{1,0:T(8,128)} %copy.13.cat_goal_ref, f32[1,128]{1,0:T(1,128)} %reshape.45.day_goal_ref, f32[1,128]{1,0:T(1,128)} %get-tuple-element.32.day_ref), custom_call_target="tpu_custom_call" | custom-call | tf_op jit(solution)/shard_map/owner_last/pallas_call | solution.py:250
  181.1 3.9 %all-to-all-start.11 = ((f32[32,16,128]{2,1,0:T(8,128)}), f32[32,16,128]{2,1,0:T(8,128)S(1)}, u32[]{:S(2)}, u32[]{:S(2)}) async-start(f32[32,16,128]{2,1,0:T(8,128)} %owner_last.1), calls=%async_computation.11 | async-start | bytes 524288 | tf_op jit(solution)/shard_map/all_to_all | solution.py:257
  184.9 0.5 broadcast.34
  185.5 0.1 copy-done.6
  185.6 0.7 reduce.3
  186.3 0.1 reshape.46
  186.4 0.6 reshape.47.factor_ref
  187.0 9.7 %all-to-all-done.11.back_ref = f32[32,16,128]{2,1,0:T(8,128)S(1)} async-done(((f32[32,16,128]{2,1,0:T(8,128)}), f32[32,16,128]{2,1,0:T(8,128)S(1)}, u32[]{:S(2)}, u32[]{:S(2)}) %all-to-all-start.11) | async-done | bytes 262176 | tf_op jit(solution)/shard_map/all_to_all | solution.py:257
  196.7 0.7 copy-done.1
  197.4 5.9 %closing.1 = (f32[64,512]{1,0:T(8,128)}, f32[8,512]{1,0:T(8,128)}, bf16[128,8,512]{2,1,0:T(8,128)(2,1)}) custom-call(s32[128]{0:T(128)} %group_ref.1, f32[128]{0:T(128)} %reshape.47.factor_ref, f32[32,16,128]{2,1,0:T(8,128)} %copy-done.1, bf16[128,8,512]{2,1,0:T(8,128)(2,1)} %x_ref.3), custom_call_target="tpu_custom_call" | custom-call | tf_op jit(solution)/shard_map/closing/pallas_call | solution.py:262
  (16 shorter events, 0.4 us)
Async XLA Ops:
  0.6 27.1 %copy-start = (f32[64,512]{1,0:T(8,128)S(1)}, f32[64,512]{1,0:T(8,128)}, u32[]{:S(2)}) copy-start(f32[64,512]{1,0:T(8,128)} %param.8) | copy-start | bytes 393220
  3.1 9.2 %all-to-all-start = ((f32[8,1,128]{2,1,0:T(1,128)}), f32[8,1,128]{2,1,0:T(1,128)S(1)}, u32[]{:S(2)}, u32[]{:S(2)}) async-start(f32[8,1,128]{2,1,0:T(1,128)} %get-tuple-element.20), calls=%async_computation | async-start | bytes 8192 | tf_op jit(solution)/shard_map/all_to_all | solution.py:223
  8.5 0.7 copy-start.4
  10.0 0.7 copy-start.5
  12.3 0.6 copy-start.3
  15.6 21.1 %all-to-all-start.1 = ((f32[32,8,128]{2,1,0:T(8,128)}), f32[32,8,128]{2,1,0:T(8,128)S(1)}, u32[]{:S(2)}, u32[]{:S(2)}) async-start(f32[32,8,128]{2,1,0:T(8,128)} %get-tuple-element.22), calls=%async_computation.1 | async-start | bytes 262144 | tf_op jit(solution)/shard_map/all_to_all | solution.py:231
  36.7 0.7 copy-start.2
  181.1 15.7 %all-to-all-start.11 = ((f32[32,16,128]{2,1,0:T(8,128)}), f32[32,16,128]{2,1,0:T(8,128)S(1)}, u32[]{:S(2)}, u32[]{:S(2)}) async-start(f32[32,16,128]{2,1,0:T(8,128)} %owner_last.1), calls=%async_computation.11 | async-start | bytes 524288 | tf_op jit(solution)/shard_map/all_to_all | solution.py:257
  184.9 0.7 copy-start.6
  196.7 0.7 copy-start.1

commit v2 on v1

--- a/solution.py
+++ b/solution.py
@@ -192,6 +192,13 @@
     return [pl.BlockSpec(memory_space=pltpu.VMEM)] * count
 
 
+def held(x):
+    return pltpu.with_memory_space_constraint(x, pltpu.VMEM)
+
+
+LIMIT = pltpu.CompilerParams(vmem_limit_bytes=8 * 1024 * 1024)
+
+
 def shards(predicted_units, product_group, product_goal, group_outlet_goal, outlet_date_goal):
     items, days, stores = predicted_units.shape
     cats = group_outlet_goal.shape[0]
@@ -200,9 +207,9 @@
     beside = lax.axis_size("store")
     at = lax.axis_index("item") * width
 
-    message = jax.ShapeDtypeStruct((owners, SUB, LANES), F32)
-    margin = jax.ShapeDtypeStruct((beside, 1, LANES), F32)
-    line = jax.ShapeDtypeStruct((1, LANES), F32)
+    message = pltpu.VMEM((owners, SUB, LANES), F32)
+    margin = pltpu.VMEM((beside, 1, LANES), F32)
+    line = pltpu.VMEM((1, LANES), F32)
 
     slot = product_group - product_group[0]
     tid = jnp.repeat(slot, days).reshape(SUB, LANES) + (jnp.arange(LANES, dtype=jnp.int32) % days)[None] * SUB
@@ -214,9 +221,10 @@
 
     flat, part = pl.pallas_call(
         first_kernel,
-        out_shape=(jax.ShapeDtypeStruct((items * days, stores), BF16), margin),
+        out_shape=(pltpu.VMEM((items * days, stores), BF16), margin),
         in_specs=vmem(1),
         out_specs=tuple(vmem(2)),
+        compiler_params=LIMIT,
         name="first",
     )(predicted_units)
     for round_index in range(ROUNDS):
@@ -226,8 +234,9 @@
             out_shape=(message, line),
             in_specs=vmem(5),
             out_specs=tuple(vmem(2)),
-            name="pool",
-        )(total, goal, flat, tid, base)
+            compiler_params=LIMIT,
+        name="pool",
+        )(*map(held, (total, goal, flat, tid, base)))
         taken = lax.all_to_all(pooled, "item", 0, 0, tiled=True)
         if round_index == ROUNDS - 1:
             break
@@ -236,24 +245,27 @@
             out_shape=(message, line),
             in_specs=vmem(4),
             out_specs=tuple(vmem(2)),
-            name="owner",
-        )(taken, cat_goal, day_goal, day)
+            compiler_params=LIMIT,
+        name="owner",
+        )(*map(held, (taken, cat_goal, day_goal, day)))
         back = lax.all_to_all(back, "item", 0, 0, tiled=True)
         part = pl.pallas_call(
             margin_kernel,
             out_shape=margin,
             in_specs=vmem(3),
             out_specs=vmem(1)[0],
-            name="margin",
-        )(back, flat, tid)
+            compiler_params=LIMIT,
+        name="margin",
+        )(*map(held, (back, flat, tid)))
 
     back = pl.pallas_call(
         functools.partial(owner_kernel, True),
-        out_shape=jax.ShapeDtypeStruct((owners, 2 * SUB, LANES), F32),
+        out_shape=pltpu.VMEM((owners, 2 * SUB, LANES), F32),
         in_specs=vmem(4),
         out_specs=vmem(1)[0],
+        compiler_params=LIMIT,
         name="owner_last",
-    )(taken, cat_goal, day_goal, day)
+    )(*map(held, (taken, cat_goal, day_goal, day)))
     back = lax.all_to_all(back, "item", 0, 0, tiled=True)
     product_factor = factor.reshape(items // SUB, SUB).T.reshape(items)
     block = 16
@@ -274,6 +286,7 @@
             wide,
         ),
         scratch_shapes=[pltpu.VMEM((SUB, days, stores), F32)],
+        compiler_params=LIMIT,
         name="closing",
     )(product_group, product_factor, back, predicted_units)
     return (product_factor, group_outlet_factor, outlet_date_factor, adjusted_tensor)

time: 205 us -> 171 us (0.83)
  Pallas kernels: 37.7 us -> 16.3 us
  blocking collectives: 117 us -> 106 us
  local copies, waits for them, and re-layouts: 7.85 us -> 4.86 us
  waiting for transfers between devices: 18.6 us -> 21 us
    pallas_call x4, Pallas kernels: 10.7 us -> 3.67 us  [shards(): pl.pallas_call(pool_kernel, out_shape=(message, line), in_specs=vmem(5),...]
    pallas_call x3, Pallas kernels: 8.11 us -> 2.64 us  [shards(): pl.pallas_call(margin_kernel, out_shape=margin, in_specs=vmem(3), out_spe...]
    pallas_call x3, Pallas kernels: 8.08 us -> 3.31 us  [shards(): pl.pallas_call(functools.partial(owner_kernel, False), out_shape=(message...]
    all_to_all x3, blocking collectives: 45.8 us -> 41.3 us  [shards(): taken = lax.all_to_all(pooled, 'item', 0, 0, tiled=True)]
    all_to_all x3, blocking collectives: 26.5 us -> 22.9 us  [shards(): total = lax.all_to_all(part, 'store', 0, 0, tiled=True)]
    all_to_all x3, blocking collectives: 44.7 us -> 41.9 us  [shards(): back = lax.all_to_all(back, 'item', 0, 0, tiled=True)]
    pallas_call x2, Pallas kernels: 5.01 us -> 2.83 us  [the longest x1 1.62 us: shards(): pl.pallas_call(functools.partial(owner_kernel, True), out_shape=pltpu.VME...]
  transfers between devices with their start and end apart: 3 -> 3, of which waited for: 3 -> 3; matrix products, arithmetic and copies ran while one was open for 3% -> 2% of each run, Pallas kernels for 0% -> 0%
where the time goes in v2:
time: 171 us; the launch traced here: 170 us
  blocking collectives  106 us (62%)
  waiting for transfers between devices  21 us (12%)
  starting transfers between devices  20.1 us (12%)
  Pallas kernels  16.3 us (10%)
  local copies, waits for them, and re-layouts  4.86 us (3%)
    all_to_all x3, blocking collectives, shards(): back = lax.all_to_all(back, 'item', 0, 0, tiled=True)  41.9 us
    all_to_all x3, blocking collectives, shards(): taken = lax.all_to_all(pooled, 'item', 0, 0, tiled=True)  41.3 us
    all_to_all x3, blocking collectives, shards(): total = lax.all_to_all(part, 'store', 0, 0, tiled=True)  22.9 us
    all_to_all x1, starting transfers between devices, shards(): taken = lax.all_to_all(pooled, 'item', 0, 0, tiled=True)  10.8 us
    all_to_all x1, waiting for transfers between devices, shards(): back = lax.all_to_all(back, 'item', 0, 0, tiled=True)  9.86 us
    all_to_all x1, waiting for transfers between devices, shards(): taken = lax.all_to_all(pooled, 'item', 0, 0, tiled=True)  9.19 us
    all_to_all x1, starting transfers between devices, shards(): total = lax.all_to_all(part, 'store', 0, 0, tiled=True)  5.38 us
    all_to_all x1, starting transfers between devices, shards(): back = lax.all_to_all(back, 'item', 0, 0, tiled=True)  3.87 us
  transfers between devices with their start and end apart: 3, of which 3 were waited for; matrix products, arithmetic and copies ran while one was open for 2% of the time, Pallas kernels for 0%

profile of v2, /device:TPU:8, one launch (start us, length us, event | category | flops | bytes accessed | tf_op | source)
XLA Modules:
  0.0 169.7 jit_solution(647531521129893375)
XLA Ops:
  0.6 0.0 copy-start
  0.7 1.3 copy-done.1
  1.9 1.2 first.1
  3.1 5.4 %all-to-all-start = ((f32[8,1,128]{2,1,0:T(1,128)}), f32[8,1,128]{2,1,0:T(1,128)S(1)}, u32[]{:S(2)}, u32[]{:S(2)}) async-start(f32[8,1,128]{2,1,0:T(1,128)} %get-tuple-element.20), calls=%async_computation | async-start | bytes 8192 | tf_op jit(solution)/shard_map/all_to_all | solution.py:231
  8.5 0.7 copy-done.4
  9.2 0.1 broadcast_in_dim.19
  9.3 0.1 broadcast_in_dim.20
  9.4 0.1 broadcast_in_dim.21
  9.5 0.6 copy-done.5
  10.1 0.1 reshape.43
  10.2 0.1 copy.11
  10.3 0.1 reshape.44.goal_ref
  10.4 1.9 %all-to-all-done.margin_ref = f32[8,1,128]{2,1,0:T(1,128)S(1)} async-done(((f32[8,1,128]{2,1,0:T(1,128)}), f32[8,1,128]{2,1,0:T(1,128)S(1)}, u32[]{:S(2)}, u32[]{:S(2)}) %all-to-all-start) | async-done | bytes 4128 | tf_op jit(solution)/shard_map/all_to_all | solution.py:231
  12.3 1.4 pool.4
  13.7 10.8 %all-to-all-start.1 = ((f32[32,8,128]{2,1,0:T(8,128)}), f32[32,8,128]{2,1,0:T(8,128)S(1)}, u32[]{:S(2)}, u32[]{:S(2)}) async-start(f32[32,8,128]{2,1,0:T(8,128)} %get-tuple-element.22), calls=%async_computation.1 | async-start | bytes 262144 | tf_op jit(solution)/shard_map/all_to_all | solution.py:240
  24.5 0.8 constant_dynamic-slice_fusion
  25.3 0.1 reshape.45.day_goal_ref
  25.4 0.1 constant_dynamic-slice_fusion.1
  25.5 0.1 copy.12
  25.5 0.1 copy.13.cat_goal_ref
  25.6 9.2 %all-to-all-done.1.taken_ref = f32[32,8,128]{2,1,0:T(8,128)S(1)} async-done(((f32[32,8,128]{2,1,0:T(8,128)}), f32[32,8,128]{2,1,0:T(8,128)S(1)}, u32[]{:S(2)}, u32[]{:S(2)}) %all-to-all-start.1) | async-done | bytes 131104 | tf_op jit(solution)/shard_map/all_to_all | solution.py:240
  34.8 1.1 owner.3
  35.9 13.9 %all_to_all.60.back_ref = f32[32,8,128]{2,1,0:T(8,128)S(1)} all-to-all(f32[32,8,128]{2,1,0:T(8,128)S(1)} %get-tuple-element.23), channel_id=1, replica_groups=mesh['item'=32,'store'=8] {'item'}, dimensions={0} | all-to-all | bytes 262144 | tf_op jit(solution)/shard_map/all_to_all | solution.py:251
  49.9 0.9 margin.3
  50.8 7.6 %all_to_all.61.margin_ref = f32[8,1,128]{2,1,0:T(1,128)S(1)} all-to-all(f32[8,1,128]{2,1,0:T(1,128)S(1)} %margin.3), channel_id=1, replica_groups=mesh['item'=32,'store'=8] {'store'}, dimensions={0} | all-to-all | bytes 8192 | tf_op jit(solution)/shard_map/all_to_all | solution.py:231
  58.4 0.8 pool.5
  59.1 13.8 %all_to_all.62.taken_ref = f32[32,8,128]{2,1,0:T(8,128)S(1)} all-to-all(f32[32,8,128]{2,1,0:T(8,128)S(1)} %get-tuple-element.24), channel_id=1, replica_groups=mesh['item'=32,'store'=8] {'item'}, dimensions={0} | all-to-all | bytes 262144 | tf_op jit(solution)/shard_map/all_to_all | solution.py:240
  72.9 1.1 owner.4
  74.0 14.0 %all_to_all.63.back_ref = f32[32,8,128]{2,1,0:T(8,128)S(1)} all-to-all(f32[32,8,128]{2,1,0:T(8,128)S(1)} %get-tuple-element.26), channel_id=1, replica_groups=mesh['item'=32,'store'=8] {'item'}, dimensions={0} | all-to-all | bytes 262144 | tf_op jit(solution)/shard_map/all_to_all | solution.py:251
  88.0 0.9 margin.4
  88.8 7.6 %all_to_all.64.margin_ref = f32[8,1,128]{2,1,0:T(1,128)S(1)} all-to-all(f32[8,1,128]{2,1,0:T(1,128)S(1)} %margin.4), channel_id=1, replica_groups=mesh['item'=32,'store'=8] {'store'}, dimensions={0} | all-to-all | bytes 8192 | tf_op jit(solution)/shard_map/all_to_all | solution.py:231
  96.5 0.8 pool.6
  97.2 13.8 %all_to_all.65.taken_ref = f32[32,8,128]{2,1,0:T(8,128)S(1)} all-to-all(f32[32,8,128]{2,1,0:T(8,128)S(1)} %get-tuple-element.27), channel_id=1, replica_groups=mesh['item'=32,'store'=8] {'item'}, dimensions={0} | all-to-all | bytes 262144 | tf_op jit(solution)/shard_map/all_to_all | solution.py:240
  111.0 1.1 owner.5
  112.1 13.9 %all_to_all.66.back_ref = f32[32,8,128]{2,1,0:T(8,128)S(1)} all-to-all(f32[32,8,128]{2,1,0:T(8,128)S(1)} %get-tuple-element.29), channel_id=1, replica_groups=mesh['item'=32,'store'=8] {'item'}, dimensions={0} | all-to-all | bytes 262144 | tf_op jit(solution)/shard_map/all_to_all | solution.py:251
  126.1 0.9 margin.5
  127.0 7.6 %all_to_all.67.margin_ref = f32[8,1,128]{2,1,0:T(1,128)S(1)} all-to-all(f32[8,1,128]{2,1,0:T(1,128)S(1)} %margin.5), channel_id=1, replica_groups=mesh['item'=32,'store'=8] {'store'}, dimensions={0} | all-to-all | bytes 8192 | tf_op jit(solution)/shard_map/all_to_all | solution.py:231
  134.6 0.7 pool.7
  135.4 13.8 %all_to_all.68.taken_ref = f32[32,8,128]{2,1,0:T(8,128)S(1)} all-to-all(f32[32,8,128]{2,1,0:T(8,128)S(1)} %get-tuple-element.31), channel_id=1, replica_groups=mesh['item'=32,'store'=8] {'item'}, dimensions={0} | all-to-all | bytes 262144 | tf_op jit(solution)/shard_map/all_to_all | solution.py:240
  149.1 1.6 owner_last.1
  150.7 3.9 %all-to-all-start.11 = ((f32[32,16,128]{2,1,0:T(8,128)}), f32[32,16,128]{2,1,0:T(8,128)S(1)}, u32[]{:S(2)}, u32[]{:S(2)}) async-start(f32[32,16,128]{2,1,0:T(8,128)} %owner_last.1), calls=%async_computation.11 | async-start | bytes 524288 | tf_op jit(solution)/shard_map/all_to_all | solution.py:269
  154.6 0.5 broadcast.34
  155.1 0.7 reduce.3
  155.8 0.1 reshape.46
  155.9 0.1 copy.16
  156.0 0.1 reshape.47.factor_ref
  156.0 9.9 %all-to-all-done.11.back_ref = f32[32,16,128]{2,1,0:T(8,128)S(1)} async-done(((f32[32,16,128]{2,1,0:T(8,128)}), f32[32,16,128]{2,1,0:T(8,128)S(1)}, u32[]{:S(2)}, u32[]{:S(2)}) %all-to-all-start.11) | async-done | bytes 262176 | tf_op jit(solution)/shard_map/all_to_all | solution.py:269
  165.9 3.8 %closing.1 = (f32[64,512]{1,0:T(8,128)}, f32[8,512]{1,0:T(8,128)}, bf16[128,8,512]{2,1,0:T(8,128)(2,1)}) custom-call(s32[128]{0:T(128)S(1)} %copy-done.4, f32[128]{0:T(128)S(1)} %reshape.47.factor_ref, f32[32,16,128]{2,1,0:T(8,128)S(1)} %all-to-all-done.11.back_ref, bf16[128,8,512]{2,1,0:T(8,128)(2,1)S(1)} %copy-done.2), custom_call_target="tpu_custom_call" | custom-call | tf_op jit(solution)/shard_map/closing/pallas_call | solution.py:274
  (14 shorter events, 0.1 us)
Async XLA Ops:
  0.6 24.8 %copy-start = (f32[64,512]{1,0:T(8,128)S(1)}, f32[64,512]{1,0:T(8,128)}, u32[]{:S(2)}) copy-start(f32[64,512]{1,0:T(8,128)} %param.8) | copy-start | bytes 393220
  0.6 1.3 copy-start.1
  3.1 9.2 %all-to-all-start = ((f32[8,1,128]{2,1,0:T(1,128)}), f32[8,1,128]{2,1,0:T(1,128)S(1)}, u32[]{:S(2)}, u32[]{:S(2)}) async-start(f32[8,1,128]{2,1,0:T(1,128)} %get-tuple-element.20), calls=%async_computation | async-start | bytes 8192 | tf_op jit(solution)/shard_map/all_to_all | solution.py:231
  8.5 0.7 copy-start.4
  9.5 0.7 copy-start.5
  13.7 21.1 %all-to-all-start.1 = ((f32[32,8,128]{2,1,0:T(8,128)}), f32[32,8,128]{2,1,0:T(8,128)S(1)}, u32[]{:S(2)}, u32[]{:S(2)}) async-start(f32[32,8,128]{2,1,0:T(8,128)} %get-tuple-element.22), calls=%async_computation.1 | async-start | bytes 262144 | tf_op jit(solution)/shard_map/all_to_all | solution.py:240
  134.6 31.3 %copy-start.2 = (bf16[128,8,512]{2,1,0:T(8,128)(2,1)S(1)}, bf16[128,8,512]{2,1,0:T(8,128)(2,1)}, u32[]{:S(2)}) copy-start(bf16[128,8,512]{2,1,0:T(8,128)(2,1)} %x_ref.3) | copy-start | bytes 3145732
  150.7 15.2 %all-to-all-start.11 = ((f32[32,16,128]{2,1,0:T(8,128)}), f32[32,16,128]{2,1,0:T(8,128)S(1)}, u32[]{:S(2)}, u32[]{:S(2)}) async-start(f32[32,16,128]{2,1,0:T(8,128)} %owner_last.1), calls=%async_computation.11 | async-start | bytes 524288 | tf_op jit(solution)/shard_map/all_to_all | solution.py:269
  156.0 13.7 %copy-start.3 = (f32[128]{0:T(128)}, f32[128]{0:T(128)S(1)}, u32[]{:S(2)}) copy-start(f32[128]{0:T(128)S(1)} %reshape.47.factor_ref) | copy-start | bytes 1540

commit v3 on v2

v3 whole, which is shorter than its diff:
```python
import functools

import jax
import jax.numpy as jnp
from jax import lax
from jax.experimental import pallas as pl
from jax.experimental.pallas import tpu as pltpu
from jax.sharding import PartitionSpec as P

ROUNDS = 4
INNER = 3
LANES = 128
SUB = 8
SLOTS = 5
BASE_ROW = 7

F32 = jnp.float32
BF16 = jnp.bfloat16


def iota(shape, dim):
    return lax.broadcasted_iota(jnp.int32, shape, dim)


def two_parts(x):
    high = x.astype(BF16)
    low = (x - high.astype(F32)).astype(BF16)
    return high, low


def swap_blocks(tiles):
    count = len(tiles)
    width = LANES // count
    group = iota(tiles[0].shape, 1) // width
    bit = 1
    while bit < count:
        low = (group & bit) == 0
        fresh = []
        for a in range(count):
            other = tiles[a ^ bit]
            if a & bit == 0:
                fresh.append(jnp.where(low, tiles[a], pltpu.roll(other, bit * width, 1)))
            else:
                fresh.append(jnp.where(low, pltpu.roll(other, LANES - bit * width, 1), tiles[a]))
        tiles = fresh
        bit *= 2
    return tiles


def eight_sum(x):
    lane = iota(x.shape, 1)
    for bit in (1, 2, 4):
        x = x + jnp.where((lane & bit) == 0, pltpu.roll(x, LANES - bit, 1), pltpu.roll(x, bit, 1))
    return x


def compacted(rows):
    row = iota((SUB, LANES), 0)
    tile = rows[0]
    for q in range(1, SUB):
        tile = jnp.where(row == q, rows[q], tile)
    tile = eight_sum(tile)
    kept = jnp.where((iota((SUB, LANES), 1) & 7) == row, tile, 0.0)
    return jnp.sum(kept, axis=0, keepdims=True)


def expanded(line):
    line = jnp.broadcast_to(line, (SUB, LANES))
    return eight_sum(jnp.where((iota((SUB, LANES), 1) & 7) == iota((SUB, LANES), 0), line, 0.0))


def picked(x, index):
    return jnp.take_along_axis(x, index, axis=1)


def first_kernel(
    x_hbm, group_hbm, goal_hbm, cat_all_hbm, day_all_hbm,
    flat_ref, out_ref, tid_ref, line_ref, cat_goal_ref,
    x_buf, group_ref, goal_ref, cat_all_ref, day_all_ref, sems, small_sems,
):
    items, days, stores = x_hbm.shape
    chunks = sems.shape[0]
    block = items // chunks
    small = []
    for n, (src, dst) in enumerate(
        ((group_hbm, group_ref), (goal_hbm, goal_ref), (cat_all_hbm, cat_all_ref), (day_all_hbm, day_all_ref))
    ):
        small.append(pltpu.make_async_copy(src, dst, small_sems.at[n]))
        small[n].start()
    copies = []
    for n in range(chunks):
        rows = pl.ds(n * block, block)
        copies.append(pltpu.make_async_copy(x_hbm.at[rows], x_buf.at[rows], sems.at[n]))
        copies[n].start()
    for copy in small:
        copy.wait()

    row, lane = iota((SUB, LANES), 0), iota((SUB, LANES), 1)
    group = jnp.broadcast_to(group_ref[...], (SUB, LANES))
    first = picked(group, jnp.zeros_like(lane))
    slot = picked(group, row * (items // SUB) + lane // days) - first
    tid_ref[...] = (lane % days) * SUB + slot
    goal = jnp.broadcast_to(goal_ref[...], (SUB, LANES))
    line_ref[0:1] = picked(goal, (lane % SUB) * (items // SUB) + lane // SUB)[:1]
    line_ref[1:2] = first[:1].astype(F32)
    width = LANES // days
    at = lax.axis_index("item") * width
    there = pl.ds(pl.multiple_of(at // LANES * LANES, LANES), LANES)
    index = at % LANES + lane % width
    for k in range(cat_goal_ref.shape[0] // SUB):
        rows = slice(k * SUB, (k + 1) * SUB)
        cat_goal_ref[rows] = picked(cat_all_ref[rows, there], index)
    day_goal = jnp.where(lane // width == row, picked(day_all_ref[:, there], index), 0.0)
    line_ref[2:3] = jnp.sum(day_goal, axis=0, keepdims=True)

    tiles = []
    for n in range(chunks):
        copies[n].wait()
        x = x_buf[n * block : (n + 1) * block].astype(F32)
        flat = x.reshape(block * days, stores).astype(BF16)
        flat_ref[n * block * days : (n + 1) * block * days] = flat
        sums = lax.dot_general(
            jnp.ones((SUB, stores), BF16), flat, (((1,), (1,)), ((), ())), preferred_element_type=F32
        )
        tiles += [sums[:, q * LANES : (q + 1) * LANES] for q in range(block * days // LANES)]
    out_ref[...] = jnp.broadcast_to(compacted(tiles)[None], out_ref.shape)


def margin_kernel(back_ref, flat_ref, tid_ref, out_ref):
    stores = flat_ref.shape[1]
    columns = []
    for t in range(stores // LANES):
        columns.append(jnp.concatenate(swap_blocks([back_ref[t * SUB + j] for j in range(SUB)]), axis=0))
    weights = jnp.concatenate(columns, axis=1)
    parts = jnp.concatenate(two_parts(weights), axis=0)
    sums = lax.dot_general(parts, flat_ref[...], (((1,), (1,)), ((), ())), preferred_element_type=F32)
    half = weights.shape[0]
    sums = sums[:half] + sums[half:]
    which = iota((half, LANES), 0)
    rows = []
    for q in range(SUB):
        kept = jnp.where(which == tid_ref[q : q + 1, :], sums[:, q * LANES : (q + 1) * LANES], 0.0)
        rows.append(jnp.broadcast_to(jnp.sum(kept, axis=0, keepdims=True), (SUB, LANES)))
    line = compacted(rows)
    out_ref[...] = jnp.broadcast_to(line[None], out_ref.shape)


def pool_kernel(margin_ref, line_ref, flat_ref, tid_ref, out_ref, *factor_out):
    stores = flat_ref.shape[1]
    total = jnp.sum(margin_ref[...], axis=0)
    factor = line_ref[0:1] / total
    if factor_out:
        lane = iota((SUB, LANES), 1)
        index = lane % (LANES // SUB) * SUB + lane // (LANES // SUB)
        factor_out[0][...] = picked(jnp.broadcast_to(factor, (SUB, LANES)), index)[:1]
    spread = expanded(factor)
    half = SUB * SUB
    which = iota((half, LANES), 0)
    columns = []
    for q in range(SUB):
        columns.append(jnp.where(which == tid_ref[q : q + 1, :], spread[q : q + 1, :], 0.0))
    weights = jnp.concatenate(columns, axis=1)
    parts = jnp.concatenate(two_parts(weights), axis=0)
    sums = jnp.dot(parts, flat_ref[...], preferred_element_type=F32)
    sums = sums[:half] + sums[half:]
    row = iota((SUB, LANES), 0)
    base = jnp.broadcast_to(line_ref[1:2], (SUB, LANES))
    for t in range(stores // LANES):
        tiles = [sums[d * SUB : (d + 1) * SUB, t * LANES : (t + 1) * LANES] for d in range(SUB)]
        for j, tile in enumerate(swap_blocks(tiles)):
            out_ref[t * SUB + j] = jnp.where(row == BASE_ROW, base, tile)


def fitted(merged, cat_goal, day_goal, day):
    width = LANES // SUB
    for _ in range(INNER):
        below = merged * day
        step = LANES // 2
        while step >= width:
            below = below + pltpu.roll(below, step, 1)
            step //= 2
        cat = cat_goal / below
        day = day_goal / jnp.sum(merged * cat, axis=0, keepdims=True)
    return cat, day


def taken_parts(taken_ref):
    devices = taken_ref.shape[0]
    return jnp.concatenate(two_parts(taken_ref[...].reshape(devices * SUB, LANES)), axis=1)


def answer(place, cat, day, out_ref):
    cats = cat.shape[0]
    product = jnp.concatenate([cat * day, jnp.zeros((LANES - cats, LANES), F32)], axis=0)
    product = jnp.concatenate(two_parts(product), axis=1)
    sent = jnp.dot(place, product, preferred_element_type=F32)
    out_ref[...] = (sent[:, :LANES] + sent[:, LANES:]).reshape(out_ref.shape)


def owner_first_kernel(taken_ref, cat_goal_ref, line_ref, out_ref, day_ref, place_ref, across_ref):
    devices = taken_ref.shape[0]
    cats = cat_goal_ref.shape[0]
    shape = taken_ref.shape
    slot = iota(shape, 1)
    base = taken_ref[:, BASE_ROW : BASE_ROW + 1, :].astype(jnp.int32)
    place = ((base + slot == iota(shape, 2)) & (slot < SLOTS)).astype(F32)
    place = place.reshape(devices * SUB, LANES)
    across = place.T[:cats].astype(BF16)
    place = place.astype(BF16)
    place_ref[...] = place
    across_ref[...] = across
    merged = jnp.dot(across, taken_parts(taken_ref), preferred_element_type=F32)
    merged = merged[:, :LANES] + merged[:, LANES:]
    cat, day = fitted(merged, cat_goal_ref[...], line_ref[2:3], jnp.ones((1, LANES), F32))
    day_ref[...] = day
    answer(place, cat, day, out_ref)


def owner_kernel(taken_ref, cat_goal_ref, line_ref, day_ref, place_ref, across_ref, out_ref, day_out_ref):
    merged = jnp.dot(across_ref[...], taken_parts(taken_ref), preferred_element_type=F32)
    merged = merged[:, :LANES] + merged[:, LANES:]
    cat, day = fitted(merged, cat_goal_ref[...], line_ref[2:3], day_ref[...])
    day_out_ref[...] = day
    answer(place_ref[...], cat, day, out_ref)


def owner_last_kernel(taken_ref, cat_goal_ref, line_ref, day_ref, across_ref, out_ref):
    merged = jnp.dot(across_ref[...], taken_parts(taken_ref), preferred_element_type=F32)
    merged = merged[:, :LANES] + merged[:, LANES:]
    cat, day = fitted(merged, cat_goal_ref[...], line_ref[2:3], day_ref[...])
    group = iota((SUB, LANES), 1) // (LANES // SUB)
    tile = cat[:SUB]
    for d in range(1, SUB):
        tile = jnp.where(group == d, cat[d * SUB : (d + 1) * SUB], tile)
    both = jnp.concatenate([tile, jnp.broadcast_to(day, (SUB, LANES))], axis=0)
    out_ref[...] = jnp.broadcast_to(both[None], out_ref.shape)


def closing_kernel(group_ref, factor_ref, back_ref, x_ref, cat_ref, day_ref, out_ref, scale_ref):
    block = x_ref.shape[0]
    stores = x_ref.shape[2]
    first = group_ref[0]
    step = pl.program_id(0)

    @pl.when(step == 0)
    def _():
        row = iota((SUB, LANES), 0)
        for t in range(stores // LANES):
            here = slice(t * LANES, (t + 1) * LANES)
            tiles = swap_blocks([back_ref[t * SUB + j, :SUB] for j in range(SUB)])
            cat_ref[:, here] = jnp.concatenate(tiles, axis=0)
            tiles = swap_blocks([back_ref[t * SUB + j, SUB:] for j in range(SUB)])
            day = tiles[0]
            for d in range(1, SUB):
                day = jnp.where(row == d, tiles[d], day)
            day_ref[:, here] = day
        last = cat_ref.shape[0] - 1
        for s in range(SLOTS):
            at = jnp.minimum(first + s, last)
            scale_ref[s] = cat_ref[pl.ds(at, 1), :] * day_ref[...]

    for i in range(block):
        at = step * block + i
        value = x_ref[i].astype(F32) * factor_ref[0, at] * scale_ref[group_ref[at] - first]
        out_ref[i] = value.astype(BF16)


def vmem(count):
    return [pl.BlockSpec(memory_space=pltpu.VMEM)] * count


def held(x):
    return pltpu.with_memory_space_constraint(x, pltpu.VMEM)


def far(x):
    return pltpu.with_memory_space_constraint(x, pltpu.HBM)


LIMIT = pltpu.CompilerParams(vmem_limit_bytes=8 * 1024 * 1024)


def call(kernel, out_shape, *args, **options):
    return pl.pallas_call(
        kernel,
        out_shape=out_shape,
        in_specs=vmem(len(args)),
        out_specs=tuple(vmem(len(out_shape))),
        compiler_params=LIMIT,
        **options,
    )(*map(held, args))


def shards(predicted_units, product_group, product_goal, group_outlet_goal, outlet_date_goal):
    items, days, stores = predicted_units.shape
    cats = group_outlet_goal.shape[0]
    owners = lax.axis_size("item")
    beside = lax.axis_size("store")

    message = pltpu.VMEM((owners, SUB, LANES), F32)
    margin = pltpu.VMEM((beside, 1, LANES), F32)
    line = pltpu.VMEM((1, LANES), F32)
    tile = pltpu.VMEM((SUB, LANES), jnp.int32)
    per_cat = pltpu.VMEM((cats, LANES), F32)

    flat, part, tid, lines, cat_goal = pl.pallas_call(
        first_kernel,
        out_shape=(
            pltpu.VMEM((items * days, stores), BF16),
            margin,
            tile,
            pltpu.VMEM((SUB, LANES), F32),
            per_cat,
        ),
        in_specs=[pl.BlockSpec(memory_space=pltpu.HBM)] * 5,
        out_specs=tuple(vmem(5)),
        scratch_shapes=[
            pltpu.VMEM(predicted_units.shape, BF16),
            pltpu.VMEM((1, items), jnp.int32),
            pltpu.VMEM((1, items), F32),
            pltpu.VMEM((cats, stores), F32),
            pltpu.VMEM((days, stores), F32),
            pltpu.SemaphoreType.DMA((4,)),
            pltpu.SemaphoreType.DMA((4,)),
        ],
        compiler_params=LIMIT,
        name="first",
    )(
        *map(
            far,
            (
                predicted_units,
                product_group.reshape(1, items),
                product_goal.reshape(1, items),
                group_outlet_goal,
                outlet_date_goal,
            ),
        )
    )
    for n in range(ROUNDS):
        total = lax.all_to_all(part, "store", 0, 0, tiled=True)
        shapes = (message,) if n < ROUNDS - 1 else (message, jax.ShapeDtypeStruct((1, LANES), F32))
        pooled, *factor = call(pool_kernel, shapes, total, lines, flat, tid, name="pool")
        taken = lax.all_to_all(pooled, "item", 0, 0, tiled=True)
        if n == ROUNDS - 1:
            break
        if n == 0:
            shapes = (message, line, pltpu.VMEM((owners * SUB, LANES), BF16), pltpu.VMEM((cats, owners * SUB), BF16))
            back, day, place, across = call(owner_first_kernel, shapes, taken, cat_goal, lines, name="owner_first")
        else:
            back, day = call(owner_kernel, (message, line), taken, cat_goal, lines, day, place, across, name="owner")
        back = lax.all_to_all(back, "item", 0, 0, tiled=True)
        (part,) = call(margin_kernel, (margin,), back, flat, tid, name="margin")

    (back,) = call(
        owner_last_kernel,
        (pltpu.VMEM((owners, 2 * SUB, LANES), F32),),
        taken, cat_goal, lines, day, across,
        name="owner_last",
    )
    back = lax.all_to_all(back, "item", 0, 0, tiled=True)
    block = 32
    smem = pl.BlockSpec(memory_space=pltpu.SMEM)
    wide = pl.BlockSpec((block, days, stores), lambda i: (i, 0, 0))
    group_outlet_factor, outlet_date_factor, adjusted_tensor = pl.pallas_call(
        closing_kernel,
        grid=(items // block,),
        out_shape=(
            jax.ShapeDtypeStruct((cats, stores), F32),
            jax.ShapeDtypeStruct((days, stores), F32),
            jax.ShapeDtypeStruct((items, days, stores), BF16),
        ),
        in_specs=[smem, smem, pl.BlockSpec((owners, 2 * SUB, LANES), lambda i: (0, 0, 0)), wide],
        out_specs=(
            pl.BlockSpec((cats, stores), lambda i: (0, 0)),
            pl.BlockSpec((days, stores), lambda i: (0, 0)),
            wide,
        ),
        scratch_shapes=[pltpu.VMEM((SUB, days, stores), F32)],
        compiler_params=LIMIT,
        name="closing",
    )(product_group, factor[0], back, predicted_units)
    return (factor[0].reshape(items), group_outlet_factor, outlet_date_factor, adjusted_tensor)


def solution(mesh):
    in_specs = (P("item", None, "store"), P("item"), P("item"), P(None, "store"), P(None, "store"))
    out_specs = (P("item"), P(None, "store"), P(None, "store"), P("item", None, "store"))
    return jax.shard_map(shards, mesh=mesh, in_specs=in_specs, out_specs=out_specs, check_vma=False)
```

time: 171 us -> 169 us (0.988)
  blocking collectives: 106 us -> 151 us
  waiting for transfers between devices: 21 us -> 0 us
  starting transfers between devices: 20.1 us -> 0 us
  local copies, waits for them, and re-layouts: 4.86 us -> 0.67 us
    all_to_all x3 -> x4, blocking collectives: 41.3 us -> 62.6 us  [shards(): taken = lax.all_to_all(pooled, 'item', 0, 0, tiled=True)]
    all_to_all x3 -> x0, waiting for transfers between devices: 21 us -> none  [the longest x1 9.86 us: shards(): back = lax.all_to_all(back, 'item', 0, 0, tiled=True)]
    all_to_all x3 -> x0, starting transfers between devices: 20.1 us -> none  [the longest x1 10.8 us: shards(): taken = lax.all_to_all(pooled, 'item', 0, 0, tiled=True)]
    all_to_all x3 -> x4, blocking collectives: 41.9 us -> 56.7 us  [shards(): back = lax.all_to_all(back, 'item', 0, 0, tiled=True)]
    all_to_all x3 -> x4, blocking collectives: 22.9 us -> 31.5 us  [shards(): total = lax.all_to_all(part, 'store', 0, 0, tiled=True)]
    unnamed x12 -> x6, local copies, waits for them, and re-layouts: 2.54 us -> 0.67 us
  transfers between devices with their start and end apart: 3 -> 0, of which waited for: 3 -> 0; matrix products, arithmetic and copies ran while one was open for 2% -> 0% of each run, Pallas kernels for 0% -> 0%
where the time goes in v3:
time: 169 us; the launch traced here: 168 us
  blocking collectives  151 us (89%)
  Pallas kernels  15.4 us (9%)
    all_to_all x4, blocking collectives, shards(): taken = lax.all_to_all(pooled, 'item', 0, 0, tiled=True)  62.6 us
    all_to_all x4, blocking collectives, shards(): back = lax.all_to_all(back, 'item', 0, 0, tiled=True)  56.7 us
    all_to_all x4, blocking collectives, shards(): total = lax.all_to_all(part, 'store', 0, 0, tiled=True)  31.5 us
    pallas_call x11, Pallas kernels, call(): pl.pallas_call(kernel, out_shape=out_shape, in_specs=vmem(len(args)), out...  10.3 us

profile of v3, /device:TPU:8, one launch (start us, length us, event | category | flops | bytes accessed | tf_op | source)
XLA Modules:
  0.0 167.6 jit_solution(3208976065171553158)
XLA Ops:
  0.6 2.5 %first.1 = (bf16[1024,512]{1,0:T(8,128)(2,1)S(1)}, f32[8,1,128]{2,1,0:T(1,128)S(1)}, s32[8,128]{1,0:T(8,128)S(1)}, f32[8,128]{1,0:T(8,128)S(1)}, f32[64,128]{1,0:T(8,128)S(1)}) custom-call(bf16[128,8,512]{2,1,0:T(8,128)(2,1)} %x_ref.1, s32[1,128]{1,0:T(1,128)} %bitcast.3, f32[1,128]{1,0:T(1,128)} %bitcast.5, f32[64,512]{1,0:T(8,128)} %cat_all_hbm.1, ...), custom_call_target="tpu_custom_call" | custom-call | tf_op jit(solution)/shard_map/first/pallas_call | solution.py:306
  3.1 8.5 %all_to_all.60.margin_ref = f32[8,1,128]{2,1,0:T(1,128)S(1)} all-to-all(f32[8,1,128]{2,1,0:T(1,128)S(1)} %get-tuple-element.22), channel_id=1, replica_groups=mesh['item'=32,'store'=8] {'store'}, dimensions={0} | all-to-all | bytes 8192 | tf_op jit(solution)/shard_map/all_to_all | solution.py:341
  11.7 0.8 pool.4
  12.4 21.4 %all_to_all.61.taken_ref = f32[32,8,128]{2,1,0:T(8,128)S(1)} all-to-all(f32[32,8,128]{2,1,0:T(8,128)S(1)} %pool.4), channel_id=1, replica_groups=mesh['item'=32,'store'=8] {'item'}, dimensions={0} | all-to-all | bytes 262144 | tf_op jit(solution)/shard_map/all_to_all | solution.py:344
  33.8 1.1 owner_first.1
  35.0 14.0 %all_to_all.62.back_ref = f32[32,8,128]{2,1,0:T(8,128)S(1)} all-to-all(f32[32,8,128]{2,1,0:T(8,128)S(1)} %get-tuple-element.27), channel_id=1, replica_groups=mesh['item'=32,'store'=8] {'item'}, dimensions={0} | all-to-all | bytes 262144 | tf_op jit(solution)/shard_map/all_to_all | solution.py:352
  48.9 0.9 margin.3
  49.8 7.7 %all_to_all.63.margin_ref = f32[8,1,128]{2,1,0:T(1,128)S(1)} all-to-all(f32[8,1,128]{2,1,0:T(1,128)S(1)} %margin.3), channel_id=1, replica_groups=mesh['item'=32,'store'=8] {'store'}, dimensions={0} | all-to-all | bytes 8192 | tf_op jit(solution)/shard_map/all_to_all | solution.py:341
  57.4 0.8 pool.5
  58.2 13.7 %all_to_all.64.taken_ref = f32[32,8,128]{2,1,0:T(8,128)S(1)} all-to-all(f32[32,8,128]{2,1,0:T(8,128)S(1)} %pool.5), channel_id=1, replica_groups=mesh['item'=32,'store'=8] {'item'}, dimensions={0} | all-to-all | bytes 262144 | tf_op jit(solution)/shard_map/all_to_all | solution.py:344
  72.0 1.1 owner.2
  73.0 13.9 %all_to_all.65.back_ref = f32[32,8,128]{2,1,0:T(8,128)S(1)} all-to-all(f32[32,8,128]{2,1,0:T(8,128)S(1)} %get-tuple-element.31), channel_id=1, replica_groups=mesh['item'=32,'store'=8] {'item'}, dimensions={0} | all-to-all | bytes 262144 | tf_op jit(solution)/shard_map/all_to_all | solution.py:352
  87.0 0.9 margin.4
  87.9 7.6 %all_to_all.66.margin_ref = f32[8,1,128]{2,1,0:T(1,128)S(1)} all-to-all(f32[8,1,128]{2,1,0:T(1,128)S(1)} %margin.4), channel_id=1, replica_groups=mesh['item'=32,'store'=8] {'store'}, dimensions={0} | all-to-all | bytes 8192 | tf_op jit(solution)/shard_map/all_to_all | solution.py:341
  95.5 0.8 pool.6
  96.3 13.8 %all_to_all.67.taken_ref = f32[32,8,128]{2,1,0:T(8,128)S(1)} all-to-all(f32[32,8,128]{2,1,0:T(8,128)S(1)} %pool.6), channel_id=1, replica_groups=mesh['item'=32,'store'=8] {'item'}, dimensions={0} | all-to-all | bytes 262144 | tf_op jit(solution)/shard_map/all_to_all | solution.py:344
  110.0 1.1 owner.3
  111.1 14.0 %all_to_all.68.back_ref = f32[32,8,128]{2,1,0:T(8,128)S(1)} all-to-all(f32[32,8,128]{2,1,0:T(8,128)S(1)} %get-tuple-element.33), channel_id=1, replica_groups=mesh['item'=32,'store'=8] {'item'}, dimensions={0} | all-to-all | bytes 262144 | tf_op jit(solution)/shard_map/all_to_all | solution.py:352
  125.0 0.9 margin.5
  125.9 7.6 %all_to_all.69.margin_ref = f32[8,1,128]{2,1,0:T(1,128)S(1)} all-to-all(f32[8,1,128]{2,1,0:T(1,128)S(1)} %margin.5), channel_id=1, replica_groups=mesh['item'=32,'store'=8] {'store'}, dimensions={0} | all-to-all | bytes 8192 | tf_op jit(solution)/shard_map/all_to_all | solution.py:341
  133.5 0.0 copy-start
  133.5 1.3 pool.7
  134.8 13.7 %all_to_all.70.taken_ref = f32[32,8,128]{2,1,0:T(8,128)S(1)} all-to-all(f32[32,8,128]{2,1,0:T(8,128)S(1)} %get-tuple-element.35), channel_id=1, replica_groups=mesh['item'=32,'store'=8] {'item'}, dimensions={0} | all-to-all | bytes 262144 | tf_op jit(solution)/shard_map/all_to_all | solution.py:344
  148.6 0.9 owner_last.1
  149.4 14.9 %all_to_all.71.back_ref = f32[32,16,128]{2,1,0:T(8,128)S(1)} all-to-all(f32[32,16,128]{2,1,0:T(8,128)S(1)} %owner_last.1), channel_id=1, replica_groups=mesh['item'=32,'store'=8] {'item'}, dimensions={0} | all-to-all | bytes 524288 | tf_op jit(solution)/shard_map/all_to_all | solution.py:361
  164.3 0.0 copy-start.1
  164.3 0.0 copy-start.2
  164.3 0.0 copy-done
  164.3 0.6 copy-done.1
  164.9 0.0 copy-done.2
  165.0 2.6 %closing.1 = (f32[64,512]{1,0:T(8,128)}, f32[8,512]{1,0:T(8,128)}, bf16[128,8,512]{2,1,0:T(8,128)(2,1)}) custom-call(s32[128]{0:T(128)S(1)} %copy-done.1, f32[1,128]{1,0:T(1,128)S(1)} %copy-done.2, f32[32,16,128]{2,1,0:T(8,128)S(1)} %all_to_all.71.back_ref, bf16[128,8,512]{2,1,0:T(8,128)(2,1)S(1)} %copy-done), custom_call_target="tpu_custom_call" | custom-call | tf_op jit(solution)/shard_map/closing/pallas_call | solution.py:365
Async XLA Ops:
  133.5 30.8 %copy-start = (bf16[128,8,512]{2,1,0:T(8,128)(2,1)S(1)}, bf16[128,8,512]{2,1,0:T(8,128)(2,1)}, u32[]{:S(2)}) copy-start(bf16[128,8,512]{2,1,0:T(8,128)(2,1)} %x_ref.1) | copy-start | bytes 3145732
  164.3 0.7 copy-start.1
  164.3 0.7 copy-start.2

commit v4 on v3

--- a/solution.py
+++ b/solution.py
@@ -45,6 +45,20 @@
         tiles = fresh
         bit *= 2
     return tiles
+
+
+def swap_within(x):
+    width = LANES // SUB
+    row, group = iota(x.shape, 0), iota(x.shape, 1) // width
+    for bit in (1, 2, 4):
+        low, same = (row & bit) == 0, (row & bit) == (group & bit)
+        above = pltpu.roll(pltpu.roll(x, SUB - bit, 0), bit * width, 1)
+        if 2 * bit == SUB:
+            x = jnp.where(same, x, above)
+        else:
+            below = pltpu.roll(pltpu.roll(x, bit, 0), LANES - bit * width, 1)
+            x = jnp.where(same, x, jnp.where(low, above, below))
+    return x
 
 
 def eight_sum(x):
@@ -127,11 +141,16 @@
 
 
 def margin_kernel(back_ref, flat_ref, tid_ref, out_ref):
-    stores = flat_ref.shape[1]
-    columns = []
+    days, stores = SUB, flat_ref.shape[1]
+    pairs = []
     for t in range(stores // LANES):
-        columns.append(jnp.concatenate(swap_blocks([back_ref[t * SUB + j] for j in range(SUB)]), axis=0))
-    weights = jnp.concatenate(columns, axis=1)
+        at = t * 2 * SUB
+        day = swap_within(back_ref[pl.ds(at, SUB, stride=2), :])
+        cat = swap_within(back_ref[pl.ds(at + 1, SUB, stride=2), :])
+        pairs.append((day, cat))
+    weights = jnp.concatenate(
+        [jnp.concatenate([cat * day[d : d + 1] for day, cat in pairs], axis=1) for d in range(days)], axis=0
+    )
     parts = jnp.concatenate(two_parts(weights), axis=0)
     sums = lax.dot_general(parts, flat_ref[...], (((1,), (1,)), ((), ())), preferred_element_type=F32)
     half = weights.shape[0]
@@ -165,10 +184,15 @@
     sums = sums[:half] + sums[half:]
     row = iota((SUB, LANES), 0)
     base = jnp.broadcast_to(line_ref[1:2], (SUB, LANES))
+    count = stores // (LANES // SUB)
+    each = out_ref.shape[0] // count
     for t in range(stores // LANES):
         tiles = [sums[d * SUB : (d + 1) * SUB, t * LANES : (t + 1) * LANES] for d in range(SUB)]
         for j, tile in enumerate(swap_blocks(tiles)):
-            out_ref[t * SUB + j] = jnp.where(row == BASE_ROW, base, tile)
+            if each > SLOTS:
+                tile = jnp.where(row == BASE_ROW, base, tile)
+            at = (t * SUB + j) * each
+            out_ref[at : at + each] = tile[:each]
 
 
 def fitted(merged, cat_goal, day_goal, day):
@@ -184,85 +208,112 @@
     return cat, day
 
 
-def taken_parts(taken_ref):
-    devices = taken_ref.shape[0]
-    return jnp.concatenate(two_parts(taken_ref[...].reshape(devices * SUB, LANES)), axis=1)
-
-
-def answer(place, cat, day, out_ref):
+def summed(across, taken):
+    merged = jnp.dot(across, jnp.concatenate(two_parts(taken), axis=1), preferred_element_type=F32)
+    return merged[:, :LANES] + merged[:, LANES:]
+
+
+def answer(choice, cat, day, out_ref):
     cats = cat.shape[0]
-    product = jnp.concatenate([cat * day, jnp.zeros((LANES - cats, LANES), F32)], axis=0)
-    product = jnp.concatenate(two_parts(product), axis=1)
-    sent = jnp.dot(place, product, preferred_element_type=F32)
-    out_ref[...] = (sent[:, :LANES] + sent[:, LANES:]).reshape(out_ref.shape)
-
-
-def owner_first_kernel(taken_ref, cat_goal_ref, line_ref, out_ref, day_ref, place_ref, across_ref):
-    devices = taken_ref.shape[0]
+    group = iota(cat.shape, 1) // (LANES // SUB)
+    blocks = [jnp.where(group == s, cat, 0.0) for s in range(choice.shape[1] // cats)]
+    parts = jnp.concatenate(two_parts(jnp.concatenate(blocks, axis=0)), axis=1)
+    rows = jnp.dot(choice, parts, preferred_element_type=F32)
+    devices = choice.shape[0]
+    out_ref[pl.ds(0, devices, stride=2), :] = jnp.broadcast_to(day, (devices, LANES))
+    out_ref[pl.ds(1, devices, stride=2), :] = rows[:, :LANES] + rows[:, LANES:]
+
+
+def owner_first_kernel(taken_ref, cat_goal_ref, line_ref, out_ref, day_ref, choice_ref, across_ref):
     cats = cat_goal_ref.shape[0]
-    shape = taken_ref.shape
-    slot = iota(shape, 1)
-    base = taken_ref[:, BASE_ROW : BASE_ROW + 1, :].astype(jnp.int32)
-    place = ((base + slot == iota(shape, 2)) & (slot < SLOTS)).astype(F32)
-    place = place.reshape(devices * SUB, LANES)
-    across = place.T[:cats].astype(BF16)
-    place = place.astype(BF16)
-    place_ref[...] = place
-    across_ref[...] = across
-    merged = jnp.dot(across, taken_parts(taken_ref), preferred_element_type=F32)
-    merged = merged[:, :LANES] + merged[:, LANES:]
+    devices = choice_ref.shape[0]
+    base = taken_ref[pl.ds(BASE_ROW, devices, stride=SUB), :]
+
+    def placed(each, slots):
+        rows = devices * each
+        at = iota((rows, devices), 0) - iota((rows, devices), 1) * each
+        spread = jnp.dot(
+            ((at >= 0) & (at < each)).astype(F32).astype(BF16), base.astype(BF16), preferred_element_type=F32
+        ).astype(jnp.int32)
+        slot = jnp.sum(jnp.where((at >= 0) & (at < each), at, 0), axis=1, keepdims=True)
+        hit = (spread + slot == iota((rows, LANES), 1)) & (slot < slots)
+        return hit.astype(F32).T[:cats].astype(BF16)
+
+    across_ref[...] = placed(SLOTS, SLOTS)
+    per = LANES // cats
+    lane = iota((devices, LANES), 1)
+    number = base.astype(jnp.int32)
+    for n in range(choice_ref.shape[1] // LANES):
+        slot = n * per + lane // cats
+        hit = (number + slot == lane % cats) & (slot < SLOTS)
+        choice_ref[:, n * LANES : (n + 1) * LANES] = hit.astype(F32).astype(BF16)
+    merged = summed(placed(SUB, SLOTS), taken_ref[...])
     cat, day = fitted(merged, cat_goal_ref[...], line_ref[2:3], jnp.ones((1, LANES), F32))
     day_ref[...] = day
-    answer(place, cat, day, out_ref)
-
-
-def owner_kernel(taken_ref, cat_goal_ref, line_ref, day_ref, place_ref, across_ref, out_ref, day_out_ref):
-    merged = jnp.dot(across_ref[...], taken_parts(taken_ref), preferred_element_type=F32)
-    merged = merged[:, :LANES] + merged[:, LANES:]
+    answer(choice_ref[...], cat, day, out_ref)
+
+
+def owner_kernel(taken_ref, cat_goal_ref, line_ref, day_ref, choice_ref, across_ref, out_ref, day_out_ref):
+    merged = summed(across_ref[...], taken_ref[...])
     cat, day = fitted(merged, cat_goal_ref[...], line_ref[2:3], day_ref[...])
     day_out_ref[...] = day
-    answer(place_ref[...], cat, day, out_ref)
+    answer(choice_ref[...], cat, day, out_ref)
 
 
 def owner_last_kernel(taken_ref, cat_goal_ref, line_ref, day_ref, across_ref, out_ref):
-    merged = jnp.dot(across_ref[...], taken_parts(taken_ref), preferred_element_type=F32)
-    merged = merged[:, :LANES] + merged[:, LANES:]
+    merged = summed(across_ref[...], taken_ref[...])
     cat, day = fitted(merged, cat_goal_ref[...], line_ref[2:3], day_ref[...])
     group = iota((SUB, LANES), 1) // (LANES // SUB)
     tile = cat[:SUB]
     for d in range(1, SUB):
         tile = jnp.where(group == d, cat[d * SUB : (d + 1) * SUB], tile)
-    both = jnp.concatenate([tile, jnp.broadcast_to(day, (SUB, LANES))], axis=0)
-    out_ref[...] = jnp.broadcast_to(both[None], out_ref.shape)
-
-
-def closing_kernel(group_ref, factor_ref, back_ref, x_ref, cat_ref, day_ref, out_ref, scale_ref):
-    block = x_ref.shape[0]
-    stores = x_ref.shape[2]
-    first = group_ref[0]
-    step = pl.program_id(0)
-
-    @pl.when(step == 0)
-    def _():
-        row = iota((SUB, LANES), 0)
-        for t in range(stores // LANES):
-            here = slice(t * LANES, (t + 1) * LANES)
-            tiles = swap_blocks([back_ref[t * SUB + j, :SUB] for j in range(SUB)])
-            cat_ref[:, here] = jnp.concatenate(tiles, axis=0)
-            tiles = swap_blocks([back_ref[t * SUB + j, SUB:] for j in range(SUB)])
-            day = tiles[0]
-            for d in range(1, SUB):
-                day = jnp.where(row == d, tiles[d], day)
-            day_ref[:, here] = day
-        last = cat_ref.shape[0] - 1
-        for s in range(SLOTS):
-            at = jnp.minimum(first + s, last)
-            scale_ref[s] = cat_ref[pl.ds(at, 1), :] * day_ref[...]
-
-    for i in range(block):
-        at = step * block + i
-        value = x_ref[i].astype(F32) * factor_ref[0, at] * scale_ref[group_ref[at] - first]
-        out_ref[i] = value.astype(BF16)
+    both = jnp.concatenate([tile, day], axis=0)
+    each = both.shape[0]
+    for j in range(out_ref.shape[0] // each):
+        out_ref[j * each : (j + 1) * each] = both
+
+
+def closing_kernel(
+    group_hbm, factor_hbm, back_ref, x_ref, cat_hbm, day_hbm, out_hbm,
+    group_ref, factor_ref, cat_ref, day_ref, scale_ref, buf_ref, sems, out_sems,
+):
+    items, _, stores = x_ref.shape
+    loads = [
+        pltpu.make_async_copy(group_hbm, group_ref, sems.at[0]),
+        pltpu.make_async_copy(factor_hbm, factor_ref, sems.at[1]),
+    ]
+    for copy in loads:
+        copy.start()
+    each = SUB + 1
+    for t in range(stores // LANES):
+        here = slice(t * LANES, (t + 1) * LANES)
+        tiles = swap_blocks([back_ref[(t * SUB + j) * each : (t * SUB + j) * each + SUB] for j in range(SUB)])
+        cat_ref[:, here] = jnp.concatenate(tiles, axis=0)
+        day_ref[:, here] = swap_within(back_ref[pl.ds(t * SUB * each + SUB, SUB, stride=each), :])
+    stores_out = [
+        pltpu.make_async_copy(cat_ref, cat_hbm, sems.at[2]),
+        pltpu.make_async_copy(day_ref, day_hbm, sems.at[3]),
+    ]
+    for copy in stores_out:
+        copy.start()
+    for copy in loads:
+        copy.wait()
+    first = group_ref[0, 0]
+    last = cat_ref.shape[0] - 1
+    for s in range(SLOTS):
+        scale_ref[s] = cat_ref[pl.ds(jnp.minimum(first + s, last), 1), :] * day_ref[...]
+    chunks = out_sems.shape[0]
+    block = items // chunks
+    for n in range(chunks):
+        for i in range(n * block, (n + 1) * block):
+            value = x_ref[i].astype(F32) * factor_ref[0, i] * scale_ref[group_ref[0, i] - first]
+            buf_ref[i] = value.astype(BF16)
+        rows = pl.ds(n * block, block)
+        copy = pltpu.make_async_copy(buf_ref.at[rows], out_hbm.at[rows], out_sems.at[n])
+        copy.start()
+        stores_out.append(copy)
+    for copy in stores_out:
+        copy.wait()
 
 
 def vmem(count):
@@ -297,7 +348,13 @@
     owners = lax.axis_size("item")
     beside = lax.axis_size("store")
 
-    message = pltpu.VMEM((owners, SUB, LANES), F32)
+    def message(each):
+        return pltpu.VMEM((owners * each, LANES), F32)
+
+    def exchanged(x):
+        sent = x.reshape(owners, 1, x.size // owners)
+        return lax.all_to_all(sent, "item", 0, 0, tiled=True).reshape(x.shape)
+
     margin = pltpu.VMEM((beside, 1, LANES), F32)
     line = pltpu.VMEM((1, LANES), F32)
     tile = pltpu.VMEM((SUB, LANES), jnp.int32)
@@ -339,47 +396,52 @@
     )
     for n in range(ROUNDS):
         total = lax.all_to_all(part, "store", 0, 0, tiled=True)
-        shapes = (message,) if n < ROUNDS - 1 else (message, jax.ShapeDtypeStruct((1, LANES), F32))
+        shapes = (message(SLOTS if n else SUB),)
+        if n == ROUNDS - 1:
+            shapes += (jax.ShapeDtypeStruct((1, LANES), F32),)
         pooled, *factor = call(pool_kernel, shapes, total, lines, flat, tid, name="pool")
-        taken = lax.all_to_all(pooled, "item", 0, 0, tiled=True)
+        taken = exchanged(pooled)
         if n == ROUNDS - 1:
             break
         if n == 0:
-            shapes = (message, line, pltpu.VMEM((owners * SUB, LANES), BF16), pltpu.VMEM((cats, owners * SUB), BF16))
-            back, day, place, across = call(owner_first_kernel, shapes, taken, cat_goal, lines, name="owner_first")
+            blocks = -(-SLOTS * cats // LANES)
+            shapes = (
+                message(2),
+                line,
+                pltpu.VMEM((owners, blocks * LANES), BF16),
+                pltpu.VMEM((cats, owners * SLOTS), BF16),
+            )
+            back, day, choice, across = call(owner_first_kernel, shapes, taken, cat_goal, lines, name="owner_first")
         else:
-            back, day = call(owner_kernel, (message, line), taken, cat_goal, lines, day, place, across, name="owner")
-        back = lax.all_to_all(back, "item", 0, 0, tiled=True)
-        (part,) = call(margin_kernel, (margin,), back, flat, tid, name="margin")
+            back, day = call(owner_kernel, (message(2), line), taken, cat_goal, lines, day, choice, across, name="owner")
+        (part,) = call(margin_kernel, (margin,), exchanged(back), flat, tid, name="margin")
 
     (back,) = call(
-        owner_last_kernel,
-        (pltpu.VMEM((owners, 2 * SUB, LANES), F32),),
-        taken, cat_goal, lines, day, across,
-        name="owner_last",
+        owner_last_kernel, (message(SUB + 1),), taken, cat_goal, lines, day, across, name="owner_last"
     )
-    back = lax.all_to_all(back, "item", 0, 0, tiled=True)
-    block = 32
-    smem = pl.BlockSpec(memory_space=pltpu.SMEM)
-    wide = pl.BlockSpec((block, days, stores), lambda i: (i, 0, 0))
+    far_spec = pl.BlockSpec(memory_space=pltpu.HBM)
     group_outlet_factor, outlet_date_factor, adjusted_tensor = pl.pallas_call(
         closing_kernel,
-        grid=(items // block,),
         out_shape=(
             jax.ShapeDtypeStruct((cats, stores), F32),
             jax.ShapeDtypeStruct((days, stores), F32),
             jax.ShapeDtypeStruct((items, days, stores), BF16),
         ),
-        in_specs=[smem, smem, pl.BlockSpec((owners, 2 * SUB, LANES), lambda i: (0, 0, 0)), wide],
-        out_specs=(
-            pl.BlockSpec((cats, stores), lambda i: (0, 0)),
-            pl.BlockSpec((days, stores), lambda i: (0, 0)),
-            wide,
-        ),
-        scratch_shapes=[pltpu.VMEM((SUB, days, stores), F32)],
+        in_specs=[far_spec] * 2 + vmem(2),
+        out_specs=(far_spec,) * 3,
+        scratch_shapes=[
+            pltpu.SMEM((1, items), jnp.int32),
+            pltpu.SMEM((1, items), F32),
+            pltpu.VMEM((cats, stores), F32),
+            pltpu.VMEM((days, stores), F32),
+            pltpu.VMEM((SUB, days, stores), F32),
+            pltpu.VMEM((items, days, stores), BF16),
+            pltpu.SemaphoreType.DMA((4,)),
+            pltpu.SemaphoreType.DMA((4,)),
+        ],
         compiler_params=LIMIT,
         name="closing",
-    )(product_group, factor[0], back, predicted_units)
+    )(far(product_group.reshape(1, items)), far(factor[0]), held(exchanged(back)), held(predicted_units))
     return (factor[0].reshape(items), group_outlet_factor, outlet_date_factor, adjusted_tensor)
 
 

time: 169 us -> 162 us (0.959)
  blocking collectives: 151 us -> 146 us
    all_to_all x8, blocking collectives: 119 us -> 114 us  [exchanged(): return lax.all_to_all(sent, 'item', 0, 0, tiled=True).reshape(x.shape)]
where the time goes in v4:
time: 162 us; the launch traced here: 161 us
  blocking collectives  146 us (90%)
  Pallas kernels  14.3 us (9%)
    all_to_all x8, blocking collectives, exchanged(): return lax.all_to_all(sent, 'item', 0, 0, tiled=True).reshape(x.shape)  114 us
    all_to_all x4, blocking collectives, shards(): total = lax.all_to_all(part, 'store', 0, 0, tiled=True)  31.6 us
    pallas_call x11, Pallas kernels, call(): pl.pallas_call(kernel, out_shape=out_shape, in_specs=vmem(len(args)), out...  10.1 us

profile of v4, /device:TPU:8, one launch (start us, length us, event | category | flops | bytes accessed | tf_op | source)
XLA Modules:
  0.0 160.8 jit_solution(10991485887108614539)
XLA Ops:
  0.6 2.5 %first.1 = (bf16[1024,512]{1,0:T(8,128)(2,1)S(1)}, f32[8,1,128]{2,1,0:T(1,128)S(1)}, s32[8,128]{1,0:T(8,128)S(1)}, f32[8,128]{1,0:T(8,128)S(1)}, f32[64,128]{1,0:T(8,128)S(1)}) custom-call(bf16[128,8,512]{2,1,0:T(8,128)(2,1)} %x_ref.1, s32[1,128]{1,0:T(1,128)} %bitcast.35, f32[1,128]{1,0:T(1,128)} %bitcast.37, f32[64,512]{1,0:T(8,128)} %cat_all_hbm.1, ...), custom_call_target="tpu_custom_call" | custom-call | tf_op jit(solution)/shard_map/first/pallas_call | solution.py:363
  3.1 8.5 %all_to_all.60.margin_ref = f32[8,1,128]{2,1,0:T(1,128)S(1)} all-to-all(f32[8,1,128]{2,1,0:T(1,128)S(1)} %get-tuple-element.22), channel_id=1, replica_groups=mesh['item'=32,'store'=8] {'store'}, dimensions={0} | all-to-all | bytes 8192 | tf_op jit(solution)/shard_map/all_to_all | solution.py:398
  11.7 0.8 pool.4
  12.4 21.4 %all_to_all.61 = f32[32,1,1024]{2,1,0:T(1,128)S(1)} all-to-all(f32[32,1,1024]{2,1,0:T(1,128)S(1)} %bitcast.21), channel_id=1, replica_groups=mesh['item'=32,'store'=8] {'item'}, dimensions={0} | all-to-all | bytes 262144 | tf_op jit(solution)/shard_map/all_to_all | solution.py:356
  33.8 1.2 owner_first.1
  35.1 13.5 %all_to_all.62 = f32[32,1,256]{2,1,0:T(1,128)S(1)} all-to-all(f32[32,1,256]{2,1,0:T(1,128)S(1)} %bitcast.32), channel_id=1, replica_groups=mesh['item'=32,'store'=8] {'item'}, dimensions={0} | all-to-all | bytes 65536 | tf_op jit(solution)/shard_map/all_to_all | solution.py:356
  48.6 0.9 margin.3
  49.4 7.7 %all_to_all.63.margin_ref = f32[8,1,128]{2,1,0:T(1,128)S(1)} all-to-all(f32[8,1,128]{2,1,0:T(1,128)S(1)} %margin.3), channel_id=1, replica_groups=mesh['item'=32,'store'=8] {'store'}, dimensions={0} | all-to-all | bytes 8192 | tf_op jit(solution)/shard_map/all_to_all | solution.py:398
  57.1 0.8 pool.5
  57.8 13.0 %all_to_all.64 = f32[32,1,640]{2,1,0:T(1,128)S(1)} all-to-all(f32[32,1,640]{2,1,0:T(1,128)S(1)} %bitcast.23), channel_id=1, replica_groups=mesh['item'=32,'store'=8] {'item'}, dimensions={0} | all-to-all | bytes 163840 | tf_op jit(solution)/shard_map/all_to_all | solution.py:356
  70.9 1.0 owner.2
  71.9 13.2 %all_to_all.65 = f32[32,1,256]{2,1,0:T(1,128)S(1)} all-to-all(f32[32,1,256]{2,1,0:T(1,128)S(1)} %bitcast.34), channel_id=1, replica_groups=mesh['item'=32,'store'=8] {'item'}, dimensions={0} | all-to-all | bytes 65536 | tf_op jit(solution)/shard_map/all_to_all | solution.py:356
  85.1 0.9 margin.4
  85.9 7.6 %all_to_all.66.margin_ref = f32[8,1,128]{2,1,0:T(1,128)S(1)} all-to-all(f32[8,1,128]{2,1,0:T(1,128)S(1)} %margin.4), channel_id=1, replica_groups=mesh['item'=32,'store'=8] {'store'}, dimensions={0} | all-to-all | bytes 8192 | tf_op jit(solution)/shard_map/all_to_all | solution.py:398
  93.5 0.8 pool.6
  94.3 13.0 %all_to_all.67 = f32[32,1,640]{2,1,0:T(1,128)S(1)} all-to-all(f32[32,1,640]{2,1,0:T(1,128)S(1)} %bitcast.24), channel_id=1, replica_groups=mesh['item'=32,'store'=8] {'item'}, dimensions={0} | all-to-all | bytes 163840 | tf_op jit(solution)/shard_map/all_to_all | solution.py:356
  107.3 1.0 owner.3
  108.3 13.2 %all_to_all.68 = f32[32,1,256]{2,1,0:T(1,128)S(1)} all-to-all(f32[32,1,256]{2,1,0:T(1,128)S(1)} %bitcast.33), channel_id=1, replica_groups=mesh['item'=32,'store'=8] {'item'}, dimensions={0} | all-to-all | bytes 65536 | tf_op jit(solution)/shard_map/all_to_all | solution.py:356
  121.5 0.9 margin.5
  122.4 0.0 copy-start
  122.4 7.7 %all_to_all.69.margin_ref = f32[8,1,128]{2,1,0:T(1,128)S(1)} all-to-all(f32[8,1,128]{2,1,0:T(1,128)S(1)} %margin.5), channel_id=1, replica_groups=mesh['item'=32,'store'=8] {'store'}, dimensions={0} | all-to-all | bytes 8192 | tf_op jit(solution)/shard_map/all_to_all | solution.py:398
  130.1 1.2 pool.7
  131.3 13.0 %all_to_all.70 = f32[32,1,640]{2,1,0:T(1,128)S(1)} all-to-all(f32[32,1,640]{2,1,0:T(1,128)S(1)} %bitcast.31), channel_id=1, replica_groups=mesh['item'=32,'store'=8] {'item'}, dimensions={0} | all-to-all | bytes 163840 | tf_op jit(solution)/shard_map/all_to_all | solution.py:356
  144.4 0.9 owner_last.1
  145.2 13.7 %all_to_all.71 = f32[32,1,1152]{2,1,0:T(1,128)S(1)} all-to-all(f32[32,1,1152]{2,1,0:T(1,128)S(1)} %bitcast.19), channel_id=1, replica_groups=mesh['item'=32,'store'=8] {'item'}, dimensions={0} | all-to-all | bytes 294912 | tf_op jit(solution)/shard_map/all_to_all | solution.py:356
  159.0 0.0 copy-done
  159.0 1.8 %closing.1 = (f32[64,512]{1,0:T(8,128)}, f32[8,512]{1,0:T(8,128)}, bf16[128,8,512]{2,1,0:T(8,128)(2,1)}) custom-call(s32[1,128]{1,0:T(1,128)} %bitcast.36, f32[1,128]{1,0:T(1,128)} %get-tuple-element.34.factor_hbm, f32[288,128]{1,0:T(8,128)S(1)} %bitcast.20, bf16[128,8,512]{2,1,0:T(8,128)(2,1)S(1)} %copy-done), custom_call_target="tpu_custom_call" | custom-call | tf_op jit(solution)/shard_map/closing/pallas_call | solution.py:423
Async XLA Ops:
  122.4 36.6 %copy-start = (bf16[128,8,512]{2,1,0:T(8,128)(2,1)S(1)}, bf16[128,8,512]{2,1,0:T(8,128)(2,1)}, u32[]{:S(2)}) copy-start(bf16[128,8,512]{2,1,0:T(8,128)(2,1)} %x_ref.1) | copy-start | bytes 3145732

commit v5 on v4

--- a/solution.py
+++ b/solution.py
@@ -78,18 +78,13 @@
     return jnp.sum(kept, axis=0, keepdims=True)
 
 
-def expanded(line):
-    line = jnp.broadcast_to(line, (SUB, LANES))
-    return eight_sum(jnp.where((iota((SUB, LANES), 1) & 7) == iota((SUB, LANES), 0), line, 0.0))
-
-
 def picked(x, index):
     return jnp.take_along_axis(x, index, axis=1)
 
 
 def first_kernel(
     x_hbm, group_hbm, goal_hbm, cat_all_hbm, day_all_hbm,
-    flat_ref, out_ref, tid_ref, line_ref, cat_goal_ref,
+    rows_ref, out_ref, slot_ref, line_ref, cat_goal_ref,
     x_buf, group_ref, goal_ref, cat_all_ref, day_all_ref, sems, small_sems,
 ):
     items, days, stores = x_hbm.shape
@@ -112,10 +107,8 @@
     row, lane = iota((SUB, LANES), 0), iota((SUB, LANES), 1)
     group = jnp.broadcast_to(group_ref[...], (SUB, LANES))
     first = picked(group, jnp.zeros_like(lane))
-    slot = picked(group, row * (items // SUB) + lane // days) - first
-    tid_ref[...] = (lane % days) * SUB + slot
-    goal = jnp.broadcast_to(goal_ref[...], (SUB, LANES))
-    line_ref[0:1] = picked(goal, (lane % SUB) * (items // SUB) + lane // SUB)[:1]
+    slot_ref[...] = group - first
+    line_ref[0:1] = goal_ref[...]
     line_ref[1:2] = first[:1].astype(F32)
     width = LANES // days
     at = lax.axis_index("item") * width
@@ -130,69 +123,72 @@
     tiles = []
     for n in range(chunks):
         copies[n].wait()
-        x = x_buf[n * block : (n + 1) * block].astype(F32)
-        flat = x.reshape(block * days, stores).astype(BF16)
-        flat_ref[n * block * days : (n + 1) * block * days] = flat
+        x = x_buf[n * block : (n + 1) * block].astype(F32).reshape(block * days, stores)
+        for t in range(stores // LANES):
+            at = (t * items + n * block) * days
+            rows_ref[at : at + block * days] = x[:, t * LANES : (t + 1) * LANES]
         sums = lax.dot_general(
-            jnp.ones((SUB, stores), BF16), flat, (((1,), (1,)), ((), ())), preferred_element_type=F32
+            jnp.ones((SUB, stores), BF16), x.astype(BF16), (((1,), (1,)), ((), ())), preferred_element_type=F32
         )
         tiles += [sums[:, q * LANES : (q + 1) * LANES] for q in range(block * days // LANES)]
-    out_ref[...] = jnp.broadcast_to(compacted(tiles)[None], out_ref.shape)
-
-
-def margin_kernel(back_ref, flat_ref, tid_ref, out_ref):
-    days, stores = SUB, flat_ref.shape[1]
-    pairs = []
-    for t in range(stores // LANES):
-        at = t * 2 * SUB
-        day = swap_within(back_ref[pl.ds(at, SUB, stride=2), :])
-        cat = swap_within(back_ref[pl.ds(at + 1, SUB, stride=2), :])
-        pairs.append((day, cat))
-    weights = jnp.concatenate(
-        [jnp.concatenate([cat * day[d : d + 1] for day, cat in pairs], axis=1) for d in range(days)], axis=0
-    )
-    parts = jnp.concatenate(two_parts(weights), axis=0)
-    sums = lax.dot_general(parts, flat_ref[...], (((1,), (1,)), ((), ())), preferred_element_type=F32)
-    half = weights.shape[0]
-    sums = sums[:half] + sums[half:]
-    which = iota((half, LANES), 0)
-    rows = []
-    for q in range(SUB):
-        kept = jnp.where(which == tid_ref[q : q + 1, :], sums[:, q * LANES : (q + 1) * LANES], 0.0)
-        rows.append(jnp.broadcast_to(jnp.sum(kept, axis=0, keepdims=True), (SUB, LANES)))
-    line = compacted(rows)
+    line = jnp.broadcast_to(compacted(tiles), (SUB, LANES))
+    half = LANES // SUB
+    line = picked(line, lane % half * SUB + lane // half)[:1]
     out_ref[...] = jnp.broadcast_to(line[None], out_ref.shape)
 
 
-def pool_kernel(margin_ref, line_ref, flat_ref, tid_ref, out_ref, *factor_out):
-    stores = flat_ref.shape[1]
+def spread_kernel(rows_ref, out_ref):
+    tall = 2 * SUB
+    items, columns = out_ref.shape
+
+    def step(n, carry):
+        into = pl.ds(pl.multiple_of(n * tall, tall), tall)
+        for t in range(columns // (SUB * LANES)):
+            at = (t * items + n * tall) * SUB
+            tiles = [rows_ref[pl.ds(at + d, tall, stride=SUB), :] for d in range(SUB)]
+            for j, tile in enumerate(swap_blocks(tiles)):
+                at = (t * SUB + j) * LANES
+                out_ref[into, at : at + LANES] = tile.astype(BF16)
+        return carry
+
+    lax.fori_loop(0, items // tall, step, 0)
+
+
+def margin_kernel(back_ref, wide_ref, slot_ref, out_ref):
+    count = wide_ref.shape[1] // LANES
+    tiles = []
+    for j in range(count):
+        at = min(j * SLOTS, count * SLOTS - SUB)
+        tile = back_ref[at : at + SUB]
+        if at < j * SLOTS:
+            tile = pltpu.roll(tile, SUB - (j * SLOTS - at), 0)
+        tiles.append(tile)
+    parts = jnp.concatenate(two_parts(jnp.concatenate(tiles, axis=1)), axis=0)
+    sums = lax.dot_general(parts, wide_ref[...], (((1,), (1,)), ((), ())), preferred_element_type=F32)
+    sums = sums[:SUB] + sums[SUB:]
+    kept = jnp.where(iota((SUB, LANES), 0) == slot_ref[...], sums, 0.0)
+    line = jnp.sum(kept, axis=0, keepdims=True)
+    out_ref[...] = jnp.broadcast_to(line[None], out_ref.shape)
+
+
+def pool_kernel(margin_ref, line_ref, wide_ref, slot_ref, out_ref, *factor_out):
     total = jnp.sum(margin_ref[...], axis=0)
     factor = line_ref[0:1] / total
     if factor_out:
-        lane = iota((SUB, LANES), 1)
-        index = lane % (LANES // SUB) * SUB + lane // (LANES // SUB)
-        factor_out[0][...] = picked(jnp.broadcast_to(factor, (SUB, LANES)), index)[:1]
-    spread = expanded(factor)
-    half = SUB * SUB
-    which = iota((half, LANES), 0)
-    columns = []
-    for q in range(SUB):
-        columns.append(jnp.where(which == tid_ref[q : q + 1, :], spread[q : q + 1, :], 0.0))
-    weights = jnp.concatenate(columns, axis=1)
+        factor_out[0][...] = factor
+    row = iota((SUB, LANES), 0)
+    weights = jnp.where(row == slot_ref[...], factor, 0.0)
     parts = jnp.concatenate(two_parts(weights), axis=0)
-    sums = jnp.dot(parts, flat_ref[...], preferred_element_type=F32)
-    sums = sums[:half] + sums[half:]
-    row = iota((SUB, LANES), 0)
+    sums = jnp.dot(parts, wide_ref[...], preferred_element_type=F32)
+    sums = sums[:SUB] + sums[SUB:]
+    count = wide_ref.shape[1] // LANES
+    each = out_ref.shape[0] // count
     base = jnp.broadcast_to(line_ref[1:2], (SUB, LANES))
-    count = stores // (LANES // SUB)
-    each = out_ref.shape[0] // count
-    for t in range(stores // LANES):
-        tiles = [sums[d * SUB : (d + 1) * SUB, t * LANES : (t + 1) * LANES] for d in range(SUB)]
-        for j, tile in enumerate(swap_blocks(tiles)):
-            if each > SLOTS:
-                tile = jnp.where(row == BASE_ROW, base, tile)
-            at = (t * SUB + j) * each
-            out_ref[at : at + each] = tile[:each]
+    for j in range(count):
+        tile = sums[:, j * LANES : (j + 1) * LANES]
+        if each > SLOTS:
+            tile = jnp.where(row == BASE_ROW, base, tile)
+        out_ref[j * each : (j + 1) * each] = tile[:each]
 
 
 def fitted(merged, cat_goal, day_goal, day):
@@ -213,51 +209,42 @@
     return merged[:, :LANES] + merged[:, LANES:]
 
 
-def answer(choice, cat, day, out_ref):
+def answer(place, cat, day, out_ref):
     cats = cat.shape[0]
-    group = iota(cat.shape, 1) // (LANES // SUB)
-    blocks = [jnp.where(group == s, cat, 0.0) for s in range(choice.shape[1] // cats)]
-    parts = jnp.concatenate(two_parts(jnp.concatenate(blocks, axis=0)), axis=1)
-    rows = jnp.dot(choice, parts, preferred_element_type=F32)
-    devices = choice.shape[0]
-    out_ref[pl.ds(0, devices, stride=2), :] = jnp.broadcast_to(day, (devices, LANES))
-    out_ref[pl.ds(1, devices, stride=2), :] = rows[:, :LANES] + rows[:, LANES:]
-
-
-def owner_first_kernel(taken_ref, cat_goal_ref, line_ref, out_ref, day_ref, choice_ref, across_ref):
+    product = jnp.concatenate([cat * day, jnp.zeros((LANES - cats, LANES), F32)], axis=0)
+    parts = jnp.concatenate(two_parts(product), axis=1)
+    sent = jnp.dot(place, parts, preferred_element_type=F32)
+    out_ref[...] = sent[:, :LANES] + sent[:, LANES:]
+
+
+def owner_first_kernel(taken_ref, cat_goal_ref, line_ref, out_ref, day_ref, place_ref, across_ref):
     cats = cat_goal_ref.shape[0]
-    devices = choice_ref.shape[0]
+    devices = taken_ref.shape[0] // SUB
     base = taken_ref[pl.ds(BASE_ROW, devices, stride=SUB), :]
 
-    def placed(each, slots):
+    def placed(each):
         rows = devices * each
         at = iota((rows, devices), 0) - iota((rows, devices), 1) * each
-        spread = jnp.dot(
-            ((at >= 0) & (at < each)).astype(F32).astype(BF16), base.astype(BF16), preferred_element_type=F32
-        ).astype(jnp.int32)
-        slot = jnp.sum(jnp.where((at >= 0) & (at < each), at, 0), axis=1, keepdims=True)
-        hit = (spread + slot == iota((rows, LANES), 1)) & (slot < slots)
-        return hit.astype(F32).T[:cats].astype(BF16)
-
-    across_ref[...] = placed(SLOTS, SLOTS)
-    per = LANES // cats
-    lane = iota((devices, LANES), 1)
-    number = base.astype(jnp.int32)
-    for n in range(choice_ref.shape[1] // LANES):
-        slot = n * per + lane // cats
-        hit = (number + slot == lane % cats) & (slot < SLOTS)
-        choice_ref[:, n * LANES : (n + 1) * LANES] = hit.astype(F32).astype(BF16)
-    merged = summed(placed(SUB, SLOTS), taken_ref[...])
+        own = (at >= 0) & (at < each)
+        spread = jnp.dot(own.astype(F32).astype(BF16), base.astype(BF16), preferred_element_type=F32)
+        slot = jnp.sum(jnp.where(own, at, 0), axis=1, keepdims=True)
+        hit = (spread.astype(jnp.int32) + slot == iota((rows, LANES), 1)) & (slot < SLOTS)
+        return hit.astype(F32)
+
+    place = placed(SLOTS)
+    across_ref[...] = place.T[:cats].astype(BF16)
+    place_ref[...] = place.astype(BF16)
+    merged = summed(placed(SUB).T[:cats].astype(BF16), taken_ref[...])
     cat, day = fitted(merged, cat_goal_ref[...], line_ref[2:3], jnp.ones((1, LANES), F32))
     day_ref[...] = day
-    answer(choice_ref[...], cat, day, out_ref)
-
-
-def owner_kernel(taken_ref, cat_goal_ref, line_ref, day_ref, choice_ref, across_ref, out_ref, day_out_ref):
+    answer(place_ref[...], cat, day, out_ref)
+
+
+def owner_kernel(taken_ref, cat_goal_ref, line_ref, day_ref, place_ref, across_ref, out_ref, day_out_ref):
     merged = summed(across_ref[...], taken_ref[...])
     cat, day = fitted(merged, cat_goal_ref[...], line_ref[2:3], day_ref[...])
     day_out_ref[...] = day
-    answer(choice_ref[...], cat, day, out_ref)
+    answer(place_ref[...], cat, day, out_ref)
 
 
 def owner_last_kernel(taken_ref, cat_goal_ref, line_ref, day_ref, across_ref, out_ref):
@@ -274,13 +261,13 @@
 
 
 def closing_kernel(
-    group_hbm, factor_hbm, back_ref, x_ref, cat_hbm, day_hbm, out_hbm,
+    group_hbm, factor_vmem, back_ref, x_ref, factor_hbm, cat_hbm, day_hbm, out_hbm,
     group_ref, factor_ref, cat_ref, day_ref, scale_ref, buf_ref, sems, out_sems,
 ):
     items, _, stores = x_ref.shape
     loads = [
         pltpu.make_async_copy(group_hbm, group_ref, sems.at[0]),
-        pltpu.make_async_copy(factor_hbm, factor_ref, sems.at[1]),
+        pltpu.make_async_copy(factor_vmem, factor_ref, sems.at[1]),
     ]
     for copy in loads:
         copy.start()
@@ -291,6 +278,7 @@
         cat_ref[:, here] = jnp.concatenate(tiles, axis=0)
         day_ref[:, here] = swap_within(back_ref[pl.ds(t * SUB * each + SUB, SUB, stride=each), :])
     stores_out = [
+        pltpu.make_async_copy(factor_vmem, factor_hbm, sems.at[4]),
         pltpu.make_async_copy(cat_ref, cat_hbm, sems.at[2]),
         pltpu.make_async_copy(day_ref, day_hbm, sems.at[3]),
     ]
@@ -360,10 +348,10 @@
     tile = pltpu.VMEM((SUB, LANES), jnp.int32)
     per_cat = pltpu.VMEM((cats, LANES), F32)
 
-    flat, part, tid, lines, cat_goal = pl.pallas_call(
+    rows, part, slot, lines, cat_goal = pl.pallas_call(
         first_kernel,
         out_shape=(
-            pltpu.VMEM((items * days, stores), BF16),
+            pltpu.VMEM((items * days * stores // LANES, LANES), F32),
             margin,
             tile,
             pltpu.VMEM((SUB, LANES), F32),
@@ -394,41 +382,43 @@
             ),
         )
     )
+    (wide,) = call(spread_kernel, (pltpu.VMEM((items, days * stores), BF16),), rows, name="spread")
     for n in range(ROUNDS):
         total = lax.all_to_all(part, "store", 0, 0, tiled=True)
         shapes = (message(SLOTS if n else SUB),)
         if n == ROUNDS - 1:
-            shapes += (jax.ShapeDtypeStruct((1, LANES), F32),)
-        pooled, *factor = call(pool_kernel, shapes, total, lines, flat, tid, name="pool")
+            shapes += (line,)
+        pooled, *factor = call(pool_kernel, shapes, total, lines, wide, slot, name="pool")
         taken = exchanged(pooled)
         if n == ROUNDS - 1:
             break
         if n == 0:
-            blocks = -(-SLOTS * cats // LANES)
             shapes = (
-                message(2),
+                message(SLOTS),
                 line,
-                pltpu.VMEM((owners, blocks * LANES), BF16),
+                pltpu.VMEM((owners * SLOTS, LANES), BF16),
                 pltpu.VMEM((cats, owners * SLOTS), BF16),
             )
-            back, day, choice, across = call(owner_first_kernel, shapes, taken, cat_goal, lines, name="owner_first")
+            back, day, place, across = call(owner_first_kernel, shapes, taken, cat_goal, lines, name="owner_first")
         else:
-            back, day = call(owner_kernel, (message(2), line), taken, cat_goal, lines, day, choice, across, name="owner")
-        (part,) = call(margin_kernel, (margin,), exchanged(back), flat, tid, name="margin")
+            shapes = (message(SLOTS), line)
+            back, day = call(owner_kernel, shapes, taken, cat_goal, lines, day, place, across, name="owner")
+        (part,) = call(margin_kernel, (margin,), exchanged(back), wide, slot, name="margin")
 
     (back,) = call(
         owner_last_kernel, (message(SUB + 1),), taken, cat_goal, lines, day, across, name="owner_last"
     )
     far_spec = pl.BlockSpec(memory_space=pltpu.HBM)
-    group_outlet_factor, outlet_date_factor, adjusted_tensor = pl.pallas_call(
+    product_factor, group_outlet_factor, outlet_date_factor, adjusted_tensor = pl.pallas_call(
         closing_kernel,
         out_shape=(
+            jax.ShapeDtypeStruct((1, items), F32),
             jax.ShapeDtypeStruct((cats, stores), F32),
             jax.ShapeDtypeStruct((days, stores), F32),
             jax.ShapeDtypeStruct((items, days, stores), BF16),
         ),
-        in_specs=[far_spec] * 2 + vmem(2),
-        out_specs=(far_spec,) * 3,
+        in_specs=[far_spec] + vmem(3),
+        out_specs=(far_spec,) * 4,
         scratch_shapes=[
             pltpu.SMEM((1, items), jnp.int32),
             pltpu.SMEM((1, items), F32),
@@ -436,13 +426,13 @@
             pltpu.VMEM((days, stores), F32),
             pltpu.VMEM((SUB, days, stores), F32),
             pltpu.VMEM((items, days, stores), BF16),
-            pltpu.SemaphoreType.DMA((4,)),
+            pltpu.SemaphoreType.DMA((5,)),
             pltpu.SemaphoreType.DMA((4,)),
         ],
         compiler_params=LIMIT,
         name="closing",
-    )(far(product_group.reshape(1, items)), far(factor[0]), held(exchanged(back)), held(predicted_units))
-    return (factor[0].reshape(items), group_outlet_factor, outlet_date_factor, adjusted_tensor)
+    )(far(product_group.reshape(1, items)), held(factor[0]), held(exchanged(back)), held(predicted_units))
+    return (product_factor.reshape(items), group_outlet_factor, outlet_date_factor, adjusted_tensor)
 
 
 def solution(mesh):

time: 162 us -> 160 us (0.988)
  blocking collectives: 146 us -> 138 us
  starting transfers between devices: 0 us -> 5.39 us
  waiting for transfers between devices: 0 us -> 1.73 us
    all_to_all x4 -> x3, blocking collectives: 31.6 us -> 23 us  [shards(): total = lax.all_to_all(part, 'store', 0, 0, tiled=True)]
    all_to_all x0 -> x1, starting transfers between devices: none -> 5.39 us  [shards(): total = lax.all_to_all(part, 'store', 0, 0, tiled=True)]
    pallas_call x11 -> x12, Pallas kernels: 10.1 us -> 8.3 us  [call(): pl.pallas_call(kernel, out_shape=out_shape, in_specs=vmem(len(args)), out...]
    all_to_all x0 -> x1, waiting for transfers between devices: none -> 1.73 us  [shards(): total = lax.all_to_all(part, 'store', 0, 0, tiled=True)]
  transfers between devices with their start and end apart: 0 -> 1, of which waited for: 0 -> 1; matrix products, arithmetic and copies ran while one was open for 0% -> 0% of each run, Pallas kernels for 0% -> 1%
where the time goes in v5:
time: 160 us; the launch traced here: 159 us
  blocking collectives  138 us (86%)
  Pallas kernels  13.2 us (8%)
  starting transfers between devices  5.39 us (3%)
  waiting for transfers between devices  1.73 us (1%)
    all_to_all x8, blocking collectives, exchanged(): return lax.all_to_all(sent, 'item', 0, 0, tiled=True).reshape(x.shape)  115 us
    all_to_all x3, blocking collectives, shards(): total = lax.all_to_all(part, 'store', 0, 0, tiled=True)  23 us
    pallas_call x12, Pallas kernels, call(): pl.pallas_call(kernel, out_shape=out_shape, in_specs=vmem(len(args)), out...  8.3 us
    all_to_all x1, starting transfers between devices, shards(): total = lax.all_to_all(part, 'store', 0, 0, tiled=True)  5.39 us
  transfers between devices with their start and end apart: 1, of which 1 were waited for; matrix products, arithmetic and copies ran while one was open for 0% of the time, Pallas kernels for 1%

profile of v5, /device:TPU:8, one launch (start us, length us, event | category | flops | bytes accessed | tf_op | source)
XLA Modules:
  0.0 159.1 jit_solution(13133619558809061449)
XLA Ops:
  0.6 3.2 %first.1 = (f32[4096,128]{1,0:T(8,128)S(1)}, f32[8,1,128]{2,1,0:T(1,128)}, s32[8,128]{1,0:T(8,128)S(1)}, f32[8,128]{1,0:T(8,128)S(1)}, f32[64,128]{1,0:T(8,128)S(1)}) custom-call(bf16[128,8,512]{2,1,0:T(8,128)(2,1)} %x_ref.1, s32[1,128]{1,0:T(1,128)} %bitcast.35, f32[1,128]{1,0:T(1,128)} %bitcast.37, f32[64,512]{1,0:T(8,128)} %cat_all_hbm.1, ...), custom_call_target="tpu_custom_call" | custom-call | tf_op jit(solution)/shard_map/first/pallas_call | solution.py:351
  3.8 5.4 %all-to-all-start = ((f32[8,1,128]{2,1,0:T(1,128)}), f32[8,1,128]{2,1,0:T(1,128)S(1)}, u32[]{:S(2)}, u32[]{:S(2)}) async-start(f32[8,1,128]{2,1,0:T(1,128)} %get-tuple-element.23), calls=%async_computation | async-start | bytes 8192 | tf_op jit(solution)/shard_map/all_to_all | solution.py:387
  9.2 2.1 %spread.1.wide_ref = bf16[128,4096]{1,0:T(8,128)(2,1)S(1)} custom-call(f32[4096,128]{1,0:T(8,128)S(1)} %get-tuple-element.25.rows_ref), custom_call_target="tpu_custom_call" | custom-call | tf_op jit(solution)/shard_map/spread/pallas_call | solution.py:323
  11.2 1.7 %all-to-all-done.margin_ref = f32[8,1,128]{2,1,0:T(1,128)S(1)} async-done(((f32[8,1,128]{2,1,0:T(1,128)}), f32[8,1,128]{2,1,0:T(1,128)S(1)}, u32[]{:S(2)}, u32[]{:S(2)}) %all-to-all-start) | async-done | bytes 4128 | tf_op jit(solution)/shard_map/all_to_all | solution.py:387
  13.0 0.2 pool.4
  13.2 20.9 %all_to_all.60 = f32[32,1,1024]{2,1,0:T(1,128)S(1)} all-to-all(f32[32,1,1024]{2,1,0:T(1,128)S(1)} %bitcast.21), channel_id=1, replica_groups=mesh['item'=32,'store'=8] {'item'}, dimensions={0} | all-to-all | bytes 262144 | tf_op jit(solution)/shard_map/all_to_all | solution.py:344
  34.1 1.2 owner_first.1
  35.4 13.7 %all_to_all.61 = f32[32,1,640]{2,1,0:T(1,128)S(1)} all-to-all(f32[32,1,640]{2,1,0:T(1,128)S(1)} %bitcast.31), channel_id=1, replica_groups=mesh['item'=32,'store'=8] {'item'}, dimensions={0} | all-to-all | bytes 163840 | tf_op jit(solution)/shard_map/all_to_all | solution.py:344
  49.0 0.4 margin.3
  49.4 7.7 %all_to_all.62.margin_ref = f32[8,1,128]{2,1,0:T(1,128)S(1)} all-to-all(f32[8,1,128]{2,1,0:T(1,128)S(1)} %margin.3), channel_id=1, replica_groups=mesh['item'=32,'store'=8] {'store'}, dimensions={0} | all-to-all | bytes 8192 | tf_op jit(solution)/shard_map/all_to_all | solution.py:387
  57.1 0.2 pool.5
  57.3 13.3 %all_to_all.63 = f32[32,1,640]{2,1,0:T(1,128)S(1)} all-to-all(f32[32,1,640]{2,1,0:T(1,128)S(1)} %bitcast.24), channel_id=1, replica_groups=mesh['item'=32,'store'=8] {'item'}, dimensions={0} | all-to-all | bytes 163840 | tf_op jit(solution)/shard_map/all_to_all | solution.py:344
  70.7 1.0 owner.2
  71.7 13.3 %all_to_all.64 = f32[32,1,640]{2,1,0:T(1,128)S(1)} all-to-all(f32[32,1,640]{2,1,0:T(1,128)S(1)} %bitcast.34), channel_id=1, replica_groups=mesh['item'=32,'store'=8] {'item'}, dimensions={0} | all-to-all | bytes 163840 | tf_op jit(solution)/shard_map/all_to_all | solution.py:344
  85.0 0.4 margin.4
  85.4 7.7 %all_to_all.65.margin_ref = f32[8,1,128]{2,1,0:T(1,128)S(1)} all-to-all(f32[8,1,128]{2,1,0:T(1,128)S(1)} %margin.4), channel_id=1, replica_groups=mesh['item'=32,'store'=8] {'store'}, dimensions={0} | all-to-all | bytes 8192 | tf_op jit(solution)/shard_map/all_to_all | solution.py:387
  93.1 0.0 copy-start
  93.1 0.2 pool.6
  93.3 13.5 %all_to_all.66 = f32[32,1,640]{2,1,0:T(1,128)S(1)} all-to-all(f32[32,1,640]{2,1,0:T(1,128)S(1)} %bitcast.26), channel_id=1, replica_groups=mesh['item'=32,'store'=8] {'item'}, dimensions={0} | all-to-all | bytes 163840 | tf_op jit(solution)/shard_map/all_to_all | solution.py:344
  106.8 1.0 owner.3
  107.8 13.3 %all_to_all.67 = f32[32,1,640]{2,1,0:T(1,128)S(1)} all-to-all(f32[32,1,640]{2,1,0:T(1,128)S(1)} %bitcast.32), channel_id=1, replica_groups=mesh['item'=32,'store'=8] {'item'}, dimensions={0} | all-to-all | bytes 163840 | tf_op jit(solution)/shard_map/all_to_all | solution.py:344
  121.1 0.4 margin.5
  121.5 7.7 %all_to_all.68.margin_ref = f32[8,1,128]{2,1,0:T(1,128)S(1)} all-to-all(f32[8,1,128]{2,1,0:T(1,128)S(1)} %margin.5), channel_id=1, replica_groups=mesh['item'=32,'store'=8] {'store'}, dimensions={0} | all-to-all | bytes 8192 | tf_op jit(solution)/shard_map/all_to_all | solution.py:387
  129.2 0.2 pool.7
  129.4 13.3 %all_to_all.69 = f32[32,1,640]{2,1,0:T(1,128)S(1)} all-to-all(f32[32,1,640]{2,1,0:T(1,128)S(1)} %bitcast.33), channel_id=1, replica_groups=mesh['item'=32,'store'=8] {'item'}, dimensions={0} | all-to-all | bytes 163840 | tf_op jit(solution)/shard_map/all_to_all | solution.py:344
  142.8 0.9 owner_last.1
  143.6 13.7 %all_to_all.70 = f32[32,1,1152]{2,1,0:T(1,128)S(1)} all-to-all(f32[32,1,1152]{2,1,0:T(1,128)S(1)} %bitcast.19), channel_id=1, replica_groups=mesh['item'=32,'store'=8] {'item'}, dimensions={0} | all-to-all | bytes 294912 | tf_op jit(solution)/shard_map/all_to_all | solution.py:344
  157.3 0.0 copy-done
  157.3 1.8 %closing.1 = (f32[1,128]{1,0:T(1,128)}, f32[64,512]{1,0:T(8,128)}, f32[8,512]{1,0:T(8,128)}, bf16[128,8,512]{2,1,0:T(8,128)(2,1)}) custom-call(s32[1,128]{1,0:T(1,128)} %bitcast.36, f32[1,128]{1,0:T(1,128)S(1)} %get-tuple-element.35.factor_vmem, f32[288,128]{1,0:T(8,128)S(1)} %bitcast.20, bf16[128,8,512]{2,1,0:T(8,128)(2,1)S(1)} %copy-done), custom_call_target="tpu_custom_call" | custom-call | tf_op jit(solution)/shard_map/closing/pallas_call | solution.py:412
Async XLA Ops:
  3.8 9.2 %all-to-all-start = ((f32[8,1,128]{2,1,0:T(1,128)}), f32[8,1,128]{2,1,0:T(1,128)S(1)}, u32[]{:S(2)}, u32[]{:S(2)}) async-start(f32[8,1,128]{2,1,0:T(1,128)} %get-tuple-element.23), calls=%async_computation | async-start | bytes 8192 | tf_op jit(solution)/shard_map/all_to_all | solution.py:387
  93.1 64.3 %copy-start = (bf16[128,8,512]{2,1,0:T(8,128)(2,1)S(1)}, bf16[128,8,512]{2,1,0:T(8,128)(2,1)}, u32[]{:S(2)}) copy-start(bf16[128,8,512]{2,1,0:T(8,128)(2,1)} %x_ref.1) | copy-start | bytes 3145732

commit v6 on v5

--- a/solution.py
+++ b/solution.py
@@ -61,49 +61,65 @@
     return x
 
 
-def eight_sum(x):
-    lane = iota(x.shape, 1)
-    for bit in (1, 2, 4):
-        x = x + jnp.where((lane & bit) == 0, pltpu.roll(x, LANES - bit, 1), pltpu.roll(x, bit, 1))
-    return x
-
-
-def compacted(rows):
-    row = iota((SUB, LANES), 0)
-    tile = rows[0]
-    for q in range(1, SUB):
-        tile = jnp.where(row == q, rows[q], tile)
-    tile = eight_sum(tile)
-    kept = jnp.where((iota((SUB, LANES), 1) & 7) == row, tile, 0.0)
-    return jnp.sum(kept, axis=0, keepdims=True)
-
-
 def picked(x, index):
     return jnp.take_along_axis(x, index, axis=1)
 
 
-def first_kernel(
-    x_hbm, group_hbm, goal_hbm, cat_all_hbm, day_all_hbm,
-    rows_ref, out_ref, slot_ref, line_ref, cat_goal_ref,
-    x_buf, group_ref, goal_ref, cat_all_ref, day_all_ref, sems, small_sems,
-):
+def first_kernel(x_hbm, x_ref, out_ref, sems):
     items, days, stores = x_hbm.shape
     chunks = sems.shape[0]
     block = items // chunks
-    small = []
-    for n, (src, dst) in enumerate(
-        ((group_hbm, group_ref), (goal_hbm, goal_ref), (cat_all_hbm, cat_all_ref), (day_all_hbm, day_all_ref))
-    ):
-        small.append(pltpu.make_async_copy(src, dst, small_sems.at[n]))
-        small[n].start()
     copies = []
     for n in range(chunks):
         rows = pl.ds(n * block, block)
-        copies.append(pltpu.make_async_copy(x_hbm.at[rows], x_buf.at[rows], sems.at[n]))
+        copies.append(pltpu.make_async_copy(x_hbm.at[rows], x_ref.at[rows], sems.at[n]))
         copies[n].start()
-    for copy in small:
+    row, lane = iota((SUB, LANES), 0), iota((SUB, LANES), 1)
+    half = items // SUB
+    gather = (iota((LANES, LANES), 0) // days == iota((LANES, LANES), 1) % half).astype(F32).astype(BF16)
+    tile, q = jnp.zeros((SUB, LANES), F32), 0
+    for n in range(chunks):
+        copies[n].wait()
+        x = x_ref[n * block : (n + 1) * block].astype(F32).reshape(block * days, stores)
+        sums = lax.dot_general(
+            jnp.ones((SUB, stores), BF16), x.astype(BF16), (((1,), (1,)), ((), ())), preferred_element_type=F32
+        )
+        for at in range(0, block * days, LANES):
+            tile = jnp.where(row == q, sums[:, at : at + LANES], tile)
+            q += 1
+    each = jnp.dot(jnp.concatenate(two_parts(tile), axis=0), gather, preferred_element_type=F32)
+    kept = jnp.where(lane // half == row, each[:SUB] + each[SUB:], 0.0)
+    line = jnp.sum(kept, axis=0, keepdims=True)
+    out_ref[...] = jnp.broadcast_to(line[None], out_ref.shape)
+
+
+def spread_kernel(
+    x_ref, group_hbm, goal_hbm, cat_all_hbm, day_all_hbm,
+    wide_ref, slot_ref, line_ref, cat_goal_ref,
+    rows_ref, group_ref, goal_ref, cat_all_ref, day_all_ref, sems,
+):
+    pairs = ((group_hbm, group_ref), (goal_hbm, goal_ref), (cat_all_hbm, cat_all_ref), (day_all_hbm, day_all_ref))
+    copies = [pltpu.make_async_copy(src, dst, sems.at[n]) for n, (src, dst) in enumerate(pairs)]
+    for copy in copies:
+        copy.start()
+    items, days, stores = x_ref.shape
+    tall = 2 * SUB
+
+    def step(n, carry):
+        into = pl.ds(pl.multiple_of(n * tall, tall), tall)
+        x = x_ref[into].astype(F32).reshape(tall * days, stores)
+        for t in range(stores // LANES):
+            at = (t * items + n * tall) * days
+            rows_ref[pl.ds(pl.multiple_of(at, SUB), tall * days), :] = x[:, t * LANES : (t + 1) * LANES]
+            tiles = [rows_ref[pl.ds(at + d, tall, stride=days), :] for d in range(days)]
+            for j, tile in enumerate(swap_blocks(tiles)):
+                column = (t * SUB + j) * LANES
+                wide_ref[into, column : column + LANES] = tile.astype(BF16)
+        return carry
+
+    lax.fori_loop(0, items // tall, step, 0)
+    for copy in copies:
         copy.wait()
-
     row, lane = iota((SUB, LANES), 0), iota((SUB, LANES), 1)
     group = jnp.broadcast_to(group_ref[...], (SUB, LANES))
     first = picked(group, jnp.zeros_like(lane))
@@ -119,39 +135,6 @@
         cat_goal_ref[rows] = picked(cat_all_ref[rows, there], index)
     day_goal = jnp.where(lane // width == row, picked(day_all_ref[:, there], index), 0.0)
     line_ref[2:3] = jnp.sum(day_goal, axis=0, keepdims=True)
-
-    tiles = []
-    for n in range(chunks):
-        copies[n].wait()
-        x = x_buf[n * block : (n + 1) * block].astype(F32).reshape(block * days, stores)
-        for t in range(stores // LANES):
-            at = (t * items + n * block) * days
-            rows_ref[at : at + block * days] = x[:, t * LANES : (t + 1) * LANES]
-        sums = lax.dot_general(
-            jnp.ones((SUB, stores), BF16), x.astype(BF16), (((1,), (1,)), ((), ())), preferred_element_type=F32
-        )
-        tiles += [sums[:, q * LANES : (q + 1) * LANES] for q in range(block * days // LANES)]
-    line = jnp.broadcast_to(compacted(tiles), (SUB, LANES))
-    half = LANES // SUB
-    line = picked(line, lane % half * SUB + lane // half)[:1]
-    out_ref[...] = jnp.broadcast_to(line[None], out_ref.shape)
-
-
-def spread_kernel(rows_ref, out_ref):
-    tall = 2 * SUB
-    items, columns = out_ref.shape
-
-    def step(n, carry):
-        into = pl.ds(pl.multiple_of(n * tall, tall), tall)
-        for t in range(columns // (SUB * LANES)):
-            at = (t * items + n * tall) * SUB
-            tiles = [rows_ref[pl.ds(at + d, tall, stride=SUB), :] for d in range(SUB)]
-            for j, tile in enumerate(swap_blocks(tiles)):
-                at = (t * SUB + j) * LANES
-                out_ref[into, at : at + LANES] = tile.astype(BF16)
-        return carry
-
-    lax.fori_loop(0, items // tall, step, 0)
 
 
 def margin_kernel(back_ref, wide_ref, slot_ref, out_ref):
@@ -195,11 +178,10 @@
     width = LANES // SUB
     for _ in range(INNER):
         below = merged * day
-        step = LANES // 2
-        while step >= width:
-            below = below + pltpu.roll(below, step, 1)
-            step //= 2
-        cat = cat_goal / below
+        turned = [below] + [pltpu.roll(below, n * width, 1) for n in range(1, SUB)]
+        while len(turned) > 1:
+            turned = [turned[n] + turned[n + 1] for n in range(0, len(turned), 2)]
+        cat = cat_goal / turned[0]
         day = day_goal / jnp.sum(merged * cat, axis=0, keepdims=True)
     return cat, day
 
@@ -210,11 +192,8 @@
 
 
 def answer(place, cat, day, out_ref):
-    cats = cat.shape[0]
-    product = jnp.concatenate([cat * day, jnp.zeros((LANES - cats, LANES), F32)], axis=0)
-    parts = jnp.concatenate(two_parts(product), axis=1)
-    sent = jnp.dot(place, parts, preferred_element_type=F32)
-    out_ref[...] = sent[:, :LANES] + sent[:, LANES:]
+    parts = jnp.concatenate(two_parts(cat * day), axis=0)
+    out_ref[...] = jnp.dot(place, parts, preferred_element_type=F32)
 
 
 def owner_first_kernel(taken_ref, cat_goal_ref, line_ref, out_ref, day_ref, place_ref, across_ref):
@@ -228,7 +207,8 @@
         own = (at >= 0) & (at < each)
         spread = jnp.dot(own.astype(F32).astype(BF16), base.astype(BF16), preferred_element_type=F32)
         slot = jnp.sum(jnp.where(own, at, 0), axis=1, keepdims=True)
-        hit = (spread.astype(jnp.int32) + slot == iota((rows, LANES), 1)) & (slot < SLOTS)
+        lane = iota((rows, LANES), 1)
+        hit = (spread.astype(jnp.int32) + slot == lane % cats) & (slot < SLOTS)
         return hit.astype(F32)
 
     place = placed(SLOTS)
@@ -348,41 +328,43 @@
     tile = pltpu.VMEM((SUB, LANES), jnp.int32)
     per_cat = pltpu.VMEM((cats, LANES), F32)
 
-    rows, part, slot, lines, cat_goal = pl.pallas_call(
+    far_spec = pl.BlockSpec(memory_space=pltpu.HBM)
+    near, part = pl.pallas_call(
         first_kernel,
+        out_shape=(pltpu.VMEM(predicted_units.shape, BF16), margin),
+        in_specs=[far_spec],
+        out_specs=tuple(vmem(2)),
+        scratch_shapes=[pltpu.SemaphoreType.DMA((8,))],
+        compiler_params=LIMIT,
+        name="first",
+    )(far(predicted_units))
+    wide, slot, lines, cat_goal = pl.pallas_call(
+        spread_kernel,
         out_shape=(
-            pltpu.VMEM((items * days * stores // LANES, LANES), F32),
-            margin,
+            pltpu.VMEM((items, days * stores), BF16),
             tile,
             pltpu.VMEM((SUB, LANES), F32),
             per_cat,
         ),
-        in_specs=[pl.BlockSpec(memory_space=pltpu.HBM)] * 5,
-        out_specs=tuple(vmem(5)),
+        in_specs=vmem(1) + [far_spec] * 4,
+        out_specs=tuple(vmem(4)),
         scratch_shapes=[
-            pltpu.VMEM(predicted_units.shape, BF16),
+            pltpu.VMEM((items * days * stores // LANES, LANES), F32),
             pltpu.VMEM((1, items), jnp.int32),
             pltpu.VMEM((1, items), F32),
             pltpu.VMEM((cats, stores), F32),
             pltpu.VMEM((days, stores), F32),
             pltpu.SemaphoreType.DMA((4,)),
-            pltpu.SemaphoreType.DMA((4,)),
         ],
         compiler_params=LIMIT,
-        name="first",
+        name="spread",
     )(
-        *map(
-            far,
-            (
-                predicted_units,
-                product_group.reshape(1, items),
-                product_goal.reshape(1, items),
-                group_outlet_goal,
-                outlet_date_goal,
-            ),
-        )
+        held(near),
+        far(product_group.reshape(1, items)),
+        far(product_goal.reshape(1, items)),
+        far(group_outlet_goal),
+        far(outlet_date_goal),
     )
-    (wide,) = call(spread_kernel, (pltpu.VMEM((items, days * stores), BF16),), rows, name="spread")
     for n in range(ROUNDS):
         total = lax.all_to_all(part, "store", 0, 0, tiled=True)
         shapes = (message(SLOTS if n else SUB),)
@@ -408,7 +390,6 @@
     (back,) = call(
         owner_last_kernel, (message(SUB + 1),), taken, cat_goal, lines, day, across, name="owner_last"
     )
-    far_spec = pl.BlockSpec(memory_space=pltpu.HBM)
     product_factor, group_outlet_factor, outlet_date_factor, adjusted_tensor = pl.pallas_call(
         closing_kernel,
         out_shape=(
@@ -431,7 +412,7 @@
         ],
         compiler_params=LIMIT,
         name="closing",
-    )(far(product_group.reshape(1, items)), held(factor[0]), held(exchanged(back)), held(predicted_units))
+    )(far(product_group.reshape(1, items)), held(factor[0]), held(exchanged(back)), held(near))
     return (product_factor.reshape(items), group_outlet_factor, outlet_date_factor, adjusted_tensor)
 
 

time: 160 us -> 159 us (level)
    pallas_call x12 -> x11, Pallas kernels: 8.3 us -> 5.19 us  [call(): pl.pallas_call(kernel, out_shape=out_shape, in_specs=vmem(len(args)), out...]
    pallas_call x1 -> x2, Pallas kernels: 3.15 us -> 5.47 us  [the longest x1 3.16 us: shards(): pl.pallas_call(first_kernel, out_shape=(pltpu.VMEM(predicted_units.shape,...]
where the time goes in v6:
time: 159 us; the launch traced here: 158 us
  blocking collectives  138 us (87%)
  Pallas kernels  12.5 us (8%)
  starting transfers between devices  5.39 us (3%)
    all_to_all x8, blocking collectives, exchanged(): return lax.all_to_all(sent, 'item', 0, 0, tiled=True).reshape(x.shape)  115 us
    all_to_all x3, blocking collectives, shards(): total = lax.all_to_all(part, 'store', 0, 0, tiled=True)  23 us
    all_to_all x1, starting transfers between devices, shards(): total = lax.all_to_all(part, 'store', 0, 0, tiled=True)  5.39 us
    pallas_call x11, Pallas kernels, call(): pl.pallas_call(kernel, out_shape=out_shape, in_specs=vmem(len(args)), out...  5.19 us
  transfers between devices with their start and end apart: 1, of which 1 were waited for; matrix products, arithmetic and copies ran while one was open for 0% of the time, Pallas kernels for 1%

profile of v6, /device:TPU:8, one launch (start us, length us, event | category | flops | bytes accessed | tf_op | source)
XLA Modules:
  0.0 157.9 jit_solution(12094535393059332179)
XLA Ops:
  0.6 3.2 %first.1 = (bf16[128,8,512]{2,1,0:T(8,128)(2,1)S(1)}, f32[8,1,128]{2,1,0:T(1,128)}) custom-call(bf16[128,8,512]{2,1,0:T(8,128)(2,1)} %x_hbm.1), custom_call_target="tpu_custom_call" | custom-call | tf_op jit(solution)/shard_map/first/pallas_call | solution.py:332
  3.8 5.4 %all-to-all-start = ((f32[8,1,128]{2,1,0:T(1,128)}), f32[8,1,128]{2,1,0:T(1,128)S(1)}, u32[]{:S(2)}, u32[]{:S(2)}) async-start(f32[8,1,128]{2,1,0:T(1,128)} %get-tuple-element.24), calls=%async_computation | async-start | bytes 8192 | tf_op jit(solution)/shard_map/all_to_all | solution.py:369
  9.2 2.3 %spread.1 = (bf16[128,4096]{1,0:T(8,128)(2,1)S(1)}, s32[8,128]{1,0:T(8,128)S(1)}, f32[8,128]{1,0:T(8,128)S(1)}, f32[64,128]{1,0:T(8,128)S(1)}) custom-call(bf16[128,8,512]{2,1,0:T(8,128)(2,1)S(1)} %get-tuple-element.25.x_ref, s32[1,128]{1,0:T(1,128)} %bitcast.35, f32[1,128]{1,0:T(1,128)} %bitcast.37, f32[64,512]{1,0:T(8,128)} %cat_all_hbm.1, ...), custom_call_target="tpu_custom_call" | custom-call | tf_op jit(solution)/shard_map/spread/pallas_call | solution.py:341
  11.5 1.5 all-to-all-done.margin_ref
  13.0 0.2 pool.4
  13.2 20.9 %all_to_all.60 = f32[32,1,1024]{2,1,0:T(1,128)S(1)} all-to-all(f32[32,1,1024]{2,1,0:T(1,128)S(1)} %bitcast.21), channel_id=1, replica_groups=mesh['item'=32,'store'=8] {'item'}, dimensions={0} | all-to-all | bytes 262144 | tf_op jit(solution)/shard_map/all_to_all | solution.py:324
  34.1 1.0 owner_first.1
  35.1 13.7 %all_to_all.61 = f32[32,1,640]{2,1,0:T(1,128)S(1)} all-to-all(f32[32,1,640]{2,1,0:T(1,128)S(1)} %bitcast.31), channel_id=1, replica_groups=mesh['item'=32,'store'=8] {'item'}, dimensions={0} | all-to-all | bytes 163840 | tf_op jit(solution)/shard_map/all_to_all | solution.py:324
  48.8 0.4 margin.3
  49.2 7.7 %all_to_all.62.margin_ref = f32[8,1,128]{2,1,0:T(1,128)S(1)} all-to-all(f32[8,1,128]{2,1,0:T(1,128)S(1)} %margin.3), channel_id=1, replica_groups=mesh['item'=32,'store'=8] {'store'}, dimensions={0} | all-to-all | bytes 8192 | tf_op jit(solution)/shard_map/all_to_all | solution.py:369
  56.9 0.2 pool.5
  57.1 13.3 %all_to_all.63 = f32[32,1,640]{2,1,0:T(1,128)S(1)} all-to-all(f32[32,1,640]{2,1,0:T(1,128)S(1)} %bitcast.24), channel_id=1, replica_groups=mesh['item'=32,'store'=8] {'item'}, dimensions={0} | all-to-all | bytes 163840 | tf_op jit(solution)/shard_map/all_to_all | solution.py:324
  70.4 0.7 owner.2
  71.2 13.3 %all_to_all.64 = f32[32,1,640]{2,1,0:T(1,128)S(1)} all-to-all(f32[32,1,640]{2,1,0:T(1,128)S(1)} %bitcast.34), channel_id=1, replica_groups=mesh['item'=32,'store'=8] {'item'}, dimensions={0} | all-to-all | bytes 163840 | tf_op jit(solution)/shard_map/all_to_all | solution.py:324
  84.5 0.4 margin.4
  84.9 7.7 %all_to_all.65.margin_ref = f32[8,1,128]{2,1,0:T(1,128)S(1)} all-to-all(f32[8,1,128]{2,1,0:T(1,128)S(1)} %margin.4), channel_id=1, replica_groups=mesh['item'=32,'store'=8] {'store'}, dimensions={0} | all-to-all | bytes 8192 | tf_op jit(solution)/shard_map/all_to_all | solution.py:369
  92.6 0.2 pool.6
  92.8 13.3 %all_to_all.66 = f32[32,1,640]{2,1,0:T(1,128)S(1)} all-to-all(f32[32,1,640]{2,1,0:T(1,128)S(1)} %bitcast.26), channel_id=1, replica_groups=mesh['item'=32,'store'=8] {'item'}, dimensions={0} | all-to-all | bytes 163840 | tf_op jit(solution)/shard_map/all_to_all | solution.py:324
  106.1 0.7 owner.3
  106.9 13.3 %all_to_all.67 = f32[32,1,640]{2,1,0:T(1,128)S(1)} all-to-all(f32[32,1,640]{2,1,0:T(1,128)S(1)} %bitcast.32), channel_id=1, replica_groups=mesh['item'=32,'store'=8] {'item'}, dimensions={0} | all-to-all | bytes 163840 | tf_op jit(solution)/shard_map/all_to_all | solution.py:324
  120.2 0.4 margin.5
  120.6 7.7 %all_to_all.68.margin_ref = f32[8,1,128]{2,1,0:T(1,128)S(1)} all-to-all(f32[8,1,128]{2,1,0:T(1,128)S(1)} %margin.5), channel_id=1, replica_groups=mesh['item'=32,'store'=8] {'store'}, dimensions={0} | all-to-all | bytes 8192 | tf_op jit(solution)/shard_map/all_to_all | solution.py:369
  128.2 0.2 pool.7
  128.5 13.3 %all_to_all.69 = f32[32,1,640]{2,1,0:T(1,128)S(1)} all-to-all(f32[32,1,640]{2,1,0:T(1,128)S(1)} %bitcast.33), channel_id=1, replica_groups=mesh['item'=32,'store'=8] {'item'}, dimensions={0} | all-to-all | bytes 163840 | tf_op jit(solution)/shard_map/all_to_all | solution.py:324
  141.8 0.6 owner_last.1
  142.4 13.7 %all_to_all.70 = f32[32,1,1152]{2,1,0:T(1,128)S(1)} all-to-all(f32[32,1,1152]{2,1,0:T(1,128)S(1)} %bitcast.19), channel_id=1, replica_groups=mesh['item'=32,'store'=8] {'item'}, dimensions={0} | all-to-all | bytes 294912 | tf_op jit(solution)/shard_map/all_to_all | solution.py:324
  156.1 1.8 %closing.1 = (f32[1,128]{1,0:T(1,128)}, f32[64,512]{1,0:T(8,128)}, f32[8,512]{1,0:T(8,128)}, bf16[128,8,512]{2,1,0:T(8,128)(2,1)}) custom-call(s32[1,128]{1,0:T(1,128)} %bitcast.36, f32[1,128]{1,0:T(1,128)S(1)} %get-tuple-element.37.factor_vmem, f32[288,128]{1,0:T(8,128)S(1)} %bitcast.20, bf16[128,8,512]{2,1,0:T(8,128)(2,1)S(1)} %get-tuple-element.25.x_ref), custom_call_target="tpu_custom_call" | custom-call | tf_op jit(solution)/shard_map/closing/pallas_call | solution.py:393
Async XLA Ops:
  3.8 9.2 %all-to-all-start = ((f32[8,1,128]{2,1,0:T(1,128)}), f32[8,1,128]{2,1,0:T(1,128)S(1)}, u32[]{:S(2)}, u32[]{:S(2)}) async-start(f32[8,1,128]{2,1,0:T(1,128)} %get-tuple-element.24), calls=%async_computation | async-start | bytes 8192 | tf_op jit(solution)/shard_map/all_to_all | solution.py:369

commit v7 on v6

--- a/solution.py
+++ b/solution.py
@@ -65,28 +65,18 @@
     return jnp.take_along_axis(x, index, axis=1)
 
 
-def first_kernel(x_hbm, x_ref, out_ref, sems):
-    items, days, stores = x_hbm.shape
-    chunks = sems.shape[0]
-    block = items // chunks
-    copies = []
-    for n in range(chunks):
-        rows = pl.ds(n * block, block)
-        copies.append(pltpu.make_async_copy(x_hbm.at[rows], x_ref.at[rows], sems.at[n]))
-        copies[n].start()
+def first_kernel(x_ref, out_ref):
+    items, days, stores = x_ref.shape
     row, lane = iota((SUB, LANES), 0), iota((SUB, LANES), 1)
     half = items // SUB
     gather = (iota((LANES, LANES), 0) // days == iota((LANES, LANES), 1) % half).astype(F32).astype(BF16)
-    tile, q = jnp.zeros((SUB, LANES), F32), 0
-    for n in range(chunks):
-        copies[n].wait()
-        x = x_ref[n * block : (n + 1) * block].astype(F32).reshape(block * days, stores)
-        sums = lax.dot_general(
-            jnp.ones((SUB, stores), BF16), x.astype(BF16), (((1,), (1,)), ((), ())), preferred_element_type=F32
-        )
-        for at in range(0, block * days, LANES):
-            tile = jnp.where(row == q, sums[:, at : at + LANES], tile)
-            q += 1
+    x = x_ref[...].astype(F32).reshape(items * days, stores).astype(BF16)
+    sums = lax.dot_general(
+        jnp.ones((SUB, stores), BF16), x, (((1,), (1,)), ((), ())), preferred_element_type=F32
+    )
+    tile = sums[:, :LANES]
+    for q in range(1, SUB):
+        tile = jnp.where(row == q, sums[:, q * LANES : (q + 1) * LANES], tile)
     each = jnp.dot(jnp.concatenate(two_parts(tile), axis=0), gather, preferred_element_type=F32)
     kept = jnp.where(lane // half == row, each[:SUB] + each[SUB:], 0.0)
     line = jnp.sum(kept, axis=0, keepdims=True)
@@ -329,15 +319,7 @@
     per_cat = pltpu.VMEM((cats, LANES), F32)
 
     far_spec = pl.BlockSpec(memory_space=pltpu.HBM)
-    near, part = pl.pallas_call(
-        first_kernel,
-        out_shape=(pltpu.VMEM(predicted_units.shape, BF16), margin),
-        in_specs=[far_spec],
-        out_specs=tuple(vmem(2)),
-        scratch_shapes=[pltpu.SemaphoreType.DMA((8,))],
-        compiler_params=LIMIT,
-        name="first",
-    )(far(predicted_units))
+    (part,) = call(first_kernel, (margin,), predicted_units, name="first")
     wide, slot, lines, cat_goal = pl.pallas_call(
         spread_kernel,
         out_shape=(
@@ -359,7 +341,7 @@
         compiler_params=LIMIT,
         name="spread",
     )(
-        held(near),
+        held(predicted_units),
         far(product_group.reshape(1, items)),
         far(product_goal.reshape(1, items)),
         far(group_outlet_goal),
@@ -412,7 +394,7 @@
         ],
         compiler_params=LIMIT,
         name="closing",
-    )(far(product_group.reshape(1, items)), held(factor[0]), held(exchanged(back)), held(near))
+    )(far(product_group.reshape(1, items)), held(factor[0]), held(exchanged(back)), held(predicted_units))
     return (product_factor.reshape(items), group_outlet_factor, outlet_date_factor, adjusted_tensor)
 
 

time: 159 us -> 158 us (level)
  Pallas kernels: 12.5 us -> 10.4 us
    pallas_call x1 -> x0, Pallas kernels: 3.16 us -> none  [shards(): pl.pallas_call(first_kernel, out_shape=(pltpu.VMEM(predicted_units.shape,...]
    pallas_call x11 -> x12, Pallas kernels: 5.19 us -> 6.3 us  [call(): pl.pallas_call(kernel, out_shape=out_shape, in_specs=vmem(len(args)), out...]
where the time goes in v7:
time: 158 us; the launch traced here: 157 us
  blocking collectives  138 us (87%)
  Pallas kernels  10.4 us (7%)
  starting transfers between devices  5.38 us (3%)
    all_to_all x8, blocking collectives, exchanged(): return lax.all_to_all(sent, 'item', 0, 0, tiled=True).reshape(x.shape)  115 us
    all_to_all x3, blocking collectives, shards(): total = lax.all_to_all(part, 'store', 0, 0, tiled=True)  23 us
    pallas_call x12, Pallas kernels, call(): pl.pallas_call(kernel, out_shape=out_shape, in_specs=vmem(len(args)), out...  6.3 us
    all_to_all x1, starting transfers between devices, shards(): total = lax.all_to_all(part, 'store', 0, 0, tiled=True)  5.38 us
  transfers between devices with their start and end apart: 1, of which 1 were waited for; matrix products, arithmetic and copies ran while one was open for 0% of the time, Pallas kernels for 1%

profile of v7, /device:TPU:8, one launch (start us, length us, event | category | flops | bytes accessed | tf_op | source)
XLA Modules:
  0.0 157.1 jit_solution(14873785437659020395)
XLA Ops:
  0.6 0.0 copy-start
  0.6 1.2 copy-done
  1.9 0.0 copy-start.1
  1.9 1.1 first.1
  3.0 5.4 %all-to-all-start = ((f32[8,1,128]{2,1,0:T(1,128)}), f32[8,1,128]{2,1,0:T(1,128)S(1)}, u32[]{:S(2)}, u32[]{:S(2)}) async-start(f32[8,1,128]{2,1,0:T(1,128)} %first.1), calls=%async_computation | async-start | bytes 8192 | tf_op jit(solution)/shard_map/all_to_all | solution.py:351
  8.3 0.0 copy-done.1
  8.3 2.3 %spread.1 = (bf16[128,4096]{1,0:T(8,128)(2,1)S(1)}, s32[8,128]{1,0:T(8,128)S(1)}, f32[8,128]{1,0:T(8,128)S(1)}, f32[64,128]{1,0:T(8,128)S(1)}) custom-call(bf16[128,8,512]{2,1,0:T(8,128)(2,1)S(1)} %copy-done.1, s32[1,128]{1,0:T(1,128)} %bitcast.35, f32[1,128]{1,0:T(1,128)} %bitcast.37, f32[64,512]{1,0:T(8,128)} %cat_all_hbm.1, f32[8,512]{1,0:T(8,128)} %day_all_hbm.1), custom_call_target="tpu_custom_call" | custom-call | tf_op jit(solution)/shard_map/spread/pallas_call | solution.py:323
  10.7 1.5 all-to-all-done.margin_ref
  12.1 0.2 pool.4
  12.4 20.9 %all_to_all.60 = f32[32,1,1024]{2,1,0:T(1,128)S(1)} all-to-all(f32[32,1,1024]{2,1,0:T(1,128)S(1)} %bitcast.21), channel_id=1, replica_groups=mesh['item'=32,'store'=8] {'item'}, dimensions={0} | all-to-all | bytes 262144 | tf_op jit(solution)/shard_map/all_to_all | solution.py:314
  33.3 1.0 owner_first.1
  34.3 13.7 %all_to_all.61 = f32[32,1,640]{2,1,0:T(1,128)S(1)} all-to-all(f32[32,1,640]{2,1,0:T(1,128)S(1)} %bitcast.31), channel_id=1, replica_groups=mesh['item'=32,'store'=8] {'item'}, dimensions={0} | all-to-all | bytes 163840 | tf_op jit(solution)/shard_map/all_to_all | solution.py:314
  48.0 0.4 margin.3
  48.4 7.7 %all_to_all.62.margin_ref = f32[8,1,128]{2,1,0:T(1,128)S(1)} all-to-all(f32[8,1,128]{2,1,0:T(1,128)S(1)} %margin.3), channel_id=1, replica_groups=mesh['item'=32,'store'=8] {'store'}, dimensions={0} | all-to-all | bytes 8192 | tf_op jit(solution)/shard_map/all_to_all | solution.py:351
  56.0 0.2 pool.5
  56.3 13.3 %all_to_all.63 = f32[32,1,640]{2,1,0:T(1,128)S(1)} all-to-all(f32[32,1,640]{2,1,0:T(1,128)S(1)} %bitcast.24), channel_id=1, replica_groups=mesh['item'=32,'store'=8] {'item'}, dimensions={0} | all-to-all | bytes 163840 | tf_op jit(solution)/shard_map/all_to_all | solution.py:314
  69.6 0.7 owner.2
  70.3 13.3 %all_to_all.64 = f32[32,1,640]{2,1,0:T(1,128)S(1)} all-to-all(f32[32,1,640]{2,1,0:T(1,128)S(1)} %bitcast.34), channel_id=1, replica_groups=mesh['item'=32,'store'=8] {'item'}, dimensions={0} | all-to-all | bytes 163840 | tf_op jit(solution)/shard_map/all_to_all | solution.py:314
  83.7 0.4 margin.4
  84.1 7.7 %all_to_all.65.margin_ref = f32[8,1,128]{2,1,0:T(1,128)S(1)} all-to-all(f32[8,1,128]{2,1,0:T(1,128)S(1)} %margin.4), channel_id=1, replica_groups=mesh['item'=32,'store'=8] {'store'}, dimensions={0} | all-to-all | bytes 8192 | tf_op jit(solution)/shard_map/all_to_all | solution.py:351
  91.7 0.2 pool.6
  91.9 13.3 %all_to_all.66 = f32[32,1,640]{2,1,0:T(1,128)S(1)} all-to-all(f32[32,1,640]{2,1,0:T(1,128)S(1)} %bitcast.26), channel_id=1, replica_groups=mesh['item'=32,'store'=8] {'item'}, dimensions={0} | all-to-all | bytes 163840 | tf_op jit(solution)/shard_map/all_to_all | solution.py:314
  105.3 0.7 owner.3
  106.0 13.3 %all_to_all.67 = f32[32,1,640]{2,1,0:T(1,128)S(1)} all-to-all(f32[32,1,640]{2,1,0:T(1,128)S(1)} %bitcast.32), channel_id=1, replica_groups=mesh['item'=32,'store'=8] {'item'}, dimensions={0} | all-to-all | bytes 163840 | tf_op jit(solution)/shard_map/all_to_all | solution.py:314
  119.4 0.4 margin.5
  119.7 7.7 %all_to_all.68.margin_ref = f32[8,1,128]{2,1,0:T(1,128)S(1)} all-to-all(f32[8,1,128]{2,1,0:T(1,128)S(1)} %margin.5), channel_id=1, replica_groups=mesh['item'=32,'store'=8] {'store'}, dimensions={0} | all-to-all | bytes 8192 | tf_op jit(solution)/shard_map/all_to_all | solution.py:351
  127.4 0.2 pool.7
  127.6 13.3 %all_to_all.69 = f32[32,1,640]{2,1,0:T(1,128)S(1)} all-to-all(f32[32,1,640]{2,1,0:T(1,128)S(1)} %bitcast.33), channel_id=1, replica_groups=mesh['item'=32,'store'=8] {'item'}, dimensions={0} | all-to-all | bytes 163840 | tf_op jit(solution)/shard_map/all_to_all | solution.py:314
  141.0 0.6 owner_last.1
  141.6 13.7 %all_to_all.70 = f32[32,1,1152]{2,1,0:T(1,128)S(1)} all-to-all(f32[32,1,1152]{2,1,0:T(1,128)S(1)} %bitcast.19), channel_id=1, replica_groups=mesh['item'=32,'store'=8] {'item'}, dimensions={0} | all-to-all | bytes 294912 | tf_op jit(solution)/shard_map/all_to_all | solution.py:314
  155.3 1.8 %closing.1 = (f32[1,128]{1,0:T(1,128)}, f32[64,512]{1,0:T(8,128)}, f32[8,512]{1,0:T(8,128)}, bf16[128,8,512]{2,1,0:T(8,128)(2,1)}) custom-call(s32[1,128]{1,0:T(1,128)} %bitcast.36, f32[1,128]{1,0:T(1,128)S(1)} %get-tuple-element.33.factor_vmem, f32[288,128]{1,0:T(8,128)S(1)} %bitcast.20, bf16[128,8,512]{2,1,0:T(8,128)(2,1)S(1)} %copy-done.1), custom_call_target="tpu_custom_call" | custom-call | tf_op jit(solution)/shard_map/closing/pallas_call | solution.py:375
Async XLA Ops:
  0.6 1.2 copy-start
  1.9 6.5 %copy-start.1 = (bf16[128,8,512]{2,1,0:T(8,128)(2,1)S(1)}, bf16[128,8,512]{2,1,0:T(8,128)(2,1)}, u32[]{:S(2)}) copy-start(bf16[128,8,512]{2,1,0:T(8,128)(2,1)} %x_ref.5) | copy-start | bytes 3145732
  3.0 9.2 %all-to-all-start = ((f32[8,1,128]{2,1,0:T(1,128)}), f32[8,1,128]{2,1,0:T(1,128)S(1)}, u32[]{:S(2)}, u32[]{:S(2)}) async-start(f32[8,1,128]{2,1,0:T(1,128)} %first.1), calls=%async_computation | async-start | bytes 8192 | tf_op jit(solution)/shard_map/all_to_all | solution.py:351

commit v8 on v7

--- a/solution.py
+++ b/solution.py
@@ -65,6 +65,12 @@
     return jnp.take_along_axis(x, index, axis=1)
 
 
+def near_kernel(x_hbm, x_ref, sem):
+    copy = pltpu.make_async_copy(x_hbm, x_ref, sem)
+    copy.start()
+    copy.wait()
+
+
 def first_kernel(x_ref, out_ref):
     items, days, stores = x_ref.shape
     row, lane = iota((SUB, LANES), 0), iota((SUB, LANES), 1)
@@ -85,7 +91,7 @@
 
 def spread_kernel(
     x_ref, group_hbm, goal_hbm, cat_all_hbm, day_all_hbm,
-    wide_ref, slot_ref, line_ref, cat_goal_ref,
+    wide_ref, slot_ref, own_ref, line_ref, cat_goal_ref,
     rows_ref, group_ref, goal_ref, cat_all_ref, day_all_ref, sems,
 ):
     pairs = ((group_hbm, group_ref), (goal_hbm, goal_ref), (cat_all_hbm, cat_all_ref), (day_all_hbm, day_all_ref))
@@ -114,6 +120,7 @@
     group = jnp.broadcast_to(group_ref[...], (SUB, LANES))
     first = picked(group, jnp.zeros_like(lane))
     slot_ref[...] = group - first
+    own_ref[...] = group_ref[...]
     line_ref[0:1] = goal_ref[...]
     line_ref[1:2] = first[:1].astype(F32)
     width = LANES // days
@@ -231,12 +238,12 @@
 
 
 def closing_kernel(
-    group_hbm, factor_vmem, back_ref, x_ref, factor_hbm, cat_hbm, day_hbm, out_hbm,
+    group_vmem, factor_vmem, back_ref, x_ref, factor_hbm, cat_hbm, day_hbm, out_hbm,
     group_ref, factor_ref, cat_ref, day_ref, scale_ref, buf_ref, sems, out_sems,
 ):
     items, _, stores = x_ref.shape
     loads = [
-        pltpu.make_async_copy(group_hbm, group_ref, sems.at[0]),
+        pltpu.make_async_copy(group_vmem, group_ref, sems.at[0]),
         pltpu.make_async_copy(factor_vmem, factor_ref, sems.at[1]),
     ]
     for copy in loads:
@@ -319,17 +326,27 @@
     per_cat = pltpu.VMEM((cats, LANES), F32)
 
     far_spec = pl.BlockSpec(memory_space=pltpu.HBM)
-    (part,) = call(first_kernel, (margin,), predicted_units, name="first")
-    wide, slot, lines, cat_goal = pl.pallas_call(
+    (near,) = pl.pallas_call(
+        near_kernel,
+        out_shape=(pltpu.VMEM(predicted_units.shape, BF16),),
+        in_specs=[far_spec],
+        out_specs=tuple(vmem(1)),
+        scratch_shapes=[pltpu.SemaphoreType.DMA],
+        compiler_params=LIMIT,
+        name="near",
+    )(far(predicted_units))
+    (part,) = call(first_kernel, (margin,), near, name="first")
+    wide, slot, own, lines, cat_goal = pl.pallas_call(
         spread_kernel,
         out_shape=(
             pltpu.VMEM((items, days * stores), BF16),
             tile,
+            pltpu.VMEM((1, items), jnp.int32),
             pltpu.VMEM((SUB, LANES), F32),
             per_cat,
         ),
         in_specs=vmem(1) + [far_spec] * 4,
-        out_specs=tuple(vmem(4)),
+        out_specs=tuple(vmem(5)),
         scratch_shapes=[
             pltpu.VMEM((items * days * stores // LANES, LANES), F32),
             pltpu.VMEM((1, items), jnp.int32),
@@ -341,7 +358,7 @@
         compiler_params=LIMIT,
         name="spread",
     )(
-        held(predicted_units),
+        held(near),
         far(product_group.reshape(1, items)),
         far(product_goal.reshape(1, items)),
         far(group_outlet_goal),
@@ -380,7 +397,7 @@
             jax.ShapeDtypeStruct((days, stores), F32),
             jax.ShapeDtypeStruct((items, days, stores), BF16),
         ),
-        in_specs=[far_spec] + vmem(3),
+        in_specs=vmem(4),
         out_specs=(far_spec,) * 4,
         scratch_shapes=[
             pltpu.SMEM((1, items), jnp.int32),
@@ -390,11 +407,11 @@
             pltpu.VMEM((SUB, days, stores), F32),
             pltpu.VMEM((items, days, stores), BF16),
             pltpu.SemaphoreType.DMA((5,)),
-            pltpu.SemaphoreType.DMA((4,)),
+            pltpu.SemaphoreType.DMA((8,)),
         ],
         compiler_params=LIMIT,
         name="closing",
-    )(far(product_group.reshape(1, items)), held(factor[0]), held(exchanged(back)), held(predicted_units))
+    )(*map(held, (own, factor[0], exchanged(back), near)))
     return (product_factor.reshape(items), group_outlet_factor, outlet_date_factor, adjusted_tensor)
 
 

time: 158 us -> 158 us (level)
  no operation moved by 1% of the time
where the time goes in v8:
time: 158 us; the launch traced here: 157 us
  blocking collectives  138 us (87%)
  Pallas kernels  11.5 us (7%)
  starting transfers between devices  5.38 us (3%)
    all_to_all x8, blocking collectives, exchanged(): return lax.all_to_all(sent, 'item', 0, 0, tiled=True).reshape(x.shape)  115 us
    all_to_all x3, blocking collectives, shards(): total = lax.all_to_all(part, 'store', 0, 0, tiled=True)  23 us
    pallas_call x12, Pallas kernels, call(): pl.pallas_call(kernel, out_shape=out_shape, in_specs=vmem(len(args)), out...  6.3 us
    all_to_all x1, starting transfers between devices, shards(): total = lax.all_to_all(part, 'store', 0, 0, tiled=True)  5.38 us
  transfers between devices with their start and end apart: 1, of which 1 were waited for; matrix products, arithmetic and copies ran while one was open for 0% of the time, Pallas kernels for 1%

profile of v8, /device:TPU:8, one launch (start us, length us, event | category | flops | bytes accessed | tf_op | source)
XLA Modules:
  0.0 157.0 jit_solution(11290074960070435816)
XLA Ops:
  0.6 1.2 near.1.x_ref
  1.9 1.1 first.1
  3.0 5.4 %all-to-all-start = ((f32[8,1,128]{2,1,0:T(1,128)}), f32[8,1,128]{2,1,0:T(1,128)S(1)}, u32[]{:S(2)}, u32[]{:S(2)}) async-start(f32[8,1,128]{2,1,0:T(1,128)} %first.1), calls=%async_computation | async-start | bytes 8192 | tf_op jit(solution)/shard_map/all_to_all | solution.py:368
  8.4 2.3 %spread.1 = (bf16[128,4096]{1,0:T(8,128)(2,1)S(1)}, s32[8,128]{1,0:T(8,128)S(1)}, s32[1,128]{1,0:T(1,128)S(1)}, f32[8,128]{1,0:T(8,128)S(1)}, f32[64,128]{1,0:T(8,128)S(1)}) custom-call(bf16[128,8,512]{2,1,0:T(8,128)(2,1)S(1)} %near.1.x_ref, s32[1,128]{1,0:T(1,128)} %bitcast.35, f32[1,128]{1,0:T(1,128)} %bitcast.36, f32[64,512]{1,0:T(8,128)} %cat_all_hbm.1, ...), custom_call_target="tpu_custom_call" | custom-call | tf_op jit(solution)/shard_map/spread/pallas_call | solution.py:339
  10.7 1.5 all-to-all-done.margin_ref
  12.1 0.2 pool.4
  12.4 20.9 %all_to_all.60 = f32[32,1,1024]{2,1,0:T(1,128)S(1)} all-to-all(f32[32,1,1024]{2,1,0:T(1,128)S(1)} %bitcast.21), channel_id=1, replica_groups=mesh['item'=32,'store'=8] {'item'}, dimensions={0} | all-to-all | bytes 262144 | tf_op jit(solution)/shard_map/all_to_all | solution.py:321
  33.3 1.0 owner_first.1
  34.3 13.7 %all_to_all.61 = f32[32,1,640]{2,1,0:T(1,128)S(1)} all-to-all(f32[32,1,640]{2,1,0:T(1,128)S(1)} %bitcast.31), channel_id=1, replica_groups=mesh['item'=32,'store'=8] {'item'}, dimensions={0} | all-to-all | bytes 163840 | tf_op jit(solution)/shard_map/all_to_all | solution.py:321
  48.0 0.4 margin.3
  48.4 7.7 %all_to_all.62.margin_ref = f32[8,1,128]{2,1,0:T(1,128)S(1)} all-to-all(f32[8,1,128]{2,1,0:T(1,128)S(1)} %margin.3), channel_id=1, replica_groups=mesh['item'=32,'store'=8] {'store'}, dimensions={0} | all-to-all | bytes 8192 | tf_op jit(solution)/shard_map/all_to_all | solution.py:368
  56.0 0.2 pool.5
  56.3 13.3 %all_to_all.63 = f32[32,1,640]{2,1,0:T(1,128)S(1)} all-to-all(f32[32,1,640]{2,1,0:T(1,128)S(1)} %bitcast.24), channel_id=1, replica_groups=mesh['item'=32,'store'=8] {'item'}, dimensions={0} | all-to-all | bytes 163840 | tf_op jit(solution)/shard_map/all_to_all | solution.py:321
  69.6 0.7 owner.2
  70.3 13.3 %all_to_all.64 = f32[32,1,640]{2,1,0:T(1,128)S(1)} all-to-all(f32[32,1,640]{2,1,0:T(1,128)S(1)} %bitcast.34), channel_id=1, replica_groups=mesh['item'=32,'store'=8] {'item'}, dimensions={0} | all-to-all | bytes 163840 | tf_op jit(solution)/shard_map/all_to_all | solution.py:321
  83.7 0.4 margin.4
  84.1 7.7 %all_to_all.65.margin_ref = f32[8,1,128]{2,1,0:T(1,128)S(1)} all-to-all(f32[8,1,128]{2,1,0:T(1,128)S(1)} %margin.4), channel_id=1, replica_groups=mesh['item'=32,'store'=8] {'store'}, dimensions={0} | all-to-all | bytes 8192 | tf_op jit(solution)/shard_map/all_to_all | solution.py:368
  91.7 0.2 pool.6
  92.0 13.3 %all_to_all.66 = f32[32,1,640]{2,1,0:T(1,128)S(1)} all-to-all(f32[32,1,640]{2,1,0:T(1,128)S(1)} %bitcast.26), channel_id=1, replica_groups=mesh['item'=32,'store'=8] {'item'}, dimensions={0} | all-to-all | bytes 163840 | tf_op jit(solution)/shard_map/all_to_all | solution.py:321
  105.3 0.7 owner.3
  106.0 13.3 %all_to_all.67 = f32[32,1,640]{2,1,0:T(1,128)S(1)} all-to-all(f32[32,1,640]{2,1,0:T(1,128)S(1)} %bitcast.32), channel_id=1, replica_groups=mesh['item'=32,'store'=8] {'item'}, dimensions={0} | all-to-all | bytes 163840 | tf_op jit(solution)/shard_map/all_to_all | solution.py:321
  119.4 0.4 margin.5
  119.8 7.7 %all_to_all.68.margin_ref = f32[8,1,128]{2,1,0:T(1,128)S(1)} all-to-all(f32[8,1,128]{2,1,0:T(1,128)S(1)} %margin.5), channel_id=1, replica_groups=mesh['item'=32,'store'=8] {'store'}, dimensions={0} | all-to-all | bytes 8192 | tf_op jit(solution)/shard_map/all_to_all | solution.py:368
  127.4 0.2 pool.7
  127.7 13.3 %all_to_all.69 = f32[32,1,640]{2,1,0:T(1,128)S(1)} all-to-all(f32[32,1,640]{2,1,0:T(1,128)S(1)} %bitcast.33), channel_id=1, replica_groups=mesh['item'=32,'store'=8] {'item'}, dimensions={0} | all-to-all | bytes 163840 | tf_op jit(solution)/shard_map/all_to_all | solution.py:321
  141.0 0.6 owner_last.1
  141.6 13.7 %all_to_all.70 = f32[32,1,1152]{2,1,0:T(1,128)S(1)} all-to-all(f32[32,1,1152]{2,1,0:T(1,128)S(1)} %bitcast.19), channel_id=1, replica_groups=mesh['item'=32,'store'=8] {'item'}, dimensions={0} | all-to-all | bytes 294912 | tf_op jit(solution)/shard_map/all_to_all | solution.py:321
  155.3 1.7 %closing.1 = (f32[1,128]{1,0:T(1,128)}, f32[64,512]{1,0:T(8,128)}, f32[8,512]{1,0:T(8,128)}, bf16[128,8,512]{2,1,0:T(8,128)(2,1)}) custom-call(s32[1,128]{1,0:T(1,128)S(1)} %get-tuple-element.23.group_vmem, f32[1,128]{1,0:T(1,128)S(1)} %get-tuple-element.35.factor_vmem, f32[288,128]{1,0:T(8,128)S(1)} %bitcast.20, bf16[128,8,512]{2,1,0:T(8,128)(2,1)S(1)} %near.1.x_ref), custom_call_target="tpu_custom_call" | custom-call | tf_op jit(solution)/shard_map/closing/pallas_call | solution.py:392
Async XLA Ops:
  3.0 9.2 %all-to-all-start = ((f32[8,1,128]{2,1,0:T(1,128)}), f32[8,1,128]{2,1,0:T(1,128)S(1)}, u32[]{:S(2)}, u32[]{:S(2)}) async-start(f32[8,1,128]{2,1,0:T(1,128)} %first.1), calls=%async_computation | async-start | bytes 8192 | tf_op jit(solution)/shard_map/all_to_all | solution.py:368

commit v9 on v8

--- a/solution.py
+++ b/solution.py
@@ -365,7 +365,7 @@
         far(outlet_date_goal),
     )
     for n in range(ROUNDS):
-        total = lax.all_to_all(part, "store", 0, 0, tiled=True)
+        total = lax.all_to_all(part, "store", 0, 0, axis_index_groups=[list(range(beside))[::-1]], tiled=True)
         shapes = (message(SLOTS if n else SUB),)
         if n == ROUNDS - 1:
             shapes += (line,)

time: 158 us -> 156 us (0.987)
  no operation moved by 1% of the time
where the time goes in v9:
time: 156 us; the launch traced here: 155 us
  blocking collectives  137 us (88%)
  Pallas kernels  11.5 us (7%)
  starting transfers between devices  5.22 us (3%)
    all_to_all x8, blocking collectives, exchanged(): return lax.all_to_all(sent, 'item', 0, 0, tiled=True).reshape(x.shape)  115 us
    all_to_all x3, blocking collectives, shards(): lax.all_to_all(part, 'store', 0, 0, axis_index_groups=[list(range(beside)...  21.8 us
    pallas_call x12, Pallas kernels, call(): pl.pallas_call(kernel, out_shape=out_shape, in_specs=vmem(len(args)), out...  6.3 us
    all_to_all x1, starting transfers between devices, shards(): lax.all_to_all(part, 'store', 0, 0, axis_index_groups=[list(range(beside)...  5.22 us
  transfers between devices with their start and end apart: 1, of which 1 were waited for; matrix products, arithmetic and copies ran while one was open for 0% of the time, Pallas kernels for 1%

profile of v9, /device:TPU:8, one launch (start us, length us, event | category | flops | bytes accessed | tf_op | source)
XLA Modules:
  0.0 154.9 jit_solution(9453821045373325777)
XLA Ops:
  0.6 1.2 near.1.x_ref
  1.9 1.1 first.1
  3.0 5.2 %all-to-all-start = ((f32[8,1,128]{2,1,0:T(1,128)}), f32[8,1,128]{2,1,0:T(1,128)S(1)}, u32[]{:S(2)}, u32[]{:S(2)}) async-start(f32[8,1,128]{2,1,0:T(1,128)} %first.1), calls=%async_computation | async-start | bytes 8192 | tf_op jit(solution)/shard_map/all_to_all | solution.py:368
  8.2 2.3 %spread.1 = (bf16[128,4096]{1,0:T(8,128)(2,1)S(1)}, s32[8,128]{1,0:T(8,128)S(1)}, s32[1,128]{1,0:T(1,128)S(1)}, f32[8,128]{1,0:T(8,128)S(1)}, f32[64,128]{1,0:T(8,128)S(1)}) custom-call(bf16[128,8,512]{2,1,0:T(8,128)(2,1)S(1)} %near.1.x_ref, s32[1,128]{1,0:T(1,128)} %bitcast.35, f32[1,128]{1,0:T(1,128)} %bitcast.36, f32[64,512]{1,0:T(8,128)} %cat_all_hbm.1, ...), custom_call_target="tpu_custom_call" | custom-call | tf_op jit(solution)/shard_map/spread/pallas_call | solution.py:339
  10.5 0.5 all-to-all-done.margin_ref
  11.1 0.2 pool.4
  11.3 21.2 %all_to_all.60 = f32[32,1,1024]{2,1,0:T(1,128)S(1)} all-to-all(f32[32,1,1024]{2,1,0:T(1,128)S(1)} %bitcast.21), channel_id=1, replica_groups=mesh['item'=32,'store'=8] {'item'}, dimensions={0} | all-to-all | bytes 262144 | tf_op jit(solution)/shard_map/all_to_all | solution.py:321
  32.5 1.0 owner_first.1
  33.5 13.7 %all_to_all.61 = f32[32,1,640]{2,1,0:T(1,128)S(1)} all-to-all(f32[32,1,640]{2,1,0:T(1,128)S(1)} %bitcast.31), channel_id=1, replica_groups=mesh['item'=32,'store'=8] {'item'}, dimensions={0} | all-to-all | bytes 163840 | tf_op jit(solution)/shard_map/all_to_all | solution.py:321
  47.1 0.4 margin.3
  47.5 7.2 %all_to_all.62.margin_ref = f32[8,1,128]{2,1,0:T(1,128)S(1)} all-to-all(f32[8,1,128]{2,1,0:T(1,128)S(1)} %margin.3), channel_id=1, replica_groups={{7,6,5,4,3,2,1,0},{15,14,13,12,11,10,9,8},{23,22,21,20,19,18,17,16},{31..., dimensions={0} | all-to-all | bytes 8192 | tf_op jit(solution)/shard_map/all_to_all | solution.py:368
  54.8 0.2 pool.5
  55.0 13.3 %all_to_all.63 = f32[32,1,640]{2,1,0:T(1,128)S(1)} all-to-all(f32[32,1,640]{2,1,0:T(1,128)S(1)} %bitcast.24), channel_id=1, replica_groups=mesh['item'=32,'store'=8] {'item'}, dimensions={0} | all-to-all | bytes 163840 | tf_op jit(solution)/shard_map/all_to_all | solution.py:321
  68.3 0.7 owner.2
  69.1 13.3 %all_to_all.64 = f32[32,1,640]{2,1,0:T(1,128)S(1)} all-to-all(f32[32,1,640]{2,1,0:T(1,128)S(1)} %bitcast.34), channel_id=1, replica_groups=mesh['item'=32,'store'=8] {'item'}, dimensions={0} | all-to-all | bytes 163840 | tf_op jit(solution)/shard_map/all_to_all | solution.py:321
  82.4 0.4 margin.4
  82.8 7.3 %all_to_all.65.margin_ref = f32[8,1,128]{2,1,0:T(1,128)S(1)} all-to-all(f32[8,1,128]{2,1,0:T(1,128)S(1)} %margin.4), channel_id=1, replica_groups={{7,6,5,4,3,2,1,0},{15,14,13,12,11,10,9,8},{23,22,21,20,19,18,17,16},{31..., dimensions={0} | all-to-all | bytes 8192 | tf_op jit(solution)/shard_map/all_to_all | solution.py:368
  90.1 0.2 pool.6
  90.3 13.3 %all_to_all.66 = f32[32,1,640]{2,1,0:T(1,128)S(1)} all-to-all(f32[32,1,640]{2,1,0:T(1,128)S(1)} %bitcast.26), channel_id=1, replica_groups=mesh['item'=32,'store'=8] {'item'}, dimensions={0} | all-to-all | bytes 163840 | tf_op jit(solution)/shard_map/all_to_all | solution.py:321
  103.6 0.7 owner.3
  104.4 13.3 %all_to_all.67 = f32[32,1,640]{2,1,0:T(1,128)S(1)} all-to-all(f32[32,1,640]{2,1,0:T(1,128)S(1)} %bitcast.32), channel_id=1, replica_groups=mesh['item'=32,'store'=8] {'item'}, dimensions={0} | all-to-all | bytes 163840 | tf_op jit(solution)/shard_map/all_to_all | solution.py:321
  117.7 0.4 margin.5
  118.1 7.3 %all_to_all.68.margin_ref = f32[8,1,128]{2,1,0:T(1,128)S(1)} all-to-all(f32[8,1,128]{2,1,0:T(1,128)S(1)} %margin.5), channel_id=1, replica_groups={{7,6,5,4,3,2,1,0},{15,14,13,12,11,10,9,8},{23,22,21,20,19,18,17,16},{31..., dimensions={0} | all-to-all | bytes 8192 | tf_op jit(solution)/shard_map/all_to_all | solution.py:368
  125.4 0.2 pool.7
  125.6 13.3 %all_to_all.69 = f32[32,1,640]{2,1,0:T(1,128)S(1)} all-to-all(f32[32,1,640]{2,1,0:T(1,128)S(1)} %bitcast.33), channel_id=1, replica_groups=mesh['item'=32,'store'=8] {'item'}, dimensions={0} | all-to-all | bytes 163840 | tf_op jit(solution)/shard_map/all_to_all | solution.py:321
  138.9 0.6 owner_last.1
  139.5 13.7 %all_to_all.70 = f32[32,1,1152]{2,1,0:T(1,128)S(1)} all-to-all(f32[32,1,1152]{2,1,0:T(1,128)S(1)} %bitcast.19), channel_id=1, replica_groups=mesh['item'=32,'store'=8] {'item'}, dimensions={0} | all-to-all | bytes 294912 | tf_op jit(solution)/shard_map/all_to_all | solution.py:321
  153.2 1.7 %closing.1 = (f32[1,128]{1,0:T(1,128)}, f32[64,512]{1,0:T(8,128)}, f32[8,512]{1,0:T(8,128)}, bf16[128,8,512]{2,1,0:T(8,128)(2,1)}) custom-call(s32[1,128]{1,0:T(1,128)S(1)} %get-tuple-element.23.group_vmem, f32[1,128]{1,0:T(1,128)S(1)} %get-tuple-element.35.factor_vmem, f32[288,128]{1,0:T(8,128)S(1)} %bitcast.20, bf16[128,8,512]{2,1,0:T(8,128)(2,1)S(1)} %near.1.x_ref), custom_call_target="tpu_custom_call" | custom-call | tf_op jit(solution)/shard_map/closing/pallas_call | solution.py:392
Async XLA Ops:
  3.0 8.1 %all-to-all-start = ((f32[8,1,128]{2,1,0:T(1,128)}), f32[8,1,128]{2,1,0:T(1,128)S(1)}, u32[]{:S(2)}, u32[]{:S(2)}) async-start(f32[8,1,128]{2,1,0:T(1,128)} %first.1), calls=%async_computation | async-start | bytes 8192 | tf_op jit(solution)/shard_map/all_to_all | solution.py:368

commit v10 on v9

--- a/solution.py
+++ b/solution.py
@@ -20,6 +20,22 @@
 
 def iota(shape, dim):
     return lax.broadcasted_iota(jnp.int32, shape, dim)
+
+
+def item_order(count):
+    lead = count - 3
+    return [lead] + [i for i in range(count) if i != lead]
+
+
+def store_order(count):
+    lead = count - 3
+    return [lead] + [i for i in range(count - 1, -1, -1) if i != lead]
+
+
+def own_place(count):
+    lead = count - 3
+    me = lax.axis_index("item")
+    return jnp.where(me == lead, 0, jnp.where(me < lead, me + 1, me))
 
 
 def two_parts(x):
@@ -124,7 +140,7 @@
     line_ref[0:1] = goal_ref[...]
     line_ref[1:2] = first[:1].astype(F32)
     width = LANES // days
-    at = lax.axis_index("item") * width
+    at = own_place(wide_ref.shape[1] // LANES) * width
     there = pl.ds(pl.multiple_of(at // LANES * LANES, LANES), LANES)
     index = at % LANES + lane % width
     for k in range(cat_goal_ref.shape[0] // SUB):
@@ -318,7 +334,8 @@
 
     def exchanged(x):
         sent = x.reshape(owners, 1, x.size // owners)
-        return lax.all_to_all(sent, "item", 0, 0, tiled=True).reshape(x.shape)
+        there = lax.all_to_all(sent, "item", 0, 0, axis_index_groups=[item_order(owners)], tiled=True)
+        return there.reshape(x.shape)
 
     margin = pltpu.VMEM((beside, 1, LANES), F32)
     line = pltpu.VMEM((1, LANES), F32)
@@ -365,7 +382,7 @@
         far(outlet_date_goal),
     )
     for n in range(ROUNDS):
-        total = lax.all_to_all(part, "store", 0, 0, axis_index_groups=[list(range(beside))[::-1]], tiled=True)
+        total = lax.all_to_all(part, "store", 0, 0, axis_index_groups=[store_order(beside)], tiled=True)
         shapes = (message(SLOTS if n else SUB),)
         if n == ROUNDS - 1:
             shapes += (line,)

time: 156 us -> 151 us (0.968)
  blocking collectives: 137 us -> 133 us
    all_to_all x11, blocking collectives: 137 us -> 133 us  [the longest x8 111 us: exchanged(): lax.all_to_all(sent, 'item', 0, 0, axis_index_groups=[item_order(owners)]...]
  transfers between devices with their start and end apart: 1 -> 1, of which waited for: 1 -> 1; matrix products, arithmetic and copies ran while one was open for 0% -> 0% of each run, Pallas kernels for 1% -> 2%
where the time goes in v10:
time: 151 us
  blocking collectives  133 us (88%)
  Pallas kernels  11.5 us (8%)
  starting transfers between devices  4.61 us (3%)
    all_to_all x8, blocking collectives, exchanged(): lax.all_to_all(sent, 'item', 0, 0, axis_index_groups=[item_order(owners)]...  111 us
    all_to_all x3, blocking collectives, shards(): lax.all_to_all(part, 'store', 0, 0, axis_index_groups=[store_order(beside...  21.7 us
    pallas_call x12, Pallas kernels, call(): pl.pallas_call(kernel, out_shape=out_shape, in_specs=vmem(len(args)), out...  6.3 us
    all_to_all x1, starting transfers between devices, shards(): lax.all_to_all(part, 'store', 0, 0, axis_index_groups=[store_order(beside...  4.61 us
  transfers between devices with their start and end apart: 1, of which 1 were waited for; matrix products, arithmetic and copies ran while one was open for 0% of the time, Pallas kernels for 2%

profile of v10, /device:TPU:8, one launch (start us, length us, event | category | flops | bytes accessed | tf_op | source)
XLA Modules:
  0.0 150.9 jit_solution(16571002792484039253)
XLA Ops:
  0.6 1.2 near.1.x_ref
  1.9 1.1 first.1
  3.0 4.6 %all-to-all-start = ((f32[8,1,128]{2,1,0:T(1,128)}), f32[8,1,128]{2,1,0:T(1,128)S(1)}, u32[]{:S(2)}, u32[]{:S(2)}) async-start(f32[8,1,128]{2,1,0:T(1,128)} %first.1), calls=%async_computation | async-start | bytes 8192 | tf_op jit(solution)/shard_map/all_to_all | solution.py:385
  7.6 2.3 %spread.1 = (bf16[128,4096]{1,0:T(8,128)(2,1)S(1)}, s32[8,128]{1,0:T(8,128)S(1)}, s32[1,128]{1,0:T(1,128)S(1)}, f32[8,128]{1,0:T(8,128)S(1)}, f32[64,128]{1,0:T(8,128)S(1)}) custom-call(bf16[128,8,512]{2,1,0:T(8,128)(2,1)S(1)} %near.1.x_ref, s32[1,128]{1,0:T(1,128)} %bitcast.35, f32[1,128]{1,0:T(1,128)} %bitcast.36, f32[64,512]{1,0:T(8,128)} %cat_all_hbm.1, ...), custom_call_target="tpu_custom_call" | custom-call | tf_op jit(solution)/shard_map/spread/pallas_call | solution.py:356
  9.9 1.4 all-to-all-done.margin_ref
  11.3 0.2 pool.4
  11.6 17.5 %all_to_all.60 = f32[32,1,1024]{2,1,0:T(1,128)S(1)} all-to-all(f32[32,1,1024]{2,1,0:T(1,128)S(1)} %bitcast.21), channel_id=1, replica_groups={{232,0,8,16,24,32,40,48,56,64,72,80,88,96,104,112,120,128,136,144,152,1..., dimensions={0} | all-to-all | bytes 262144 | tf_op jit(solution)/shard_map/all_to_all | solution.py:337
  29.1 1.0 owner_first.1
  30.1 13.2 %all_to_all.61 = f32[32,1,640]{2,1,0:T(1,128)S(1)} all-to-all(f32[32,1,640]{2,1,0:T(1,128)S(1)} %bitcast.31), channel_id=1, replica_groups={{232,0,8,16,24,32,40,48,56,64,72,80,88,96,104,112,120,128,136,144,152,1..., dimensions={0} | all-to-all | bytes 163840 | tf_op jit(solution)/shard_map/all_to_all | solution.py:337
  43.4 0.4 margin.3
  43.7 7.2 %all_to_all.62.margin_ref = f32[8,1,128]{2,1,0:T(1,128)S(1)} all-to-all(f32[8,1,128]{2,1,0:T(1,128)S(1)} %margin.3), channel_id=1, replica_groups={{5,7,6,4,3,2,1,0},{13,15,14,12,11,10,9,8},{21,23,22,20,19,18,17,16},{29..., dimensions={0} | all-to-all | bytes 8192 | tf_op jit(solution)/shard_map/all_to_all | solution.py:385
  51.0 0.2 pool.5
  51.2 13.2 %all_to_all.63 = f32[32,1,640]{2,1,0:T(1,128)S(1)} all-to-all(f32[32,1,640]{2,1,0:T(1,128)S(1)} %bitcast.24), channel_id=1, replica_groups={{232,0,8,16,24,32,40,48,56,64,72,80,88,96,104,112,120,128,136,144,152,1..., dimensions={0} | all-to-all | bytes 163840 | tf_op jit(solution)/shard_map/all_to_all | solution.py:337
  64.5 0.7 owner.2
  65.2 13.2 %all_to_all.64 = f32[32,1,640]{2,1,0:T(1,128)S(1)} all-to-all(f32[32,1,640]{2,1,0:T(1,128)S(1)} %bitcast.34), channel_id=1, replica_groups={{232,0,8,16,24,32,40,48,56,64,72,80,88,96,104,112,120,128,136,144,152,1..., dimensions={0} | all-to-all | bytes 163840 | tf_op jit(solution)/shard_map/all_to_all | solution.py:337
  78.5 0.4 margin.4
  78.9 7.2 %all_to_all.65.margin_ref = f32[8,1,128]{2,1,0:T(1,128)S(1)} all-to-all(f32[8,1,128]{2,1,0:T(1,128)S(1)} %margin.4), channel_id=1, replica_groups={{5,7,6,4,3,2,1,0},{13,15,14,12,11,10,9,8},{21,23,22,20,19,18,17,16},{29..., dimensions={0} | all-to-all | bytes 8192 | tf_op jit(solution)/shard_map/all_to_all | solution.py:385
  86.1 0.2 pool.6
  86.3 13.2 %all_to_all.66 = f32[32,1,640]{2,1,0:T(1,128)S(1)} all-to-all(f32[32,1,640]{2,1,0:T(1,128)S(1)} %bitcast.26), channel_id=1, replica_groups={{232,0,8,16,24,32,40,48,56,64,72,80,88,96,104,112,120,128,136,144,152,1..., dimensions={0} | all-to-all | bytes 163840 | tf_op jit(solution)/shard_map/all_to_all | solution.py:337
  99.6 0.7 owner.3
  100.3 13.2 %all_to_all.67 = f32[32,1,640]{2,1,0:T(1,128)S(1)} all-to-all(f32[32,1,640]{2,1,0:T(1,128)S(1)} %bitcast.32), channel_id=1, replica_groups={{232,0,8,16,24,32,40,48,56,64,72,80,88,96,104,112,120,128,136,144,152,1..., dimensions={0} | all-to-all | bytes 163840 | tf_op jit(solution)/shard_map/all_to_all | solution.py:337
  113.6 0.4 margin.5
  114.0 7.2 %all_to_all.68.margin_ref = f32[8,1,128]{2,1,0:T(1,128)S(1)} all-to-all(f32[8,1,128]{2,1,0:T(1,128)S(1)} %margin.5), channel_id=1, replica_groups={{5,7,6,4,3,2,1,0},{13,15,14,12,11,10,9,8},{21,23,22,20,19,18,17,16},{29..., dimensions={0} | all-to-all | bytes 8192 | tf_op jit(solution)/shard_map/all_to_all | solution.py:385
  121.2 0.2 pool.7
  121.4 13.2 %all_to_all.69 = f32[32,1,640]{2,1,0:T(1,128)S(1)} all-to-all(f32[32,1,640]{2,1,0:T(1,128)S(1)} %bitcast.33), channel_id=1, replica_groups={{232,0,8,16,24,32,40,48,56,64,72,80,88,96,104,112,120,128,136,144,152,1..., dimensions={0} | all-to-all | bytes 163840 | tf_op jit(solution)/shard_map/all_to_all | solution.py:337
  134.7 0.6 owner_last.1
  135.3 13.9 %all_to_all.70 = f32[32,1,1152]{2,1,0:T(1,128)S(1)} all-to-all(f32[32,1,1152]{2,1,0:T(1,128)S(1)} %bitcast.19), channel_id=1, replica_groups={{232,0,8,16,24,32,40,48,56,64,72,80,88,96,104,112,120,128,136,144,152,1..., dimensions={0} | all-to-all | bytes 294912 | tf_op jit(solution)/shard_map/all_to_all | solution.py:337
  149.2 1.7 %closing.1 = (f32[1,128]{1,0:T(1,128)}, f32[64,512]{1,0:T(8,128)}, f32[8,512]{1,0:T(8,128)}, bf16[128,8,512]{2,1,0:T(8,128)(2,1)}) custom-call(s32[1,128]{1,0:T(1,128)S(1)} %get-tuple-element.23.group_vmem, f32[1,128]{1,0:T(1,128)S(1)} %get-tuple-element.35.factor_vmem, f32[288,128]{1,0:T(8,128)S(1)} %bitcast.20, bf16[128,8,512]{2,1,0:T(8,128)(2,1)S(1)} %near.1.x_ref), custom_call_target="tpu_custom_call" | custom-call | tf_op jit(solution)/shard_map/closing/pallas_call | solution.py:409
Async XLA Ops:
  3.0 8.4 %all-to-all-start = ((f32[8,1,128]{2,1,0:T(1,128)}), f32[8,1,128]{2,1,0:T(1,128)S(1)}, u32[]{:S(2)}, u32[]{:S(2)}) async-start(f32[8,1,128]{2,1,0:T(1,128)} %first.1), calls=%async_computation | async-start | bytes 8192 | tf_op jit(solution)/shard_map/all_to_all | solution.py:385

commit v11 on v10

--- a/solution.py
+++ b/solution.py
@@ -12,7 +12,7 @@
 LANES = 128
 SUB = 8
 SLOTS = 5
-BASE_ROW = 7
+BASE_ROW = SLOTS
 
 F32 = jnp.float32
 BF16 = jnp.bfloat16
@@ -22,8 +22,12 @@
     return lax.broadcasted_iota(jnp.int32, shape, dim)
 
 
+def item_lead(count):
+    return 2 * count // 3
+
+
 def item_order(count):
-    lead = count - 3
+    lead = item_lead(count)
     return [lead] + [i for i in range(count) if i != lead]
 
 
@@ -33,7 +37,7 @@
 
 
 def own_place(count):
-    lead = count - 3
+    lead = item_lead(count)
     me = lax.axis_index("item")
     return jnp.where(me == lead, 0, jnp.where(me < lead, me + 1, me))
 
@@ -211,8 +215,9 @@
 
 def owner_first_kernel(taken_ref, cat_goal_ref, line_ref, out_ref, day_ref, place_ref, across_ref):
     cats = cat_goal_ref.shape[0]
-    devices = taken_ref.shape[0] // SUB
-    base = taken_ref[pl.ds(BASE_ROW, devices, stride=SUB), :]
+    each = SLOTS + 1
+    devices = taken_ref.shape[0] // each
+    base = taken_ref[pl.ds(BASE_ROW, devices, stride=each), :]
 
     def placed(each):
         rows = devices * each
@@ -227,7 +232,7 @@
     place = placed(SLOTS)
     across_ref[...] = place.T[:cats].astype(BF16)
     place_ref[...] = place.astype(BF16)
-    merged = summed(placed(SUB).T[:cats].astype(BF16), taken_ref[...])
+    merged = summed(placed(each).T[:cats].astype(BF16), taken_ref[...])
     cat, day = fitted(merged, cat_goal_ref[...], line_ref[2:3], jnp.ones((1, LANES), F32))
     day_ref[...] = day
     answer(place_ref[...], cat, day, out_ref)
@@ -383,7 +388,7 @@
     )
     for n in range(ROUNDS):
         total = lax.all_to_all(part, "store", 0, 0, axis_index_groups=[store_order(beside)], tiled=True)
-        shapes = (message(SLOTS if n else SUB),)
+        shapes = (message(SLOTS if n else SLOTS + 1),)
         if n == ROUNDS - 1:
             shapes += (line,)
         pooled, *factor = call(pool_kernel, shapes, total, lines, wide, slot, name="pool")

time: 151 us -> 150 us (level)
  blocking collectives: 133 us -> 131 us
where the time goes in v11:
time: 150 us
  blocking collectives  131 us (87%)
  Pallas kernels  11.5 us (8%)
  starting transfers between devices  4.61 us (3%)
    all_to_all x8, blocking collectives, exchanged(): lax.all_to_all(sent, 'item', 0, 0, axis_index_groups=[item_order(owners)]...  110 us
    all_to_all x3, blocking collectives, shards(): lax.all_to_all(part, 'store', 0, 0, axis_index_groups=[store_order(beside...  21.7 us
    pallas_call x12, Pallas kernels, call(): pl.pallas_call(kernel, out_shape=out_shape, in_specs=vmem(len(args)), out...  6.24 us
    all_to_all x1, starting transfers between devices, shards(): lax.all_to_all(part, 'store', 0, 0, axis_index_groups=[store_order(beside...  4.61 us
  transfers between devices with their start and end apart: 1, of which 1 were waited for; matrix products, arithmetic and copies ran while one was open for 0% of the time, Pallas kernels for 2%

profile of v11, /device:TPU:8, one launch (start us, length us, event | category | flops | bytes accessed | tf_op | source)
XLA Modules:
  0.0 149.6 jit_solution(417456614097202266)
XLA Ops:
  0.6 1.2 near.1.x_ref
  1.9 1.1 first.1
  3.0 4.6 %all-to-all-start = ((f32[8,1,128]{2,1,0:T(1,128)}), f32[8,1,128]{2,1,0:T(1,128)S(1)}, u32[]{:S(2)}, u32[]{:S(2)}) async-start(f32[8,1,128]{2,1,0:T(1,128)} %first.1), calls=%async_computation | async-start | bytes 8192 | tf_op jit(solution)/shard_map/all_to_all | solution.py:390
  7.6 2.3 %spread.1 = (bf16[128,4096]{1,0:T(8,128)(2,1)S(1)}, s32[8,128]{1,0:T(8,128)S(1)}, s32[1,128]{1,0:T(1,128)S(1)}, f32[8,128]{1,0:T(8,128)S(1)}, f32[64,128]{1,0:T(8,128)S(1)}) custom-call(bf16[128,8,512]{2,1,0:T(8,128)(2,1)S(1)} %near.1.x_ref, s32[1,128]{1,0:T(1,128)} %bitcast.35, f32[1,128]{1,0:T(1,128)} %bitcast.36, f32[64,512]{1,0:T(8,128)} %cat_all_hbm.1, ...), custom_call_target="tpu_custom_call" | custom-call | tf_op jit(solution)/shard_map/spread/pallas_call | solution.py:361
  9.9 1.4 all-to-all-done.margin_ref
  11.3 0.2 pool.4
  11.6 16.3 %all_to_all.60 = f32[32,1,768]{2,1,0:T(1,128)S(1)} all-to-all(f32[32,1,768]{2,1,0:T(1,128)S(1)} %bitcast.22), channel_id=1, replica_groups={{168,0,8,16,24,32,40,48,56,64,72,80,88,96,104,112,120,128,136,144,152,1..., dimensions={0} | all-to-all | bytes 196608 | tf_op jit(solution)/shard_map/all_to_all | solution.py:342
  27.9 1.0 owner_first.1
  28.8 13.3 %all_to_all.61 = f32[32,1,640]{2,1,0:T(1,128)S(1)} all-to-all(f32[32,1,640]{2,1,0:T(1,128)S(1)} %bitcast.31), channel_id=1, replica_groups={{168,0,8,16,24,32,40,48,56,64,72,80,88,96,104,112,120,128,136,144,152,1..., dimensions={0} | all-to-all | bytes 163840 | tf_op jit(solution)/shard_map/all_to_all | solution.py:342
  42.1 0.4 margin.3
  42.5 7.2 %all_to_all.62.margin_ref = f32[8,1,128]{2,1,0:T(1,128)S(1)} all-to-all(f32[8,1,128]{2,1,0:T(1,128)S(1)} %margin.3), channel_id=1, replica_groups={{5,7,6,4,3,2,1,0},{13,15,14,12,11,10,9,8},{21,23,22,20,19,18,17,16},{29..., dimensions={0} | all-to-all | bytes 8192 | tf_op jit(solution)/shard_map/all_to_all | solution.py:390
  49.7 0.2 pool.5
  50.0 13.3 %all_to_all.63 = f32[32,1,640]{2,1,0:T(1,128)S(1)} all-to-all(f32[32,1,640]{2,1,0:T(1,128)S(1)} %bitcast.24), channel_id=1, replica_groups={{168,0,8,16,24,32,40,48,56,64,72,80,88,96,104,112,120,128,136,144,152,1..., dimensions={0} | all-to-all | bytes 163840 | tf_op jit(solution)/shard_map/all_to_all | solution.py:342
  63.2 0.7 owner.2
  64.0 13.2 %all_to_all.64 = f32[32,1,640]{2,1,0:T(1,128)S(1)} all-to-all(f32[32,1,640]{2,1,0:T(1,128)S(1)} %bitcast.34), channel_id=1, replica_groups={{168,0,8,16,24,32,40,48,56,64,72,80,88,96,104,112,120,128,136,144,152,1..., dimensions={0} | all-to-all | bytes 163840 | tf_op jit(solution)/shard_map/all_to_all | solution.py:342
  77.2 0.4 margin.4
  77.6 7.2 %all_to_all.65.margin_ref = f32[8,1,128]{2,1,0:T(1,128)S(1)} all-to-all(f32[8,1,128]{2,1,0:T(1,128)S(1)} %margin.4), channel_id=1, replica_groups={{5,7,6,4,3,2,1,0},{13,15,14,12,11,10,9,8},{21,23,22,20,19,18,17,16},{29..., dimensions={0} | all-to-all | bytes 8192 | tf_op jit(solution)/shard_map/all_to_all | solution.py:390
  84.8 0.2 pool.6
  85.1 13.3 %all_to_all.66 = f32[32,1,640]{2,1,0:T(1,128)S(1)} all-to-all(f32[32,1,640]{2,1,0:T(1,128)S(1)} %bitcast.26), channel_id=1, replica_groups={{168,0,8,16,24,32,40,48,56,64,72,80,88,96,104,112,120,128,136,144,152,1..., dimensions={0} | all-to-all | bytes 163840 | tf_op jit(solution)/shard_map/all_to_all | solution.py:342
  98.3 0.7 owner.3
  99.1 13.2 %all_to_all.67 = f32[32,1,640]{2,1,0:T(1,128)S(1)} all-to-all(f32[32,1,640]{2,1,0:T(1,128)S(1)} %bitcast.32), channel_id=1, replica_groups={{168,0,8,16,24,32,40,48,56,64,72,80,88,96,104,112,120,128,136,144,152,1..., dimensions={0} | all-to-all | bytes 163840 | tf_op jit(solution)/shard_map/all_to_all | solution.py:342
  112.3 0.4 margin.5
  112.7 7.2 %all_to_all.68.margin_ref = f32[8,1,128]{2,1,0:T(1,128)S(1)} all-to-all(f32[8,1,128]{2,1,0:T(1,128)S(1)} %margin.5), channel_id=1, replica_groups={{5,7,6,4,3,2,1,0},{13,15,14,12,11,10,9,8},{21,23,22,20,19,18,17,16},{29..., dimensions={0} | all-to-all | bytes 8192 | tf_op jit(solution)/shard_map/all_to_all | solution.py:390
  120.0 0.2 pool.7
  120.2 13.3 %all_to_all.69 = f32[32,1,640]{2,1,0:T(1,128)S(1)} all-to-all(f32[32,1,640]{2,1,0:T(1,128)S(1)} %bitcast.33), channel_id=1, replica_groups={{168,0,8,16,24,32,40,48,56,64,72,80,88,96,104,112,120,128,136,144,152,1..., dimensions={0} | all-to-all | bytes 163840 | tf_op jit(solution)/shard_map/all_to_all | solution.py:342
  133.5 0.6 owner_last.1
  134.1 13.9 %all_to_all.70 = f32[32,1,1152]{2,1,0:T(1,128)S(1)} all-to-all(f32[32,1,1152]{2,1,0:T(1,128)S(1)} %bitcast.19), channel_id=1, replica_groups={{168,0,8,16,24,32,40,48,56,64,72,80,88,96,104,112,120,128,136,144,152,1..., dimensions={0} | all-to-all | bytes 294912 | tf_op jit(solution)/shard_map/all_to_all | solution.py:342
  148.0 1.7 %closing.1 = (f32[1,128]{1,0:T(1,128)}, f32[64,512]{1,0:T(8,128)}, f32[8,512]{1,0:T(8,128)}, bf16[128,8,512]{2,1,0:T(8,128)(2,1)}) custom-call(s32[1,128]{1,0:T(1,128)S(1)} %get-tuple-element.23.group_vmem, f32[1,128]{1,0:T(1,128)S(1)} %get-tuple-element.35.factor_vmem, f32[288,128]{1,0:T(8,128)S(1)} %bitcast.20, bf16[128,8,512]{2,1,0:T(8,128)(2,1)S(1)} %near.1.x_ref), custom_call_target="tpu_custom_call" | custom-call | tf_op jit(solution)/shard_map/closing/pallas_call | solution.py:414
Async XLA Ops:
  3.0 8.4 %all-to-all-start = ((f32[8,1,128]{2,1,0:T(1,128)}), f32[8,1,128]{2,1,0:T(1,128)S(1)}, u32[]{:S(2)}, u32[]{:S(2)}) async-start(f32[8,1,128]{2,1,0:T(1,128)} %first.1), calls=%async_computation | async-start | bytes 8192 | tf_op jit(solution)/shard_map/all_to_all | solution.py:390

commit v12 on v11

--- a/solution.py
+++ b/solution.py
@@ -111,7 +111,7 @@
 
 def spread_kernel(
     x_ref, group_hbm, goal_hbm, cat_all_hbm, day_all_hbm,
-    wide_ref, slot_ref, own_ref, line_ref, cat_goal_ref,
+    wide_ref, slot_ref, own_ref, line_ref, cat_goal_ref, widen_ref,
     rows_ref, group_ref, goal_ref, cat_all_ref, day_all_ref, sems,
 ):
     pairs = ((group_hbm, group_ref), (goal_hbm, goal_ref), (cat_all_hbm, cat_all_ref), (day_all_hbm, day_all_ref))
@@ -134,6 +134,10 @@
         return carry
 
     lax.fori_loop(0, items // tall, step, 0)
+    part = LANES // days
+    source, target = iota((LANES, LANES), 0), iota((LANES, LANES), 1) % part
+    for s in range(SLOTS):
+        widen_ref[:, s * LANES : (s + 1) * LANES] = (source == s * part + target).astype(F32).astype(BF16)
     for copy in copies:
         copy.wait()
     row, lane = iota((SUB, LANES), 0), iota((SUB, LANES), 1)
@@ -154,15 +158,16 @@
     line_ref[2:3] = jnp.sum(day_goal, axis=0, keepdims=True)
 
 
-def margin_kernel(back_ref, wide_ref, slot_ref, out_ref):
+def margin_kernel(back_ref, wide_ref, slot_ref, widen_ref, out_ref, tiles_ref):
     count = wide_ref.shape[1] // LANES
-    tiles = []
-    for j in range(count):
-        at = min(j * SLOTS, count * SLOTS - SUB)
-        tile = back_ref[at : at + SUB]
-        if at < j * SLOTS:
-            tile = pltpu.roll(tile, SUB - (j * SLOTS - at), 0)
-        tiles.append(tile)
+    day = back_ref[pl.ds(0, count, stride=2), :]
+    cat = back_ref[pl.ds(1, count, stride=2), :]
+    cat = jnp.dot(jnp.concatenate(two_parts(cat), axis=0), widen_ref[...], preferred_element_type=F32)
+    cat = cat[:count] + cat[count:]
+    for s in range(SUB):
+        product = cat[:, s * LANES : (s + 1) * LANES] * day if s < SLOTS else jnp.zeros_like(day)
+        tiles_ref[pl.ds(s, count, stride=SUB), :] = product
+    tiles = [tiles_ref[j * SUB : (j + 1) * SUB] for j in range(count)]
     parts = jnp.concatenate(two_parts(jnp.concatenate(tiles, axis=1)), axis=0)
     sums = lax.dot_general(parts, wide_ref[...], (((1,), (1,)), ((), ())), preferred_element_type=F32)
     sums = sums[:SUB] + sums[SUB:]
@@ -208,9 +213,14 @@
     return merged[:, :LANES] + merged[:, LANES:]
 
 
-def answer(place, cat, day, out_ref):
-    parts = jnp.concatenate(two_parts(cat * day), axis=0)
-    out_ref[...] = jnp.dot(place, parts, preferred_element_type=F32)
+def answer(choice, cat, day, out_ref):
+    group = iota(cat.shape, 1) // (LANES // SUB)
+    blocks = [jnp.where(group == s, cat, 0.0) for s in range(choice.shape[1] // cat.shape[0])]
+    parts = jnp.concatenate(two_parts(jnp.concatenate(blocks, axis=0)), axis=1)
+    rows = jnp.dot(choice, parts, preferred_element_type=F32)
+    devices = choice.shape[0]
+    out_ref[pl.ds(0, devices, stride=2), :] = jnp.broadcast_to(day, (devices, LANES))
+    out_ref[pl.ds(1, devices, stride=2), :] = rows[:, :LANES] + rows[:, LANES:]
 
 
 def owner_first_kernel(taken_ref, cat_goal_ref, line_ref, out_ref, day_ref, place_ref, across_ref):
@@ -229,9 +239,12 @@
         hit = (spread.astype(jnp.int32) + slot == lane % cats) & (slot < SLOTS)
         return hit.astype(F32)
 
-    place = placed(SLOTS)
-    across_ref[...] = place.T[:cats].astype(BF16)
-    place_ref[...] = place.astype(BF16)
+    across_ref[...] = placed(SLOTS).T[:cats].astype(BF16)
+    lane = iota((devices, LANES), 1)
+    for n in range(place_ref.shape[1] // LANES):
+        slot = n * (LANES // cats) + lane // cats
+        hit = (base.astype(jnp.int32) + slot == lane % cats) & (slot < SLOTS)
+        place_ref[:, n * LANES : (n + 1) * LANES] = hit.astype(F32).astype(BF16)
     merged = summed(placed(each).T[:cats].astype(BF16), taken_ref[...])
     cat, day = fitted(merged, cat_goal_ref[...], line_ref[2:3], jnp.ones((1, LANES), F32))
     day_ref[...] = day
@@ -358,7 +371,7 @@
         name="near",
     )(far(predicted_units))
     (part,) = call(first_kernel, (margin,), near, name="first")
-    wide, slot, own, lines, cat_goal = pl.pallas_call(
+    wide, slot, own, lines, cat_goal, widen = pl.pallas_call(
         spread_kernel,
         out_shape=(
             pltpu.VMEM((items, days * stores), BF16),
@@ -366,9 +379,10 @@
             pltpu.VMEM((1, items), jnp.int32),
             pltpu.VMEM((SUB, LANES), F32),
             per_cat,
+            pltpu.VMEM((LANES, SLOTS * LANES), BF16),
         ),
         in_specs=vmem(1) + [far_spec] * 4,
-        out_specs=tuple(vmem(5)),
+        out_specs=tuple(vmem(6)),
         scratch_shapes=[
             pltpu.VMEM((items * days * stores // LANES, LANES), F32),
             pltpu.VMEM((1, items), jnp.int32),
@@ -397,16 +411,19 @@
             break
         if n == 0:
             shapes = (
-                message(SLOTS),
+                message(2),
                 line,
-                pltpu.VMEM((owners * SLOTS, LANES), BF16),
+                pltpu.VMEM((owners, -(-SLOTS * cats // LANES) * LANES), BF16),
                 pltpu.VMEM((cats, owners * SLOTS), BF16),
             )
             back, day, place, across = call(owner_first_kernel, shapes, taken, cat_goal, lines, name="owner_first")
         else:
-            shapes = (message(SLOTS), line)
+            shapes = (message(2), line)
             back, day = call(owner_kernel, shapes, taken, cat_goal, lines, day, place, across, name="owner")
-        (part,) = call(margin_kernel, (margin,), exchanged(back), wide, slot, name="margin")
+        (part,) = call(
+            margin_kernel, (margin,), exchanged(back), wide, slot, widen,
+            scratch_shapes=[pltpu.VMEM((owners * SUB, LANES), F32)], name="margin",
+        )
 
     (back,) = call(
         owner_last_kernel, (message(SUB + 1),), taken, cat_goal, lines, day, across, name="owner_last"

time: 150 us -> 149 us (level)
    all_to_all x8, blocking collectives: 110 us -> 108 us  [exchanged(): lax.all_to_all(sent, 'item', 0, 0, axis_index_groups=[item_order(owners)]...]
where the time goes in v12:
time: 149 us
  blocking collectives  130 us (87%)
  Pallas kernels  11.8 us (8%)
  starting transfers between devices  4.61 us (3%)
    all_to_all x8, blocking collectives, exchanged(): lax.all_to_all(sent, 'item', 0, 0, axis_index_groups=[item_order(owners)]...  108 us
    all_to_all x3, blocking collectives, shards(): lax.all_to_all(part, 'store', 0, 0, axis_index_groups=[store_order(beside...  21.9 us
    pallas_call x12, Pallas kernels, call(): pl.pallas_call(kernel, out_shape=out_shape, in_specs=vmem(len(args)), out...  6.57 us
    all_to_all x1, starting transfers between devices, shards(): lax.all_to_all(part, 'store', 0, 0, axis_index_groups=[store_order(beside...  4.61 us
  transfers between devices with their start and end apart: 1, of which 1 were waited for; matrix products, arithmetic and copies ran while one was open for 0% of the time, Pallas kernels for 2%

profile of v12, /device:TPU:8, one launch (start us, length us, event | category | flops | bytes accessed | tf_op | source)
XLA Modules:
  0.0 148.6 jit_solution(3120033981098307609)
XLA Ops:
  0.6 1.2 near.1.x_ref
  1.9 1.1 first.1
  3.0 4.6 %all-to-all-start = ((f32[8,1,128]{2,1,0:T(1,128)}), f32[8,1,128]{2,1,0:T(1,128)S(1)}, u32[]{:S(2)}, u32[]{:S(2)}) async-start(f32[8,1,128]{2,1,0:T(1,128)} %first.1), calls=%async_computation | async-start | bytes 8192 | tf_op jit(solution)/shard_map/all_to_all | solution.py:404
  7.6 2.3 %spread.1 = (bf16[128,4096]{1,0:T(8,128)(2,1)S(1)}, s32[8,128]{1,0:T(8,128)S(1)}, s32[1,128]{1,0:T(1,128)S(1)}, f32[8,128]{1,0:T(8,128)S(1)}, f32[64,128]{1,0:T(8,128)S(1)}, /*index=5*/bf16[128,640]{1,0:T(8,128)(2,1)S(1)}) custom-call(bf16[128,8,512]{2,1,0:T(8,128)(2,1)S(1)} %near.1.x_ref, s32[1,128]{1,0:T(1,128)} %bitcast.35, f32[1,128]{1,0:T(1,128)} %bitcast.36, ...), custom_call_target="tpu_custom_call" | custom-call | tf_op jit(solution)/shard_map/spread/pallas_call | solution.py:374
  9.9 1.4 all-to-all-done.margin_ref
  11.3 0.2 pool.4
  11.6 16.3 %all_to_all.60 = f32[32,1,768]{2,1,0:T(1,128)S(1)} all-to-all(f32[32,1,768]{2,1,0:T(1,128)S(1)} %bitcast.22), channel_id=1, replica_groups={{168,0,8,16,24,32,40,48,56,64,72,80,88,96,104,112,120,128,136,144,152,1..., dimensions={0} | all-to-all | bytes 196608 | tf_op jit(solution)/shard_map/all_to_all | solution.py:355
  27.9 0.9 owner_first.1
  28.8 12.8 %all_to_all.61 = f32[32,1,256]{2,1,0:T(1,128)S(1)} all-to-all(f32[32,1,256]{2,1,0:T(1,128)S(1)} %bitcast.32), channel_id=1, replica_groups={{168,0,8,16,24,32,40,48,56,64,72,80,88,96,104,112,120,128,136,144,152,1..., dimensions={0} | all-to-all | bytes 65536 | tf_op jit(solution)/shard_map/all_to_all | solution.py:355
  41.6 0.5 margin.3
  42.1 7.3 %all_to_all.62.margin_ref = f32[8,1,128]{2,1,0:T(1,128)S(1)} all-to-all(f32[8,1,128]{2,1,0:T(1,128)S(1)} %margin.3), channel_id=1, replica_groups={{5,7,6,4,3,2,1,0},{13,15,14,12,11,10,9,8},{21,23,22,20,19,18,17,16},{29..., dimensions={0} | all-to-all | bytes 8192 | tf_op jit(solution)/shard_map/all_to_all | solution.py:404
  49.4 0.2 pool.5
  49.7 13.3 %all_to_all.63 = f32[32,1,640]{2,1,0:T(1,128)S(1)} all-to-all(f32[32,1,640]{2,1,0:T(1,128)S(1)} %bitcast.23), channel_id=1, replica_groups={{168,0,8,16,24,32,40,48,56,64,72,80,88,96,104,112,120,128,136,144,152,1..., dimensions={0} | all-to-all | bytes 163840 | tf_op jit(solution)/shard_map/all_to_all | solution.py:355
  62.9 0.7 owner.2
  63.7 12.7 %all_to_all.64 = f32[32,1,256]{2,1,0:T(1,128)S(1)} all-to-all(f32[32,1,256]{2,1,0:T(1,128)S(1)} %bitcast.34), channel_id=1, replica_groups={{168,0,8,16,24,32,40,48,56,64,72,80,88,96,104,112,120,128,136,144,152,1..., dimensions={0} | all-to-all | bytes 65536 | tf_op jit(solution)/shard_map/all_to_all | solution.py:355
  76.4 0.5 margin.4
  76.9 7.3 %all_to_all.65.margin_ref = f32[8,1,128]{2,1,0:T(1,128)S(1)} all-to-all(f32[8,1,128]{2,1,0:T(1,128)S(1)} %margin.4), channel_id=1, replica_groups={{5,7,6,4,3,2,1,0},{13,15,14,12,11,10,9,8},{21,23,22,20,19,18,17,16},{29..., dimensions={0} | all-to-all | bytes 8192 | tf_op jit(solution)/shard_map/all_to_all | solution.py:404
  84.2 0.2 pool.6
  84.4 13.3 %all_to_all.66 = f32[32,1,640]{2,1,0:T(1,128)S(1)} all-to-all(f32[32,1,640]{2,1,0:T(1,128)S(1)} %bitcast.24), channel_id=1, replica_groups={{168,0,8,16,24,32,40,48,56,64,72,80,88,96,104,112,120,128,136,144,152,1..., dimensions={0} | all-to-all | bytes 163840 | tf_op jit(solution)/shard_map/all_to_all | solution.py:355
  97.7 0.7 owner.3
  98.4 12.7 %all_to_all.67 = f32[32,1,256]{2,1,0:T(1,128)S(1)} all-to-all(f32[32,1,256]{2,1,0:T(1,128)S(1)} %bitcast.33), channel_id=1, replica_groups={{168,0,8,16,24,32,40,48,56,64,72,80,88,96,104,112,120,128,136,144,152,1..., dimensions={0} | all-to-all | bytes 65536 | tf_op jit(solution)/shard_map/all_to_all | solution.py:355
  111.1 0.5 margin.5
  111.6 7.3 %all_to_all.68.margin_ref = f32[8,1,128]{2,1,0:T(1,128)S(1)} all-to-all(f32[8,1,128]{2,1,0:T(1,128)S(1)} %margin.5), channel_id=1, replica_groups={{5,7,6,4,3,2,1,0},{13,15,14,12,11,10,9,8},{21,23,22,20,19,18,17,16},{29..., dimensions={0} | all-to-all | bytes 8192 | tf_op jit(solution)/shard_map/all_to_all | solution.py:404
  118.9 0.2 pool.7
  119.2 13.3 %all_to_all.69 = f32[32,1,640]{2,1,0:T(1,128)S(1)} all-to-all(f32[32,1,640]{2,1,0:T(1,128)S(1)} %bitcast.31), channel_id=1, replica_groups={{168,0,8,16,24,32,40,48,56,64,72,80,88,96,104,112,120,128,136,144,152,1..., dimensions={0} | all-to-all | bytes 163840 | tf_op jit(solution)/shard_map/all_to_all | solution.py:355
  132.5 0.6 owner_last.1
  133.1 13.8 %all_to_all.70 = f32[32,1,1152]{2,1,0:T(1,128)S(1)} all-to-all(f32[32,1,1152]{2,1,0:T(1,128)S(1)} %bitcast.19), channel_id=1, replica_groups={{168,0,8,16,24,32,40,48,56,64,72,80,88,96,104,112,120,128,136,144,152,1..., dimensions={0} | all-to-all | bytes 294912 | tf_op jit(solution)/shard_map/all_to_all | solution.py:355
  146.9 1.7 %closing.1 = (f32[1,128]{1,0:T(1,128)}, f32[64,512]{1,0:T(8,128)}, f32[8,512]{1,0:T(8,128)}, bf16[128,8,512]{2,1,0:T(8,128)(2,1)}) custom-call(s32[1,128]{1,0:T(1,128)S(1)} %get-tuple-element.24.group_vmem, f32[1,128]{1,0:T(1,128)S(1)} %get-tuple-element.37.factor_vmem, f32[288,128]{1,0:T(8,128)S(1)} %bitcast.20, bf16[128,8,512]{2,1,0:T(8,128)(2,1)S(1)} %near.1.x_ref), custom_call_target="tpu_custom_call" | custom-call | tf_op jit(solution)/shard_map/closing/pallas_call | solution.py:431
Async XLA Ops:
  3.0 8.4 %all-to-all-start = ((f32[8,1,128]{2,1,0:T(1,128)}), f32[8,1,128]{2,1,0:T(1,128)S(1)}, u32[]{:S(2)}, u32[]{:S(2)}) async-start(f32[8,1,128]{2,1,0:T(1,128)} %first.1), calls=%async_computation | async-start | bytes 8192 | tf_op jit(solution)/shard_map/all_to_all | solution.py:404

commit v13 on v12

--- a/solution.py
+++ b/solution.py
@@ -96,9 +96,12 @@
     row, lane = iota((SUB, LANES), 0), iota((SUB, LANES), 1)
     half = items // SUB
     gather = (iota((LANES, LANES), 0) // days == iota((LANES, LANES), 1) % half).astype(F32).astype(BF16)
-    x = x_ref[...].astype(F32).reshape(items * days, stores).astype(BF16)
+    folded = x_ref[:, :, :LANES].astype(F32)
+    for t in range(1, stores // LANES):
+        folded = folded + x_ref[:, :, t * LANES : (t + 1) * LANES].astype(F32)
+    parts = jnp.concatenate(two_parts(folded.reshape(items * days, LANES)), axis=1)
     sums = lax.dot_general(
-        jnp.ones((SUB, stores), BF16), x, (((1,), (1,)), ((), ())), preferred_element_type=F32
+        jnp.ones((SUB, 2 * LANES), BF16), parts, (((1,), (1,)), ((), ())), preferred_element_type=F32
     )
     tile = sums[:, :LANES]
     for q in range(1, SUB):
@@ -165,8 +168,8 @@
     cat = jnp.dot(jnp.concatenate(two_parts(cat), axis=0), widen_ref[...], preferred_element_type=F32)
     cat = cat[:count] + cat[count:]
     for s in range(SUB):
-        product = cat[:, s * LANES : (s + 1) * LANES] * day if s < SLOTS else jnp.zeros_like(day)
-        tiles_ref[pl.ds(s, count, stride=SUB), :] = product
+        here = min(s, SLOTS - 1) * LANES
+        tiles_ref[pl.ds(s, count, stride=SUB), :] = cat[:, here : here + LANES] * day
     tiles = [tiles_ref[j * SUB : (j + 1) * SUB] for j in range(count)]
     parts = jnp.concatenate(two_parts(jnp.concatenate(tiles, axis=1)), axis=0)
     sums = lax.dot_general(parts, wide_ref[...], (((1,), (1,)), ((), ())), preferred_element_type=F32)

time: 149 us -> 149 us (level)
  no operation moved by 1% of the time
where the time goes in v13:
time: 149 us; the launch traced here: 148 us
  blocking collectives  130 us (87%)
  Pallas kernels  11.7 us (8%)
  starting transfers between devices  4.61 us (3%)
    all_to_all x8, blocking collectives, exchanged(): lax.all_to_all(sent, 'item', 0, 0, axis_index_groups=[item_order(owners)]...  108 us
    all_to_all x3, blocking collectives, shards(): lax.all_to_all(part, 'store', 0, 0, axis_index_groups=[store_order(beside...  21.9 us
    pallas_call x12, Pallas kernels, call(): pl.pallas_call(kernel, out_shape=out_shape, in_specs=vmem(len(args)), out...  6.49 us
    all_to_all x1, starting transfers between devices, shards(): lax.all_to_all(part, 'store', 0, 0, axis_index_groups=[store_order(beside...  4.61 us
  transfers between devices with their start and end apart: 1, of which 1 were waited for; matrix products, arithmetic and copies ran while one was open for 0% of the time, Pallas kernels for 2%

profile of v13, /device:TPU:8, one launch (start us, length us, event | category | flops | bytes accessed | tf_op | source)
XLA Modules:
  0.0 148.5 jit_solution(13374539752321707914)
XLA Ops:
  0.6 1.2 near.1.x_ref
  1.9 1.0 first.1
  2.9 4.6 %all-to-all-start = ((f32[8,1,128]{2,1,0:T(1,128)}), f32[8,1,128]{2,1,0:T(1,128)S(1)}, u32[]{:S(2)}, u32[]{:S(2)}) async-start(f32[8,1,128]{2,1,0:T(1,128)} %first.1), calls=%async_computation | async-start | bytes 8192 | tf_op jit(solution)/shard_map/all_to_all | solution.py:407
  7.5 2.3 %spread.1 = (bf16[128,4096]{1,0:T(8,128)(2,1)S(1)}, s32[8,128]{1,0:T(8,128)S(1)}, s32[1,128]{1,0:T(1,128)S(1)}, f32[8,128]{1,0:T(8,128)S(1)}, f32[64,128]{1,0:T(8,128)S(1)}, /*index=5*/bf16[128,640]{1,0:T(8,128)(2,1)S(1)}) custom-call(bf16[128,8,512]{2,1,0:T(8,128)(2,1)S(1)} %near.1.x_ref, s32[1,128]{1,0:T(1,128)} %bitcast.35, f32[1,128]{1,0:T(1,128)} %bitcast.36, ...), custom_call_target="tpu_custom_call" | custom-call | tf_op jit(solution)/shard_map/spread/pallas_call | solution.py:377
  9.8 1.4 all-to-all-done.margin_ref
  11.2 0.2 pool.4
  11.5 16.3 %all_to_all.60 = f32[32,1,768]{2,1,0:T(1,128)S(1)} all-to-all(f32[32,1,768]{2,1,0:T(1,128)S(1)} %bitcast.22), channel_id=1, replica_groups={{168,0,8,16,24,32,40,48,56,64,72,80,88,96,104,112,120,128,136,144,152,1..., dimensions={0} | all-to-all | bytes 196608 | tf_op jit(solution)/shard_map/all_to_all | solution.py:358
  27.8 0.9 owner_first.1
  28.7 12.8 %all_to_all.61 = f32[32,1,256]{2,1,0:T(1,128)S(1)} all-to-all(f32[32,1,256]{2,1,0:T(1,128)S(1)} %bitcast.32), channel_id=1, replica_groups={{168,0,8,16,24,32,40,48,56,64,72,80,88,96,104,112,120,128,136,144,152,1..., dimensions={0} | all-to-all | bytes 65536 | tf_op jit(solution)/shard_map/all_to_all | solution.py:358
  41.5 0.5 margin.3
  42.0 7.3 %all_to_all.62.margin_ref = f32[8,1,128]{2,1,0:T(1,128)S(1)} all-to-all(f32[8,1,128]{2,1,0:T(1,128)S(1)} %margin.3), channel_id=1, replica_groups={{5,7,6,4,3,2,1,0},{13,15,14,12,11,10,9,8},{21,23,22,20,19,18,17,16},{29..., dimensions={0} | all-to-all | bytes 8192 | tf_op jit(solution)/shard_map/all_to_all | solution.py:407
  49.3 0.2 pool.5
  49.6 13.3 %all_to_all.63 = f32[32,1,640]{2,1,0:T(1,128)S(1)} all-to-all(f32[32,1,640]{2,1,0:T(1,128)S(1)} %bitcast.23), channel_id=1, replica_groups={{168,0,8,16,24,32,40,48,56,64,72,80,88,96,104,112,120,128,136,144,152,1..., dimensions={0} | all-to-all | bytes 163840 | tf_op jit(solution)/shard_map/all_to_all | solution.py:358
  62.8 0.7 owner.2
  63.6 12.7 %all_to_all.64 = f32[32,1,256]{2,1,0:T(1,128)S(1)} all-to-all(f32[32,1,256]{2,1,0:T(1,128)S(1)} %bitcast.34), channel_id=1, replica_groups={{168,0,8,16,24,32,40,48,56,64,72,80,88,96,104,112,120,128,136,144,152,1..., dimensions={0} | all-to-all | bytes 65536 | tf_op jit(solution)/shard_map/all_to_all | solution.py:358
  76.3 0.5 margin.4
  76.8 7.3 %all_to_all.65.margin_ref = f32[8,1,128]{2,1,0:T(1,128)S(1)} all-to-all(f32[8,1,128]{2,1,0:T(1,128)S(1)} %margin.4), channel_id=1, replica_groups={{5,7,6,4,3,2,1,0},{13,15,14,12,11,10,9,8},{21,23,22,20,19,18,17,16},{29..., dimensions={0} | all-to-all | bytes 8192 | tf_op jit(solution)/shard_map/all_to_all | solution.py:407
  84.1 0.2 pool.6
  84.3 13.3 %all_to_all.66 = f32[32,1,640]{2,1,0:T(1,128)S(1)} all-to-all(f32[32,1,640]{2,1,0:T(1,128)S(1)} %bitcast.24), channel_id=1, replica_groups={{168,0,8,16,24,32,40,48,56,64,72,80,88,96,104,112,120,128,136,144,152,1..., dimensions={0} | all-to-all | bytes 163840 | tf_op jit(solution)/shard_map/all_to_all | solution.py:358
  97.6 0.7 owner.3
  98.3 12.7 %all_to_all.67 = f32[32,1,256]{2,1,0:T(1,128)S(1)} all-to-all(f32[32,1,256]{2,1,0:T(1,128)S(1)} %bitcast.33), channel_id=1, replica_groups={{168,0,8,16,24,32,40,48,56,64,72,80,88,96,104,112,120,128,136,144,152,1..., dimensions={0} | all-to-all | bytes 65536 | tf_op jit(solution)/shard_map/all_to_all | solution.py:358
  111.0 0.5 margin.5
  111.6 7.3 %all_to_all.68.margin_ref = f32[8,1,128]{2,1,0:T(1,128)S(1)} all-to-all(f32[8,1,128]{2,1,0:T(1,128)S(1)} %margin.5), channel_id=1, replica_groups={{5,7,6,4,3,2,1,0},{13,15,14,12,11,10,9,8},{21,23,22,20,19,18,17,16},{29..., dimensions={0} | all-to-all | bytes 8192 | tf_op jit(solution)/shard_map/all_to_all | solution.py:407
  118.9 0.2 pool.7
  119.1 13.3 %all_to_all.69 = f32[32,1,640]{2,1,0:T(1,128)S(1)} all-to-all(f32[32,1,640]{2,1,0:T(1,128)S(1)} %bitcast.31), channel_id=1, replica_groups={{168,0,8,16,24,32,40,48,56,64,72,80,88,96,104,112,120,128,136,144,152,1..., dimensions={0} | all-to-all | bytes 163840 | tf_op jit(solution)/shard_map/all_to_all | solution.py:358
  132.4 0.6 owner_last.1
  133.0 13.8 %all_to_all.70 = f32[32,1,1152]{2,1,0:T(1,128)S(1)} all-to-all(f32[32,1,1152]{2,1,0:T(1,128)S(1)} %bitcast.19), channel_id=1, replica_groups={{168,0,8,16,24,32,40,48,56,64,72,80,88,96,104,112,120,128,136,144,152,1..., dimensions={0} | all-to-all | bytes 294912 | tf_op jit(solution)/shard_map/all_to_all | solution.py:358
  146.8 1.7 %closing.1 = (f32[1,128]{1,0:T(1,128)}, f32[64,512]{1,0:T(8,128)}, f32[8,512]{1,0:T(8,128)}, bf16[128,8,512]{2,1,0:T(8,128)(2,1)}) custom-call(s32[1,128]{1,0:T(1,128)S(1)} %get-tuple-element.24.group_vmem, f32[1,128]{1,0:T(1,128)S(1)} %get-tuple-element.37.factor_vmem, f32[288,128]{1,0:T(8,128)S(1)} %bitcast.20, bf16[128,8,512]{2,1,0:T(8,128)(2,1)S(1)} %near.1.x_ref), custom_call_target="tpu_custom_call" | custom-call | tf_op jit(solution)/shard_map/closing/pallas_call | solution.py:434
Async XLA Ops:
  2.9 8.4 %all-to-all-start = ((f32[8,1,128]{2,1,0:T(1,128)}), f32[8,1,128]{2,1,0:T(1,128)S(1)}, u32[]{:S(2)}, u32[]{:S(2)}) async-start(f32[8,1,128]{2,1,0:T(1,128)} %first.1), calls=%async_computation | async-start | bytes 8192 | tf_op jit(solution)/shard_map/all_to_all | solution.py:407
